TPU v7x, 32 devices: a whole 2x2x4 slice. The times are simulated.
32 devices in a mesh: dp: 8 (over z, y), seq: 4 (over x, core).
Axes of the slice: x: 2, y: 2, z: 4, core: 2. Of those that a mesh axis runs over, the one named last changes fastest.
Arguments:
- hidden_in: bfloat16 [8, 512, 768], P('dp', 'seq'), may hold values from -6 to 6
- segments: int32 [8, 512], P('dp'), may hold values from 0 to 3, never falling along the last dimension, each value on 1 to 256 neighbouring positions
- norm_gain: bfloat16 [768], P(('dp', 'seq')), may hold values from 0.5 to 1.5
- in_weight: bfloat16 [768, 3352], P(('dp', 'seq')), may hold values from -0.21875 to 0.21875
- conv_weight: bfloat16 [4, 1792], P(None, ('dp', 'seq')), may hold values from -0.5 to 0.5
- conv_bias: bfloat16 [1792], P(('dp', 'seq')), may hold values from -0.5 to 0.5
- step_bias: float32 [24], replicated, may hold values from -4.5 to -1
- decay_log: float32 [24], replicated, may hold values from -4 to 1.5
- skip_weight: float32 [24], replicated, may hold values from 0.5 to 1.5
- gate_gain: bfloat16 [1536], P(('dp', 'seq')), may hold values from 0.5 to 1.5
- out_weight: bfloat16 [1536, 768], P(('dp', 'seq')), may hold values from -0.15625 to 0.15625
- out_grad: bfloat16 [8, 512, 768], P('dp', 'seq'), may hold values from -6 to 6
Outputs:
- output: float32 [8, 512, 768], P('dp', 'seq')
- grad_hidden: float32 [8, 512, 768], P('dp', 'seq')
- grad_norm_gain: float32 [768], P(('dp', 'seq'))
- grad_in_weight: float32 [768, 3352], P(('dp', 'seq'))
- grad_conv_weight: float32 [4, 1792], P(None, ('dp', 'seq'))
- grad_conv_bias: float32 [1792], P(('dp', 'seq'))
- grad_step_bias: float32 [24], replicated
- grad_decay_log: float32 [24], replicated
- grad_skip_weight: float32 [24], replicated
- grad_gate_gain: float32 [1536], P(('dp', 'seq'))
- grad_out_weight: float32 [1536, 768], P(('dp', 'seq'))
Inputs may be any that keep to these rules, and one draw needn't show every extreme that they name: `segments`: within each row the segment numbers never fall and start at 0; each segment has 1 to 256 tokens and one has exactly 256.
All inputs are finite; a program needn't handle non-finite values.
Results may differ from a plain program's by a relative error of at most 0.007.
Values may be sent and summed in bfloat16 or wider, within the bound.
No kernel may reach another device: no remote copies, remote signals or barrier semaphores. Data moves between devices by JAX's collectives and lax.ppermute only.
A program may use at most 128 MiB of HBM per device.

v0:
```python
import jax
import jax.numpy as jnp
from jax import lax
from jax.sharding import PartitionSpec as P

HEADS = 24
HEAD_DIM = 64
STATE = 128
CONV = 4


EPSILON = 1e-05
PRECISE = lax.Precision.HIGHEST


def passed_along(x, axis, by):
    length = lax.axis_size(axis)
    pairs = [(i, i + by) for i in range(length) if 0 <= i + by < length]
    return lax.ppermute(x, axis, pairs)


def carried_in(part, axis, combine, identity, reverse):
    count = lax.axis_size(axis)
    place = lax.axis_index(axis)
    ahead = count - 1 - place if reverse else place
    gathered = jax.tree.map(lambda a: lax.all_gather(a, axis), part)
    state = jax.tree.map(lambda a, e: jnp.zeros_like(a) + jnp.asarray(e, a.dtype), part, identity)

    def one(turn, state):
        source = count - 1 - turn if reverse else turn
        return combine(
            state, jax.tree.map(lambda a: lax.dynamic_index_in_dim(a, source, 0, False), gathered)
        )

    return lax.fori_loop(0, ahead, one, state)


def conv_block(window_in, segment_window, conv_taps, conv_shift):
    length_now = window_in.shape[0] - (CONV - 1)
    running = jnp.zeros((length_now, window_in.shape[1]), jnp.float32) + conv_shift[None, :]
    for offset in range(CONV):
        same_segment = (
            segment_window[offset : offset + length_now] == segment_window[CONV - 1 :]
        ).astype(jnp.float32)
        running = (
            running
            + conv_taps[offset][None, :]
            * window_in[offset : offset + length_now]
            * same_segment[:, None]
        )
    return jax.nn.silu(running)


def ssd_core(channels, raw_steps, segment_now, segment_before, bias_step, log_rate, skip_term):
    length_now = channels.shape[0]
    inner_width = channels.shape[1] - 2 * STATE
    values = channels[:, :inner_width].reshape(length_now, HEADS, HEAD_DIM)
    keys_b = channels[:, inner_width : inner_width + STATE]
    query_c = channels[:, inner_width + STATE :]
    step_size = jax.nn.softplus(raw_steps + bias_step[None, :])
    log_decay = step_size * (-jnp.exp(log_rate))[None, :]
    cumulative = jnp.cumsum(log_decay, axis=0)
    places = jnp.arange(length_now)
    pair_mask = (
        (places[:, None] >= places[None, :]) & (segment_now[:, None] == segment_now[None, :])
    )[:, :, None]
    gap_log = cumulative[:, None, :] - cumulative[None, :, :]
    decay_pair = jnp.where(pair_mask, jnp.exp(jnp.where(pair_mask, gap_log, 0.0)), 0.0)
    scores = jnp.dot(query_c, keys_b.T, precision=PRECISE, preferred_element_type=jnp.float32)
    mixing = scores[:, :, None] * decay_pair * step_size[None, :, :]
    inner_out = jnp.einsum("tsh,shp->thp", mixing, values, precision=PRECISE)
    local_out = inner_out + skip_term[None, :, None] * values
    entry_gate = jnp.exp(cumulative) * (segment_now == segment_before).astype(jnp.float32)[:, None]
    last_log = cumulative[length_now - 1]
    tail_weight = (
        jnp.exp(last_log[None, :] - cumulative)
        * (segment_now == segment_now[length_now - 1]).astype(jnp.float32)[:, None]
        * step_size
    )
    weighted = values * tail_weight[:, :, None]
    fresh_state = jnp.einsum("shp,sn->hpn", weighted, keys_b, precision=PRECISE)
    through = jnp.exp(last_log) * (segment_now[length_now - 1] == segment_before).astype(
        jnp.float32
    )
    return (local_out, through, fresh_state, entry_gate, query_c)


def split_mixer(
    window_in,
    raw_steps,
    segment_window,
    segment_before,
    conv_taps,
    conv_shift,
    bias_step,
    log_rate,
    skip_term,
):
    channels = conv_block(window_in, segment_window, conv_taps, conv_shift)
    return ssd_core(
        channels,
        raw_steps,
        segment_window[CONV - 1 :],
        segment_before,
        bias_step,
        log_rate,
        skip_term,
    )


def full_mixer(
    window_in,
    raw_steps,
    segment_window,
    segment_before,
    conv_taps,
    conv_shift,
    bias_step,
    log_rate,
    skip_term,
    held_state,
):
    local_out, through, fresh_state, entry_gate, query_c = split_mixer(
        window_in,
        raw_steps,
        segment_window,
        segment_before,
        conv_taps,
        conv_shift,
        bias_step,
        log_rate,
        skip_term,
    )
    mixed = (
        local_out
        + jnp.einsum("tn,hpn->thp", query_c, held_state, precision=PRECISE) * entry_gate[:, :, None]
    )
    return (mixed, through, fresh_state)


def gated_norm(mixed_flat, gate_half, gain_vec):
    product = mixed_flat * jax.nn.silu(gate_half)
    scale_inv = lax.rsqrt(jnp.mean(product * product, axis=-1, keepdims=True) + EPSILON)
    return product * scale_inv * gain_vec[None, :]


def pre_norm(widened, gain_vec):
    scale_inv = lax.rsqrt(jnp.mean(widened * widened, axis=-1, keepdims=True) + EPSILON)
    return widened * scale_inv * gain_vec[None, :]


def join_forward(earlier_part, later_part):
    return (
        earlier_part[0] * later_part[0],
        later_part[0][..., None, None] * earlier_part[1] + later_part[1],
    )


def join_backward(earlier_part, later_part):
    return (
        earlier_part[0] * later_part[0],
        later_part[1] + later_part[0][..., None, None] * earlier_part[1],
    )


def on_device(
    hidden_in,
    segments,
    norm_gain,
    in_weight,
    conv_weight,
    conv_bias,
    step_bias,
    decay_log,
    skip_weight,
    gate_gain,
    out_weight,
    out_grad,
):
    row_count, piece_len, model_width = hidden_in.shape
    gathered = (
        lax.all_gather(norm_gain, ("dp", "seq"), axis=0, tiled=True),
        lax.all_gather(in_weight, ("dp", "seq"), axis=0, tiled=True),
        lax.all_gather(conv_weight, ("dp", "seq"), axis=1, tiled=True),
        lax.all_gather(conv_bias, ("dp", "seq"), axis=0, tiled=True),
        lax.all_gather(gate_gain, ("dp", "seq"), axis=0, tiled=True),
        lax.all_gather(out_weight, ("dp", "seq"), axis=0, tiled=True),
    )
    in_full = gathered[1]
    conv_taps = gathered[2].astype(jnp.float32)
    conv_shift = gathered[3].astype(jnp.float32)
    out_full = gathered[5]
    channel_count = conv_taps.shape[1]
    inner_width = out_full.shape[0]
    tokens_here = row_count * piece_len
    widened = hidden_in.astype(jnp.float32).reshape(tokens_here, model_width)
    normed = pre_norm(widened, gathered[0].astype(jnp.float32)).astype(jnp.bfloat16)
    projected = jnp.dot(normed, in_full, preferred_element_type=jnp.float32).reshape(
        row_count, piece_len, -1
    )
    gate_half = projected[:, :, :inner_width].reshape(tokens_here, inner_width)
    conv_input = projected[:, :, inner_width : inner_width + channel_count]
    step_raw = projected[:, :, inner_width + channel_count :]
    rim_rows = conv_input[:, piece_len - (CONV - 1) :, :]
    arrived = passed_along(rim_rows, "seq", 1)
    extended = jnp.concatenate([arrived, conv_input], axis=1)
    position = lax.axis_index("seq")
    segment_pad = jnp.concatenate(
        [jnp.full((row_count, CONV - 1), -1, jnp.int32), segments], axis=1
    )
    segment_window = lax.dynamic_slice_in_dim(
        segment_pad, position * piece_len, piece_len + CONV - 1, axis=1
    )
    segment_before = segment_window[:, CONV - 2]
    split_rows = jax.vmap(split_mixer, in_axes=(0, 0, 0, 0, None, None, None, None, None))
    local_out, through, fresh_state, entry_gate, query_c = split_rows(
        extended,
        step_raw,
        segment_window,
        segment_before,
        conv_taps,
        conv_shift,
        step_bias,
        decay_log,
        skip_weight,
    )
    carried = carried_in(
        (through, fresh_state),
        "seq",
        join_forward,
        (jnp.ones_like(through), jnp.zeros_like(fresh_state)),
        False,
    )[1]
    mixed = (
        local_out
        + jnp.einsum("rtn,rhpn->rthp", query_c, carried, precision=PRECISE) * entry_gate[..., None]
    )
    mixed_flat = mixed.reshape(tokens_here, inner_width)
    gated_out = gated_norm(mixed_flat, gate_half, gathered[4].astype(jnp.float32)).astype(
        jnp.bfloat16
    )
    result = widened + jnp.dot(gated_out, out_full, preferred_element_type=jnp.float32)
    backward_set = (
        lax.all_gather(norm_gain, ("dp", "seq"), axis=0, tiled=True),
        lax.all_gather(in_weight, ("dp", "seq"), axis=0, tiled=True),
        lax.all_gather(conv_weight, ("dp", "seq"), axis=1, tiled=True),
        lax.all_gather(conv_bias, ("dp", "seq"), axis=0, tiled=True),
        lax.all_gather(gate_gain, ("dp", "seq"), axis=0, tiled=True),
        lax.all_gather(out_weight, ("dp", "seq"), axis=0, tiled=True),
    )
    back_norm = backward_set[0].astype(jnp.float32)
    back_in = backward_set[1]
    back_taps = backward_set[2].astype(jnp.float32)
    back_shift = backward_set[3].astype(jnp.float32)
    back_gate = backward_set[4].astype(jnp.float32)
    back_out = backward_set[5]
    cotangent = out_grad.reshape(tokens_here, model_width)
    grad_out_w = jnp.einsum("ti,td->id", gated_out, cotangent, preferred_element_type=jnp.float32)
    d_gated = jnp.einsum("td,id->ti", cotangent, back_out, preferred_element_type=jnp.float32)
    _, gate_back = jax.vjp(gated_norm, mixed_flat, gate_half, back_gate)
    d_mixed, d_gate_half, grad_gate = gate_back(d_gated)
    d_mixed4 = d_mixed.reshape(row_count, piece_len, HEADS, HEAD_DIM)
    gated_back = d_mixed4 * entry_gate[..., None]
    state_local = jnp.einsum("rthp,rtn->rhpn", gated_back, query_c, precision=PRECISE)
    later_total = carried_in(
        (through, state_local),
        "seq",
        join_backward,
        (jnp.ones_like(through), jnp.zeros_like(state_local)),
        True,
    )[1]
    d_through = jnp.sum(later_total * carried, axis=(2, 3))
    full_rows = jax.vmap(full_mixer, in_axes=(0, 0, 0, 0, None, None, None, None, None, 0))

    def mixer_rows(window_in, raw_steps, taps_in, shift_in, bias_in, rate_in, skip_in, held_state):
        return full_rows(
            window_in,
            raw_steps,
            segment_window,
            segment_before,
            taps_in,
            shift_in,
            bias_in,
            rate_in,
            skip_in,
            held_state,
        )

    _, mixer_back = jax.vjp(
        mixer_rows,
        extended,
        step_raw,
        back_taps,
        back_shift,
        step_bias,
        decay_log,
        skip_weight,
        carried,
    )
    mixer_grads = mixer_back((d_mixed4, d_through, later_total))
    d_extended, d_step_raw, d_taps, d_shift, d_bias, d_rate, d_skip = mixer_grads[:7]
    returned = passed_along(d_extended[:, : CONV - 1, :], "seq", -1)
    d_main = d_extended[:, CONV - 1 :, :]
    d_conv = jnp.concatenate(
        [d_main[:, : piece_len - (CONV - 1)], d_main[:, piece_len - (CONV - 1) :] + returned],
        axis=1,
    )
    d_projected = jnp.concatenate(
        [d_gate_half.reshape(row_count, piece_len, inner_width), d_conv, d_step_raw], axis=-1
    )
    d_projected = d_projected.astype(jnp.bfloat16).reshape(tokens_here, -1)
    grad_in_w = jnp.einsum("td,tk->dk", normed, d_projected, preferred_element_type=jnp.float32)
    d_normed = jnp.einsum("tk,dk->td", d_projected, back_in, preferred_element_type=jnp.float32)
    _, norm_back = jax.vjp(pre_norm, widened, back_norm)
    d_wide, grad_norm = norm_back(d_normed)
    grad_hidden = (cotangent.astype(jnp.float32) + d_wide).reshape(
        row_count, piece_len, model_width
    )
    shards = (
        lax.psum_scatter(grad_norm, ("dp", "seq"), scatter_dimension=0, tiled=True),
        lax.psum_scatter(grad_in_w, ("dp", "seq"), scatter_dimension=0, tiled=True),
        lax.psum_scatter(d_taps, ("dp", "seq"), scatter_dimension=1, tiled=True),
        lax.psum_scatter(d_shift, ("dp", "seq"), scatter_dimension=0, tiled=True),
        lax.psum_scatter(grad_gate, ("dp", "seq"), scatter_dimension=0, tiled=True),
        lax.psum_scatter(grad_out_w, ("dp", "seq"), scatter_dimension=0, tiled=True),
    )
    head_grads = lax.psum((d_bias, d_rate, d_skip), ("dp", "seq"))
    return (
        result.reshape(row_count, piece_len, model_width),
        grad_hidden,
        shards[0],
        shards[1],
        shards[2],
        shards[3],
        head_grads[0],
        head_grads[1],
        head_grads[2],
        shards[4],
        shards[5],
    )


def solution(mesh):
    in_specs = (
        P("dp", "seq", None),
        P("dp", None),
        P(("dp", "seq")),
        P(("dp", "seq"), None),
        P(None, ("dp", "seq")),
        P(("dp", "seq")),
        P(),
        P(),
        P(),
        P(("dp", "seq")),
        P(("dp", "seq"), None),
        P("dp", "seq", None),
    )
    out_specs = (
        P("dp", "seq", None),
        P("dp", "seq", None),
        P(("dp", "seq")),
        P(("dp", "seq"), None),
        P(None, ("dp", "seq")),
        P(("dp", "seq")),
        P(),
        P(),
        P(),
        P(("dp", "seq")),
        P(("dp", "seq"), None),
    )
    return jax.shard_map(
        on_device, mesh=mesh, in_specs=in_specs, out_specs=out_specs, check_vma=False
    )
```

profile of v0, /device:TPU:0, one launch (start us, length us, event | category | flops | bytes accessed | tf_op | source)
XLA Modules:
  0.0 515.8 jit_solution(3508917722114791065)
XLA Ops:
  10.5 42.9 %all-reduce.22 = (bf16[768]{0:T(1024)(128)(2,1)S(1)}, bf16[1792]{0:T(1024)(128)(2,1)S(1)}, bf16[1536]{0:T(1024)(128)(2,1)S(1)}) all-reduce(bf16[768]{0:T(1024)(128)(2,1)S(1)} %dynamic-update-slice.1, bf16[1792]{0:T(1024)(128)(2,1)S(1)} %dynamic-update-slice, ...), channel_id=1, replica_groups=mesh['dp'=8,'seq'=4] {'dp','seq'}, use_global_device_ids=true, to_apply=%add.14 | all-reduce | flops 4096 | bytes 16384
  56.0 40.9 %all-gather.2 = bf16[32,56,4]{1,2,0:T(4,128)(2,1)S(1)} all-gather(bf16[1,56,4]{1,2,0:T(4,128)(2,1)} %bitcast.288), channel_id=1, replica_groups=mesh['dp'=8,'seq'=4] {'dp','seq'}, dimensions={0}, use_global_device_ids=true | all-gather | bytes 14784 | tf_op jit(solution)/shard_map/all_gather | solution.py:184
  104.1 3.6 convolution_bitcast_fusion
  113.8 4.0 fusion.16
  133.1 5.3 %all_gather.46 = f32[4,1,24]{2,1,0:T(1,128)} all-gather(f32[1,1,24]{2,1,0:T(1,128)} %get-tuple-element.281), channel_id=1, replica_groups=mesh['dp'=8,'seq'=4] {'seq'}, dimensions={0}, use_global_device_ids=true | all-gather | bytes 480 | tf_op jit(solution)/shard_map/all_gather | solution.py:26
  141.6 5.2 %all-gather.12.cloned.1.call-done = f32[96,64,128]{2,1,0:T(8,128)} async-done(((f32[24,64,128]{2,1,0:T(8,128)}), f32[96,64,128]{2,1,0:T(8,128)}) %all-gather.12.cloned.1.call-update) | async-done | bytes 3145744 | tf_op jit(solution)/shard_map/all_gather | solution.py:26
  147.9 6.7 %multiply_reduce_fusion.10 = (f32[128]{0:T(128)}, f32[1,128,24,64]{1,3,2,0:T(8,128)}, f32[1,128,24,64]{1,3,2,0:T(8,128)}) fusion(f32[1,128,24,64]{1,3,2,0:T(8,128)} %bitcast.278, f32[128,24,64]{0,2,1:T(8,128)S(1)} %fusion.29, f32[128,24]{0,1:T(8,128)} %copy-done.42, f32[1,128,24,64]{1,3,2,0:T(8,128)} %bitcast.273, f32[24]{0:T(128)} %param.24, ...), kind=kOutput, calls=%fused_computation.83 | convolution fusion | flops 306118528 | bytes 4837984 | tf_op jit(solution)/shard_map/vmap(tsh,shp->thp)/dot_general | solution.py:71
  158.1 48.7 %all-gather.10.cloned.1.call-done = bf16[1536,768]{1,0:T(8,128)(2,1)} async-done(((bf16[48,768]{1,0:T(8,128)(2,1)}), bf16[1536,768]{1,0:T(8,128)(2,1)}) %all-gather.10.cloned.1.call-update) | async-done | bytes 2359312 | tf_op jit(solution)/shard_map/all_gather | solution.py:187
  206.8 3.6 multiply_reduce_fusion.5
  216.6 2.8 fusion.72
  222.5 5.7 %fusion.18 = (f32[128,24]{0,1:T(8,128)}, f32[128,24]{0,1:T(8,128)}, f32[128,24]{0,1:T(8,128)}, f32[128,128]{1,0:T(8,128)}) fusion(f32[128,128]{1,0:T(8,128)} %fusion.76, f32[128,24]{0,1:T(8,128)} %bitcast.285, f32[128,24]{0,1:T(8,128)} %copy.203, pred[128,128]{1,0:T(8,128)(4,1)} %fusion.80, f32[24,64,128]{2,1,0:T(8,128)} %bitcast.267, ...), kind=kOutput, calls=%fused_computation.55 | convolution fusion | flops 307862528 | bytes 1781760 | tf_op jit(solution)/shard_map/transpose(jvp(vmap(tsh,shp->thp)))/dot_general | solution.py:71
  237.4 3.8 fusion.56
  243.3 2.5 convolution_bitcast_fusion.3
  247.0 6.0 %while.27 = (s32[]{:T(128)}, f32[1,24,64,128]{3,2,1,0:T(8,128)S(1)}, s32[]{:T(128)}, f32[4,1,24,64,128]{4,3,2,1,0:T(8,128)}, f32[4,1,24]{2,1,0:T(1,128)}, /*index=5*/s32[]{:T(128)}, s32[]{:T(128)}, s32[]{:T(128)}, s32[]{:T(128)}) while((s32[]{:T(128)}, f32[1,24,64,128]{3,2,1,0:T(8,128)S(1)}, s32[]{:T(128)}, f32[4,1,24,64,128]{4,3,2,1,0:T(8,128)}, ...), condition=%wide.region_8.9_spmd, body=%wide.region_7.8_spmd.sunk | while | flops 393222 | bytes 2359739 | solution.py:35
  253.0 3.5 multiply_reduce_fusion.8
  257.3 4.5 fusion.6
  264.3 2.7 fusion.10
  267.0 2.9 multiply_reduce_fusion.3
  276.1 2.5 pad_add_fusion
  281.2 5.7 %fusion.54 = f32[768,3352]{1,0:T(8,128)} fusion(bf16[128,24]{1,0:T(8,128)(2,1)S(1)} %bitcast.281, bf16[128,1792]{1,0:T(8,128)(2,1)S(1)} %maximum_bitcast_fusion, bf16[128,1536]{1,0:T(8,128)(2,1)S(1)} %copy-done.23, bf16[1,128,768]{2,1,0:T(8,128)(2,1)S(1)} %copy-done.12, f32[768]{0:T(1024)S(1)} %convert_element_type.60, f32[128]{0:T(128)S(1)} %copy-done.56), kind=kOutput, calls=%fused_computation.111 | convolution fusion | flops 661997568 | bytes 11355648 | tf_op jit(solution)/shard_map/td,tk->dk/dot_general | solution.py:312
  290.5 4.4 fusion.46
  294.9 41.7 %all-reduce.21 = (f32[768]{0:T(1024)S(1)}, f32[4,1792]{1,0:T(4,128)S(1)}, f32[1792]{0:T(1024)S(1)}, f32[24]{0:T(128)}, f32[24]{0:T(128)}, /*index=5*/f32[24]{0:T(128)}, f32[1536]{0:T(1024)S(1)}) all-reduce(f32[768]{0:T(1024)S(1)} %get-tuple-element.222, ...), channel_id=4, replica_groups=mesh['dp'=8,'seq'=4] {'dp','seq'}, use_global_device_ids=true, to_apply=%region_19.20.clone | all-reduce | flops 11336 | bytes 90688
  339.9 21.3 %reduce-scatter.6.cloned.1.call-done = f32[48,768]{1,0:T(8,128)} async-done(((f32[1536,768]{1,0:T(8,128)}), f32[48,768]{1,0:T(8,128)}) %reduce-scatter.6.cloned.1.call-update) | async-done | bytes 147472 | tf_op jit(solution)/shard_map/reduce_scatter | solution.py:325
  361.2 147.7 %reduce-scatter.8.cloned.1.call-done = f32[24,3352]{1,0:T(8,128)} async-done(((f32[768,3352]{1,0:T(8,128)}), f32[24,3352]{1,0:T(8,128)}) %reduce-scatter.8.cloned.1.call-update) | async-done | bytes 321808
  (265 shorter events, 86.7 us)
Async XLA Ops:
  7.2 96.9 %all-gather.8.cloned.1.call-start = ((), (), s32[]{:S(2)}) async-start(), calls=%async_computation.2 | async-start | bytes 5474304 | tf_op jit(solution)/shard_map/all_gather | solution.py:183
  7.9 138.9 %all-gather.12.cloned.1.call-start = ((), (), s32[]{:S(2)}) async-start(), calls=%async_computation.5 | async-start | bytes 3932160 | tf_op jit(solution)/shard_map/all_gather | solution.py:26
  99.6 8.1 %copy-start.58 = (s32[1,128]{1,0:T(1,128)}, s32[1,128]{1,0:T(1,128)S(1)}, u32[]{:S(2)}) copy-start(s32[1,128]{1,0:T(1,128)S(1)} %get-tuple-element.267) | copy-start | bytes 1540
  101.3 6.4 %copy-start.55 = (f32[128]{0:T(128)}, f32[128]{0:T(128)S(1)}, u32[]{:S(2)}) copy-start(f32[128]{0:T(128)S(1)} %fusion.97) | copy-start | bytes 1540
  102.0 8.0 %copy-start.66 = (f32[24]{0:T(128)}, f32[24]{0:T(128)S(1)}, u32[]{:S(2)}) copy-start(f32[24]{0:T(128)S(1)} %exponential_negate_fusion) | copy-start | bytes 292
  104.1 6.7 %copy-start.53 = (f32[128]{0:T(128)}, f32[128]{0:T(128)S(1)}, u32[]{:S(2)}) copy-start(f32[128]{0:T(128)S(1)} %get-tuple-element.287) | copy-start | bytes 1540
  104.1 5.9 %copy-start.49 = (f32[24]{0:T(128)S(1)}, f32[24]{0:T(128)}, u32[]{:S(2)}) copy-start(f32[24]{0:T(128)} %param.22) | copy-start | bytes 292
  107.7 6.0 %collective-permute-start = (f32[1,3,1792]{2,0,1:T(1,128)S(1)}, f32[1,3,1792]{2,0,1:T(1,128)S(1)}, u32[]{:S(2)}, u32[]{:S(2)}) collective-permute-start(f32[1,3,1792]{2,0,1:T(1,128)S(1)} %copy.199), channel_id=1, source_target_pairs={{0,1},{1,2},{2,3},{4,5},{5,6},{6,7},{8,9},{9,10},{10,11},{12,13},{... | collective-permute-start | bytes 64520 | tf_op jit(solution)/shard_map/ppermute | solution.py:19
  113.7 5.5 %copy-start.32 = (f32[1,3,1792]{2,1,0:T(4,128)}, f32[1,3,1792]{2,1,0:T(4,128)S(1)}, u32[]{:S(2)}) copy-start(f32[1,3,1792]{2,1,0:T(4,128)S(1)} %copy.200) | copy-start | bytes 64516
  117.7 128.2 %copy-start.8 = (f32[1,128,1792]{2,1,0:T(8,128)}, f32[1,128,1792]{2,1,0:T(8,128)S(1)}, u32[]{:S(2)}) copy-start(f32[1,128,1792]{2,1,0:T(8,128)S(1)} %get-tuple-element.268) | copy-start | bytes 2752516
  120.6 5.4 %copy-start.10 = (f32[1,128,1536]{1,2,0:T(8,128)}, f32[1,128,1536]{1,2,0:T(8,128)S(1)}, u32[]{:S(2)}) copy-start(f32[1,128,1536]{1,2,0:T(8,128)S(1)} %copy.207) | copy-start | bytes 2359300
  122.3 84.5 %all-gather.10.cloned.1.call-start = ((), (), s32[]{:S(2)}) async-start(), calls=%async_computation.3 | async-start | bytes 2433024 | tf_op jit(solution)/shard_map/all_gather | solution.py:187
  123.0 123.9 %all-gather.14.cloned.1.call-start = ((), (), s32[]{:S(2)}) async-start(), calls=%async_computation.6 | async-start | bytes 3932160 | tf_op jit(solution)/shard_map/all_gather | solution.py:26
  147.9 6.7 %copy-start.14 = (f32[128,24,64]{0,2,1:T(8,128)}, f32[128,24,64]{0,2,1:T(8,128)S(1)}, u32[]{:S(2)}) copy-start(f32[128,24,64]{0,2,1:T(8,128)S(1)} %fusion.29) | copy-start | bytes 2359300
  219.4 141.8 %reduce-scatter.6.cloned.1.call-start = ((), (), s32[]{:S(2)}) async-start(), calls=%async_computation.4 | async-start | bytes 4866048 | tf_op jit(solution)/shard_map/reduce_scatter | solution.py:325
  228.2 7.8 %copy-start.64 = (f32[128]{0:T(128)S(1)}, f32[128]{0:T(128)}, u32[]{:S(2)}) copy-start(f32[128]{0:T(128)} %fusion.98) | copy-start | bytes 1540
  241.2 267.7 %reduce-scatter.8.cloned.1.call-start = ((), (), s32[]{:S(2)}) async-start(), calls=%async_computation.7 | async-start | bytes 10948608
  261.9 5.1 copy-start.26
  261.9 5.1 copy-start.59
  272.8 6.6 %collective-permute-start.1 = (f32[1,3,1792]{2,0,1:T(1,128)}, f32[1,3,1792]{2,0,1:T(1,128)}, u32[]{:S(2)}, u32[]{:S(2)}) collective-permute-start(f32[1,3,1792]{2,0,1:T(1,128)} %copy.219), channel_id=1, source_target_pairs={{1,0},{2,1},{3,2},{5,4},{6,5},{7,6},{9,8},{10,9},{11,10},{13,12},{... | collective-permute-start | bytes 64520 | tf_op jit(solution)/shard_map/ppermute | solution.py:19
  290.4 4.4 copy-start.43
  290.4 4.4 copy-start.57
  290.5 48.6 %copy-start.70 = (f32[128]{0:T(128)S(1)}, f32[128]{0:T(128)}, u32[]{:S(2)}) copy-start(f32[128]{0:T(128)} %copy-done.69) | copy-start | bytes 1540
  290.5 48.6 %copy-start.25 = (bf16[1,128,768]{2,1,0:T(8,128)(2,1)S(1)}, bf16[1,128,768]{2,1,0:T(8,128)(2,1)}, u32[]{:S(2)}) copy-start(bf16[1,128,768]{2,1,0:T(8,128)(2,1)} %param.27) | copy-start | bytes 589828
  (59 other events, 140.9 us)
Sparse Core Ops, SparseCore 0:
  10.9 68.4 all-gather.7
  122.4 24.3 all-gather.11
  149.7 56.9 all-gather.9
  219.5 27.3 all-gather.13
  252.8 108.3 reduce-scatter.5
  367.7 141.1 reduce-scatter.7
where the time goes:
time: 518 us; the launch traced here: 516 us
  waiting for transfers between devices  224 us (43%)
  blocking collectives  131 us (25%)
  matrix products  56.8 us (11%)
  local copies, waits for them, and re-layouts  45.2 us (9%)
  other arithmetic  37.5 us (7%)
  between operations  16.4 us (3%)
    unnamed x7, waiting for transfers between devices  149 us
    unnamed x2, blocking collectives  84.6 us
    all_gather x1, waiting for transfers between devices, on_device(): lax.all_gather(out_weight, ('dp', 'seq'), axis=0, tiled=True)  48.7 us
    all_gather x1, blocking collectives, on_device(): lax.all_gather(conv_weight, ('dp', 'seq'), axis=1, tiled=True)  40.9 us
    reduce_scatter x1, waiting for transfers between devices, on_device(): lax.psum_scatter(grad_out_w, ('dp', 'seq'), scatter_dimension=0, tiled=True)  21.3 us
    dot_general x3, matrix products, ssd_core(): inner_out = jnp.einsum('tsh,shp->thp', mixing, values, precision=PRECISE)  17 us
    unnamed x160, local copies, waits for them, and re-layouts  11 us
  transfers between devices with their start and end apart: 8, of which 5 were waited for; matrix products, arithmetic and copies ran while one was open for 21% of the time, Pallas kernels for 0%

commit v1 on v0

v1 whole, which is shorter than its diff:
```python
import jax
import jax.numpy as jnp
from jax import lax
from jax.experimental import pallas as pl
from jax.experimental.pallas import tpu as pltpu
from jax.sharding import PartitionSpec as P

HEAD_DIM = 64
STATE = 128
CONV = 4
CHUNK = 128
LANES = 128
EPSILON = 1e-05
FULL = lax.Precision.HIGHEST
F32 = jnp.float32
BF16 = jnp.bfloat16


def swap(x, axis, offset):
    count = lax.axis_size(axis)
    return lax.ppermute(x, axis, [(i, i ^ offset) for i in range(count)])


def tree_sum(parts):
    while len(parts) > 1:
        parts = [parts[i] + parts[i + 1] for i in range(0, len(parts), 2)]
    return parts[0]


def in_order(pieces, place):
    stacked = jnp.stack(pieces)
    return [lax.dynamic_index_in_dim(stacked, j ^ place, 0, False) for j in range(len(pieces))]


def gather_xor(x, axis):
    return [x] + [swap(x, axis, k) for k in range(1, lax.axis_size(axis))]


def scatter_xor(blocks, axis):
    place = lax.axis_index(axis)
    return [
        swap(lax.dynamic_index_in_dim(blocks, place ^ k, 0, False), axis, k)
        if k
        else lax.dynamic_index_in_dim(blocks, place, 0, False)
        for k in range(lax.axis_size(axis))
    ]


def inner_of(count):
    inner = 1
    while 2 * inner * inner < count:
        inner *= 2
    return inner


def gather_dp(x):
    count = lax.axis_size("dp")
    inner = inner_of(count)
    far = [x] + [swap(x, "dp", k * inner) for k in range(1, count // inner)]
    near = [[piece] + [swap(piece, "dp", j) for j in range(1, inner)] for piece in far]
    return [near[m // inner][m % inner] for m in range(count)]


def reduce_dp(grads):
    count = lax.axis_size("dp")
    inner = inner_of(count)
    place = lax.axis_index("dp")
    outer_place, inner_place = place // inner, place % inner
    shaped = grads.reshape(count // inner, inner, *grads.shape[1:])
    parts = []
    for j in range(inner):
        slab = lax.dynamic_index_in_dim(shaped, inner_place ^ j, 1, False)
        parts.append(swap(slab, "dp", j) if j else slab)
    near = tree_sum([p.astype(F32) for p in parts]).astype(BF16)
    parts = []
    for k in range(count // inner):
        slab = lax.dynamic_index_in_dim(near, outer_place ^ k, 0, False)
        parts.append(swap(slab, "dp", k * inner) if k else slab)
    return tree_sum([p.astype(F32) for p in parts])


def dot(a, b, ca, cb, precision=None):
    return lax.dot_general(
        a, b, (((ca,), (cb,)), ((), ())), precision=precision, preferred_element_type=F32
    )


def mm(a, b):
    return dot(a, b, 1, 0, FULL)


def mm_nt(a, b):
    return dot(a, b, 1, 1, FULL)


def mm_tn(a, b):
    return dot(a, b, 0, 0, FULL)


def softplus(x):
    small = jnp.exp(-jnp.abs(x))
    up = 1.0 + small
    down = up - 1.0
    log1p = jnp.where(down == 0.0, small, jnp.log(up) * (small / jnp.where(down == 0.0, 1.0, down)))
    return jnp.maximum(x, 0.0) + log1p


def expand_matrix(width):
    head = lax.broadcasted_iota(jnp.int32, (LANES, width), 0)
    column = lax.broadcasted_iota(jnp.int32, (LANES, width), 1)
    return (column // HEAD_DIM == head).astype(F32)


def triangle(lower):
    row = lax.broadcasted_iota(jnp.int32, (CHUNK, CHUNK), 0)
    column = lax.broadcasted_iota(jnp.int32, (CHUNK, CHUNK), 1)
    return row >= column if lower else row <= column


def masks_of(segment_col, segment_rows, i):
    far = (segment_col == segment_rows[i]).astype(F32)
    near = (segment_col == segment_rows[i + 1]).astype(F32)
    own = (segment_col == segment_rows[i + 2]) & triangle(True)
    return far, near, own


def lane_halves():
    lane = lax.broadcasted_iota(jnp.int32, (1, LANES), 1)
    low = (lane < HEAD_DIM).astype(F32)
    return low, 1.0 - low


def rms_inverse(x):
    return lax.rsqrt(jnp.mean(x * x, axis=-1, keepdims=True) + EPSILON)


def gain_row(weights, lane_of_gain):
    tail = weights[:, weights.shape[1] - LANES :]
    pick = (lax.broadcasted_iota(jnp.int32, (8, LANES), 1) == lane_of_gain).astype(BF16)
    return dot(pick, tail, 1, 1)[:1]


def decays(raw, heads):
    step = softplus(raw + heads[0:1])
    return step, step * (-jnp.exp(heads[1:2]))


def fill_sources(i, v, step, decay, expand, vd, vt, ecx):
    cumulative = mm(triangle(True).astype(F32), decay)
    step_x = mm(step, expand)
    cum_x = mm(cumulative, expand)
    last = cum_x[CHUNK - 1 :]
    vd_now = v * step_x
    vd[pl.ds(i * CHUNK, CHUNK), :] = vd_now
    vt[pl.ds((i + 2) * CHUNK, CHUNK), :] = vd_now * jnp.exp(last - cum_x)
    ecx[pl.ds(i * CHUNK + 8, CHUNK), :] = jnp.exp(cum_x)
    return cumulative, step_x, cum_x, last


def head_decay(cumulative, cumulative_t, own, h):
    gap = cumulative[:, h : h + 1] - cumulative_t[h : h + 1, :]
    return jnp.exp(jnp.where(own, gap, -1e30))


def forward_kernel(width, lane_of_gain):
    heads_here = width // HEAD_DIM

    def body(x_ref, w_ref, conv_ref, same_ref, seg_ref, segr_ref, head_ref, normed_ref, proj_ref, pre_ref, y_ref, bpad, vd, vt, ecx):
        x = x_ref[...].astype(F32)
        gain = gain_row(w_ref[...], lane_of_gain)
        normed_ref[...] = (x * rms_inverse(x) * gain).astype(BF16)
        proj_ref[...] = dot(normed_ref[...], w_ref[...], 1, 0)
        channels = width + 2 * STATE
        u = proj_ref[:, :channels]
        running = conv_ref[CONV : CONV + 1, :] + conv_ref[CONV - 1 : CONV, :] * u
        for back in range(1, CONV):
            tap = conv_ref[CONV - 1 - back : CONV - back, :]
            running = running + tap * pltpu.roll(u, back, 0) * same_ref[:, back : back + 1]
        pre_ref[...] = running
        bpad[pl.ds(0, 2 * CHUNK), :] = jnp.zeros((2 * CHUNK, STATE), F32)
        vt[pl.ds(0, 2 * CHUNK), :] = jnp.zeros((2 * CHUNK, width), F32)
        ecx[pl.ds(0, 8), :] = jnp.zeros((8, width), F32)
        b_pre = running[:, width : width + STATE]
        bpad[pl.ds(2 * CHUNK, x.shape[0]), :] = b_pre * jax.nn.sigmoid(b_pre)
        expand = expand_matrix(width)
        low, high = lane_halves()
        heads = head_ref[...]
        skip_x = mm(jnp.broadcast_to(heads[2:3], (8, LANES)), expand)[:1]

        def chunk(i, carry):
            rows = pl.ds(pl.multiple_of(i * CHUNK, CHUNK), CHUNK)
            v_pre = pre_ref[rows, :width]
            c_pre = pre_ref[rows, width + STATE :]
            v = v_pre * jax.nn.sigmoid(v_pre)
            c = c_pre * jax.nn.sigmoid(c_pre)
            step, decay = decays(proj_ref[rows, channels:], heads)
            cumulative, _, _, _ = fill_sources(i, v, step, decay, expand, vd, vt, ecx)
            cumulative_t = cumulative.T
            far, near, own = masks_of(seg_ref[rows, :], segr_ref, i)
            window = pl.ds(pl.multiple_of(i * CHUNK, CHUNK), 3 * CHUNK)
            scores = mm_nt(c, bpad[window, :])
            s_far = scores[:, :CHUNK] * far
            s_near = scores[:, CHUNK : 2 * CHUNK] * near
            s_own = scores[:, 2 * CHUNK :]
            ecx_now = ecx[pl.ds(pl.multiple_of(i * CHUNK, 8) + 8, CHUNK), :]
            last_before = ecx[pl.ds(pl.multiple_of(i * CHUNK, 8), 8), :][7:8]
            vt_far = vt[rows, :] * last_before
            vt_near = vt[pl.ds(pl.multiple_of((i + 1) * CHUNK, CHUNK), CHUNK), :]
            off = mm(s_far, vt_far) + mm(s_near, vt_near)
            y_ref[rows, :] = off * ecx_now + skip_x * v
            for pair in range(heads_here // 2):
                lanes = slice(pair * LANES, (pair + 1) * LANES)
                n0 = s_own * head_decay(cumulative, cumulative_t, own, 2 * pair)
                n1 = s_own * head_decay(cumulative, cumulative_t, own, 2 * pair + 1)
                vp = vd[rows, lanes]
                both = mm(jnp.concatenate([n0, n1], 1), jnp.concatenate([vp * low, vp * high], 0))
                y_ref[rows, lanes] = y_ref[rows, lanes] + both
            return carry

        lax.fori_loop(0, x.shape[0] // CHUNK, chunk, 0)

    return body


def gate_kernel(width):
    def body(normed_ref, wg_ref, og_ref, wo_ref, y_ref, gain_ref, gate_ref, dg_ref, stats_ref):
        gate = dot(normed_ref[...], wg_ref[...], 1, 0)
        gate_ref[...] = gate
        d_gated = dot(og_ref[...], wo_ref[...], 1, 1)
        dg_ref[...] = d_gated
        v = y_ref[...] * (gate * jax.nn.sigmoid(gate))
        squares = jnp.sum(v * v, axis=1, keepdims=True)
        cross = jnp.sum(v * (d_gated * gain_ref[...]), axis=1, keepdims=True)
        lane = lax.broadcasted_iota(jnp.int32, (CHUNK, LANES), 1)
        for i in range(stats_ref.shape[0]):
            rows = slice(i * CHUNK, (i + 1) * CHUNK)
            both = jnp.where(lane == 0, squares[rows], jnp.where(lane == 1, cross[rows], 0.0))
            stats_ref[i] = both.T[:8]

    return body


def out_kernel(width, whole_width):
    def body(stats_ref, normed_ref, gate_ref, dg_ref, y_ref, gain_ref, og_ref, wo_ref, out_ref, gout_ref, ggate_ref, dgate_ref, dy_ref, ggain_ref):
        columns = []
        for i in range(stats_ref.shape[0]):
            square = jnp.concatenate([stats_ref[i], jnp.zeros((CHUNK - 8, LANES), F32)], 0)
            columns.append(square.T)
        columns = jnp.concatenate(columns, 0)
        inverse = lax.rsqrt(columns[:, 0:1] / whole_width + EPSILON)
        cross = columns[:, 1:2] / whole_width
        gate = gate_ref[...]
        sig = jax.nn.sigmoid(gate)
        silu = gate * sig
        y = y_ref[...]
        v = y * silu
        gain = gain_ref[...]
        scaled = v * inverse
        gated = (scaled * gain).astype(BF16)
        out_ref[...] = dot(gated, wo_ref[...], 1, 0).astype(BF16)
        gout_ref[...] = dot(gated, og_ref[...], 0, 0).astype(BF16)
        d_gated = dg_ref[...]
        ggain_ref[...] = jnp.broadcast_to(jnp.sum(d_gated * scaled, axis=0, keepdims=True), (8, width))
        dv = inverse * (d_gated * gain - v * (inverse * inverse * cross))
        dy_ref[...] = dv * silu
        dgate = (dv * y * (sig * (1.0 + gate * (1.0 - sig)))).astype(BF16)
        dgate_ref[...] = dgate
        ggate_ref[...] = dot(normed_ref[...], dgate, 0, 0).astype(BF16)

    return body


def backward_kernel(width, lane_of_gain):
    heads_here = width // HEAD_DIM

    def body(x_ref, normed_ref, w_ref, wg_ref, conv_ref, same_ref, seg_ref, segr_ref, head_ref, proj_ref, pre_ref, y_ref, dy_ref, dgate_ref, gin_ref, dn_ref, conv_grad_ref, head_grad_ref, norm_grad_ref, bpad, vd, vt, ecx, tailx, stepx, cums, ua, db, dpre, draw):
        length = x_ref.shape[0]
        chunks = length // CHUNK
        channels = width + 2 * STATE
        expand = expand_matrix(width)
        low, high = lane_halves()
        heads = head_ref[...]
        rate = jnp.exp(heads[1:2])
        skip_x = mm(jnp.broadcast_to(heads[2:3], (8, LANES)), expand)[:1]
        bpad[pl.ds(0, 2 * CHUNK), :] = jnp.zeros((2 * CHUNK, STATE), F32)
        vt[pl.ds(0, 2 * CHUNK), :] = jnp.zeros((2 * CHUNK, width), F32)
        tailx[pl.ds(0, 2 * CHUNK), :] = jnp.zeros((2 * CHUNK, width), F32)
        ecx[pl.ds(0, 8), :] = jnp.zeros((8, width), F32)
        b_pre = pre_ref[:, width : width + STATE]
        bpad[pl.ds(2 * CHUNK, length), :] = b_pre * jax.nn.sigmoid(b_pre)
        ua[...] = jnp.zeros(ua.shape, F32)
        db[...] = jnp.zeros(db.shape, F32)

        def prepare(i, carry):
            rows = pl.ds(pl.multiple_of(i * CHUNK, CHUNK), CHUNK)
            v_pre = pre_ref[rows, :width]
            v = v_pre * jax.nn.sigmoid(v_pre)
            step, decay = decays(proj_ref[rows, channels:], heads)
            cumulative, step_x, cum_x, last = fill_sources(i, v, step, decay, expand, vd, vt, ecx)
            cums[rows, :] = cumulative
            stepx[rows, :] = step_x
            tailx[pl.ds(pl.multiple_of((i + 2) * CHUNK, CHUNK), CHUNK), :] = jnp.exp(last - cum_x)
            return carry

        lax.fori_loop(0, chunks, prepare, 0)

        def chunk(turn, carry):
            later, g_bias, g_rate, g_skip = carry
            i = chunks - 1 - turn
            rows = pl.ds(pl.multiple_of(i * CHUNK, CHUNK), CHUNK)
            rows_near = pl.ds(pl.multiple_of((i + 1) * CHUNK, CHUNK), CHUNK)
            rows_own = pl.ds(pl.multiple_of((i + 2) * CHUNK, CHUNK), CHUNK)
            window = pl.ds(pl.multiple_of(i * CHUNK, CHUNK), 3 * CHUNK)
            v_pre = pre_ref[rows, :width]
            v_sig = jax.nn.sigmoid(v_pre)
            v = v_pre * v_sig
            c_pre = pre_ref[rows, width + STATE :]
            c_sig = jax.nn.sigmoid(c_pre)
            c = c_pre * c_sig
            raw = proj_ref[rows, channels:]
            step, decay = decays(raw, heads)
            cumulative = cums[rows, :]
            cumulative_t = cumulative.T
            far, near, own = masks_of(seg_ref[rows, :], segr_ref, i)
            b_window = bpad[window, :]
            scores = mm_nt(c, b_window)
            s_far = scores[:, :CHUNK] * far
            s_near = scores[:, CHUNK : 2 * CHUNK] * near
            s_own = scores[:, 2 * CHUNK :]
            dy = dy_ref[rows, :]
            dye = dy * ecx[pl.ds(pl.multiple_of(i * CHUNK, 8) + 8, CHUNK), :]
            dye_far = dye * ecx[pl.ds(pl.multiple_of(i * CHUNK, 8), 8), :][7:8]
            ds_far = mm_nt(dye_far, vt[rows, :]) * far
            ds_near = mm_nt(dye, vt[rows_near, :]) * near
            ua[rows, :] = ua[rows, :] + tailx[rows, :] * mm_tn(s_far, dye_far)
            ua[rows_near, :] = ua[rows_near, :] + tailx[rows_near, :] * mm_tn(s_near, dye)
            ds_own = jnp.zeros((CHUNK, CHUNK), F32)
            for pair in range(heads_here // 2):
                lanes = slice(pair * LANES, (pair + 1) * LANES)
                d0 = head_decay(cumulative, cumulative_t, own, 2 * pair)
                d1 = head_decay(cumulative, cumulative_t, own, 2 * pair + 1)
                dyp = dy_ref[rows, lanes]
                split = jnp.concatenate([dyp * low, dyp * high], 0)
                dm = mm_nt(split, vd[rows, lanes])
                ds_own = ds_own + dm[:CHUNK] * d0 + dm[CHUNK:] * d1
                u_pair = mm_tn(jnp.concatenate([s_own * d0, s_own * d1], 0), split)
                ua[rows_own, lanes] = ua[rows_own, lanes] + u_pair
            ds_all = jnp.concatenate([ds_far, ds_near, ds_own], 1)
            dc = mm(ds_all, b_window)
            db[window, :] = db[window, :] + mm_tn(ds_all, c)
            u_total = ua[rows_own, :]
            received = dot(dy * (y_ref[rows, :] - skip_x * v), expand, 1, 1, FULL)
            d_step = dot(v * u_total, expand, 1, 1, FULL)
            gap = received - step * d_step
            d_decay = mm(triangle(False).astype(F32), gap) + later
            d_step = d_step - d_decay * rate
            d_raw = d_step * jax.nn.sigmoid(raw + heads[0:1])
            draw[rows, :] = d_raw
            dv = stepx[rows, :] * u_total + skip_x * dy
            dpre[rows, :width] = dv * (v_sig * (1.0 + v_pre * (1.0 - v_sig)))
            b_pre = pre_ref[rows, width : width + STATE]
            b_sig = jax.nn.sigmoid(b_pre)
            dpre[rows, width : width + STATE] = db[rows_own, :] * (b_sig * (1.0 + b_pre * (1.0 - b_sig)))
            dpre[rows, width + STATE :] = dc * (c_sig * (1.0 + c_pre * (1.0 - c_sig)))
            g_skip = g_skip + jnp.sum(dot(dy * v, expand, 1, 1, FULL), axis=0, keepdims=True)
            g_bias = g_bias + jnp.sum(d_raw, axis=0, keepdims=True)
            g_rate = g_rate + jnp.sum(d_decay * decay, axis=0, keepdims=True)
            return (later + jnp.sum(gap, axis=0, keepdims=True), g_bias, g_rate, g_skip)

        none = jnp.zeros((1, LANES), F32)
        _, g_bias, g_rate, g_skip = lax.fori_loop(0, chunks, chunk, (none, none, none, none))
        head_grad_ref[...] = jnp.concatenate([g_bias, g_rate, g_skip, jnp.zeros((5, LANES), F32)], 0)
        u = proj_ref[:, :channels]
        d = dpre[...]
        du = conv_ref[CONV - 1 : CONV, :] * d
        taps = [jnp.sum(d * u, axis=0, keepdims=True)]
        for back in range(1, CONV):
            masked = d * same_ref[:, back : back + 1]
            taps.insert(0, jnp.sum(masked * pltpu.roll(u, back, 0), axis=0, keepdims=True))
            du = du + conv_ref[CONV - 1 - back : CONV - back, :] * pltpu.roll(masked, length - back, 0)
        taps.append(jnp.sum(d, axis=0, keepdims=True))
        taps.append(jnp.zeros((8 - CONV - 1, channels), F32))
        conv_grad_ref[...] = jnp.concatenate(taps, 0)
        d_proj = jnp.concatenate([du, draw[...]], 1).astype(BF16)
        gin_ref[...] = dot(normed_ref[...], d_proj, 0, 0).astype(BF16)
        dn = dot(d_proj, w_ref[...], 1, 1) + dot(dgate_ref[...], wg_ref[...], 1, 1)
        dn_ref[...] = dn.astype(BF16)
        x = x_ref[...].astype(F32)
        norm_grad_ref[...] = jnp.broadcast_to(
            jnp.sum(dn * (x * rms_inverse(x)), axis=0, keepdims=True), (8, x.shape[1])
        )

    return body


def call(body, outs, scratch, *operands):
    vmem = pl.BlockSpec(memory_space=pltpu.VMEM)
    return pl.pallas_call(
        body,
        out_shape=[jax.ShapeDtypeStruct(shape, kind) for shape, kind in outs],
        in_specs=[vmem] * len(operands),
        out_specs=[vmem] * len(outs),
        scratch_shapes=[pltpu.VMEM(shape, F32) for shape in scratch],
        compiler_params=pltpu.CompilerParams(vmem_limit_bytes=50 * 2**20),
    )(*operands)


def slots(flat, rows):
    owners, count = flat.shape
    lanes = -(-count // rows)
    return jnp.pad(flat, ((0, 0), (0, lanes * rows - count))).reshape(owners * rows, lanes)


def on_device(
    hidden_in,
    segments,
    norm_gain,
    in_weight,
    conv_weight,
    conv_bias,
    step_bias,
    decay_log,
    skip_weight,
    gate_gain,
    out_weight,
    out_grad,
):
    row_count, piece, model = hidden_in.shape
    assert row_count == 1
    seq_n, dp_n = lax.axis_size("seq"), lax.axis_size("dp")
    owners = seq_n * dp_n
    place, dp_place = lax.axis_index("seq"), lax.axis_index("dp")
    length = piece * seq_n
    head_count = step_bias.shape[0]
    inner = head_count * HEAD_DIM
    heads_here = head_count // seq_n
    width = inner // seq_n
    channels = width + 2 * STATE
    cols = channels + LANES
    rows = in_weight.shape[0]
    conv_here = conv_bias.shape[0]
    gate_here = gate_gain.shape[0]

    conv_flat = jnp.concatenate([conv_weight.reshape(1, -1), conv_bias.reshape(1, -1)], 1)
    conv_slots = slots(conv_flat, rows)
    gate_slots = slots(gate_gain.reshape(1, -1), rows)
    conv_lanes, gate_lanes = conv_slots.shape[1], gate_slots.shape[1]
    rest = LANES - heads_here - 1 - conv_lanes - gate_lanes
    shared = [norm_gain[:, None], conv_slots, gate_slots, jnp.zeros((rows, rest), BF16)]
    both_states = in_weight[:, 2 * inner : 2 * inner + 2 * STATE]
    to_send = []
    for j in range(seq_n):
        first = 2 * inner + 2 * STATE + j * heads_here
        to_send.append(
            jnp.concatenate(
                [in_weight[:, inner + j * width : inner + (j + 1) * width], both_states]
                + [in_weight[:, first : first + heads_here]]
                + shared
                + [in_weight[:, j * width : (j + 1) * width]],
                axis=1,
            )
        )
    mine = jnp.concatenate(in_order(scatter_xor(jnp.stack(to_send), "seq"), place), 0)
    first_part, gate_part = mine[:, :cols], mine[:, cols:]
    w_first = jnp.concatenate(in_order(gather_dp(first_part), dp_place), 0)

    acts = in_order(gather_xor(jnp.stack([hidden_in[0], out_grad[0]]), "seq"), place)
    x_row = jnp.concatenate([a[0] for a in acts], 0)
    og_row = jnp.concatenate([a[1] for a in acts], 0)

    def linear(d, s):
        return d * seq_n + s

    to_heads = [(b, linear(b % dp_n, b // dp_n)) for b in range(owners)]
    out_block = lax.ppermute(out_weight, ("dp", "seq"), to_heads)
    out_rows = out_block.shape[0]
    folded = jnp.concatenate(
        [out_block[:, k * width : (k + 1) * width] for k in range(model // width)], 0
    )
    second = jnp.concatenate([gate_part, folded], 1)
    w_second = in_order(gather_dp(second), dp_place)
    w_gate = jnp.concatenate([p[:, :width] for p in w_second], 0)
    w_out = jnp.concatenate(
        [
            jnp.concatenate(
                [p[k * out_rows : (k + 1) * out_rows, width:] for k in range(model // width)], 1
            )
            for p in w_second
        ],
        0,
    )

    tail = w_first[:, channels:]
    at = heads_here + 1
    conv_all = tail[:, at : at + conv_lanes].reshape(owners, rows * conv_lanes)
    conv_all = conv_all[:, : (CONV + 1) * conv_here].reshape(owners, CONV + 1, conv_here)
    conv_all = conv_all.transpose(1, 0, 2).reshape(CONV + 1, owners * conv_here)
    conv_mine = jnp.concatenate(
        [
            lax.dynamic_slice_in_dim(conv_all[:, :inner], place * width, width, 1),
            conv_all[:, inner:],
        ],
        1,
    )
    conv_mine = jnp.pad(conv_mine.astype(F32), ((0, 8 - CONV - 1), (0, 0)))
    at = at + conv_lanes
    gain_all = tail[:, at : at + gate_lanes].reshape(owners, rows * gate_lanes)[:, :gate_here]
    gain_mine = lax.dynamic_slice_in_dim(gain_all.reshape(1, inner), place * width, width, 1)
    gain_mine = gain_mine.astype(F32)

    head_params = jnp.stack([step_bias, decay_log, skip_weight])
    head_params = lax.dynamic_slice_in_dim(head_params, place * heads_here, heads_here, 1)
    head_params = jnp.pad(head_params, ((0, 5), (0, LANES - heads_here)))
    row_segments = segments[0]
    same = [jnp.ones((length,), F32)]
    for back in range(1, CONV):
        matches = (row_segments[back:] == row_segments[:-back]).astype(F32)
        same.append(jnp.concatenate([jnp.zeros((back,), F32), matches]))
    same = jnp.pad(jnp.stack(same, 1), ((0, 0), (0, 8 - CONV)))
    segment_col = row_segments[:, None]
    padded = jnp.concatenate([jnp.full((2 * CHUNK,), -1, jnp.int32), row_segments])
    segment_rows = padded.reshape(-1, 1, CHUNK)

    chunks = length // CHUNK
    tall = length + 2 * CHUNK
    sources = [(tall, STATE), (length, width), (tall, width), (length + 8, width)]
    normed, proj, pre, y = call(
        forward_kernel(width, heads_here),
        [((length, model), BF16), ((length, cols), F32), ((length, channels), F32), ((length, width), F32)],
        sources,
        x_row, w_first, conv_mine, same, segment_col, segment_rows, head_params,
    )
    gate, d_gated, stats = call(
        gate_kernel(width),
        [((length, width), F32), ((length, width), F32), ((chunks, 8, LANES), F32)],
        [],
        normed, w_gate, og_row, w_out, y, gain_mine,
    )
    step = 1
    while step < seq_n:
        stats = stats + swap(stats, "seq", step)
        step *= 2
    out_part, g_out, g_gate, d_gate, dy, g_gain = call(
        out_kernel(width, inner),
        [((length, model), BF16), ((width, model), BF16), ((model, width), BF16)]
        + [((length, width), BF16), ((length, width), F32), ((8, width), F32)],
        [],
        stats, normed, gate, d_gated, y, gain_mine, og_row, w_out,
    )

    g_out = g_out.reshape(dp_n, out_rows, model)
    g_out = jnp.concatenate(
        [g_out[:, :, k * width : (k + 1) * width] for k in range(model // width)], 1
    )
    early = reduce_dp(jnp.concatenate([g_gate.reshape(dp_n, -1, width), g_out], 2))
    own_out = early[:, width:]
    own_out = jnp.concatenate(
        [own_out[k * out_rows : (k + 1) * out_rows] for k in range(model // width)], 1
    )
    back_pairs = [(target, source) for source, target in to_heads]
    grad_out_w = lax.ppermute(own_out, ("dp", "seq"), back_pairs)
    result = tree_sum(
        [p.astype(F32) for p in scatter_xor(out_part.reshape(seq_n, piece, model), "seq")]
    )
    result = hidden_in[0].astype(F32) + result

    g_in, dn, conv_grad, head_grad, norm_grad = call(
        backward_kernel(width, heads_here),
        [((model, cols), BF16), ((length, model), BF16), ((8, channels), F32)]
        + [((8, LANES), F32), ((8, model), F32)],
        sources
        + [(tall, width), (length, width), (length, LANES), (tall, width), (tall, STATE)]
        + [(length, channels), (length, LANES)],
        x_row, normed, w_first, w_gate, conv_mine, same, segment_col, segment_rows, head_params,
        proj, pre, y, dy, d_gate,
    )

    conv_full = jnp.zeros((CONV + 1, inner), F32)
    conv_full = lax.dynamic_update_slice_in_dim(
        conv_full, conv_grad[: CONV + 1, :width], place * width, 1
    )
    conv_full = jnp.concatenate([conv_full, conv_grad[: CONV + 1, width:]], 1)
    conv_full = conv_full.reshape(CONV + 1, owners, conv_here).transpose(1, 0, 2)
    gain_full = lax.dynamic_update_slice_in_dim(
        jnp.zeros((inner,), F32), g_gain[0], place * width, 0
    )
    heads_full = lax.dynamic_update_slice_in_dim(
        jnp.zeros((3, head_count), F32), head_grad[:3, :heads_here], place * heads_here, 1
    )
    small = jnp.concatenate(
        [
            norm_grad[0].reshape(owners, rows),
            conv_full.reshape(owners, -1),
            gain_full.reshape(owners, gate_here),
            jnp.broadcast_to(heads_full.reshape(1, -1), (owners, 3 * head_count)),
        ],
        1,
    )
    small_count = small.shape[1]
    small = slots(small, rows).astype(BF16)
    small_lanes = small.shape[1]
    tail_block = g_in[:, channels:] + jnp.pad(
        small, ((0, 0), (heads_here, LANES - heads_here - small_lanes))
    )
    late = jnp.concatenate([g_in[:, :channels], tail_block], 1).reshape(dp_n, -1, cols)
    late = reduce_dp(late)
    dn_parts = scatter_xor(dn.reshape(seq_n, piece, model), "seq")
    d_normed = tree_sum([p.astype(F32) for p in dn_parts])

    both = jnp.concatenate([late, early[:, :width]], 1).reshape(seq_n, rows, cols + width)
    parts = scatter_xor(both, "seq")
    ordered = in_order(parts, place)
    grad_in_w = jnp.concatenate(
        [b[:, cols:] for b in ordered]
        + [b[:, :width] for b in ordered]
        + [tree_sum([p[:, width:channels] for p in parts])]
        + [b[:, channels : channels + heads_here] for b in ordered],
        1,
    )
    first = channels + heads_here
    small = tree_sum([p[:, first : first + small_lanes] for p in parts])
    small = small.reshape(-1)[:small_count]
    at = rows
    grad_norm = small[:at]
    conv_own = small[at : at + (CONV + 1) * conv_here].reshape(CONV + 1, conv_here)
    at += (CONV + 1) * conv_here
    grad_gain = small[at : at + gate_here]
    at += gate_here
    head_own = small[at:].reshape(3, head_count)

    widened = hidden_in[0].astype(F32)
    inverse = lax.rsqrt(jnp.mean(widened * widened, axis=-1, keepdims=True) + EPSILON)
    gain_full_row = tail[:, heads_here].astype(F32)[None, :]
    scaled = d_normed * gain_full_row
    along = jnp.mean(scaled * widened, axis=-1, keepdims=True)
    grad_hidden = out_grad[0].astype(F32) + inverse * (scaled - widened * (inverse * inverse * along))
    return (
        result[None],
        grad_hidden[None],
        grad_norm,
        grad_in_w,
        conv_own[:CONV],
        conv_own[CONV],
        head_own[0],
        head_own[1],
        head_own[2],
        grad_gain,
        grad_out_w,
    )


def solution(mesh):
    in_specs = (
        P("dp", "seq", None),
        P("dp", None),
        P(("dp", "seq")),
        P(("dp", "seq"), None),
        P(None, ("dp", "seq")),
        P(("dp", "seq")),
        P(),
        P(),
        P(),
        P(("dp", "seq")),
        P(("dp", "seq"), None),
        P("dp", "seq", None),
    )
    out_specs = (
        P("dp", "seq", None),
        P("dp", "seq", None),
        P(("dp", "seq")),
        P(("dp", "seq"), None),
        P(None, ("dp", "seq")),
        P(("dp", "seq")),
        P(),
        P(),
        P(),
        P(("dp", "seq")),
        P(("dp", "seq"), None),
    )
    return jax.shard_map(
        on_device, mesh=mesh, in_specs=in_specs, out_specs=out_specs, check_vma=False
    )
```

time: 518 us -> 191 us (0.37)
  waiting for transfers between devices: 224 us -> 73.6 us
  blocking collectives: 131 us -> 0 us
  matrix products: 56.8 us -> 0 us
  starting transfers between devices: 4.24 us -> 43.6 us
  Pallas kernels: 0 us -> 35.7 us
  other arithmetic: 37.5 us -> 9.29 us
  local copies, waits for them, and re-layouts: 45.2 us -> 24 us
  between operations: 16.4 us -> 1.8 us
    unnamed x7 -> x0, waiting for transfers between devices: 149 us -> none
    unnamed x2 -> x0, blocking collectives: 84.6 us -> none
    ppermute x2 -> x41, waiting for transfers between devices: 0.01 us -> 73.6 us  [the longest x39 73.6 us: swap(): return lax.ppermute(x, axis, [(i, i ^ offset) for i in range(count)])]
    dot_general x18 -> x0, matrix products: 56.8 us -> none  [the longest x3 17 us: ssd_core(): inner_out = jnp.einsum('tsh,shp->thp', mixing, values, precision=PRECISE)]
    all_gather x4 -> x0, waiting for transfers between devices: 54.1 us -> none  [the longest x1 48.7 us: on_device(): lax.all_gather(out_weight, ('dp', 'seq'), axis=0, tiled=True)]
    all_gather x2 -> x0, blocking collectives: 46.2 us -> none  [the longest x1 40.9 us: on_device(): lax.all_gather(conv_weight, ('dp', 'seq'), axis=1, tiled=True)]
    ppermute x2 -> x41, starting transfers between devices: 3.78 us -> 43.6 us  [the longest x39 42.3 us: swap(): return lax.ppermute(x, axis, [(i, i ^ offset) for i in range(count)])]
    pallas_call x0 -> x4, Pallas kernels: none -> 35.7 us  [call(): pl.pallas_call(body, out_shape=[jax.ShapeDtypeStruct(shape, kind) for sha...]
  transfers between devices with their start and end apart: 8 -> 41, of which waited for: 5 -> 24; matrix products, arithmetic and copies ran while one was open for 21% -> 11% of each run, Pallas kernels for 0% -> 11%
where the time goes in v1:
time: 191 us; the launch traced here: 188 us
  waiting for transfers between devices  73.6 us (39%)
  starting transfers between devices  43.6 us (23%)
  Pallas kernels  35.7 us (19%)
  local copies, waits for them, and re-layouts  24 us (13%)
  other arithmetic  9.29 us (5%)
    ppermute x39, waiting for transfers between devices, swap(): return lax.ppermute(x, axis, [(i, i ^ offset) for i in range(count)])  73.6 us
    ppermute x39, starting transfers between devices, swap(): return lax.ppermute(x, axis, [(i, i ^ offset) for i in range(count)])  42.3 us
    pallas_call x4, Pallas kernels, call(): pl.pallas_call(body, out_shape=[jax.ShapeDtypeStruct(shape, kind) for sha...  35.7 us
    unnamed x85, local copies, waits for them, and re-layouts  10 us
  transfers between devices with their start and end apart: 41, of which 24 were waited for; matrix products, arithmetic and copies ran while one was open for 11% of the time, Pallas kernels for 11%

profile of v1, /device:TPU:0, one launch (start us, length us, event | category | flops | bytes accessed | tf_op | source)
XLA Modules:
  0.0 188.0 jit_solution(3337584235868104961)
XLA Ops:
  3.3 2.6 %collective-permute-start.1 = (bf16[2,128,768]{2,1,0:T(8,128)(2,1)S(1)}, bf16[2,128,768]{2,1,0:T(8,128)(2,1)}, u32[]{:S(2)}, u32[]{:S(2)}) collective-permute-start(bf16[2,128,768]{2,1,0:T(8,128)(2,1)S(1)} %constant_dynamic-update-slice_fusion), channel_id=1, source_target_pairs={{0,2},{1,3},{2,0},{3,1},{4,6},{5,7},{6,4},{7,5},{8,10},{9,11},{10,... | collective-permute-start | bytes 1179656 | tf_op jit(solution)/shard_map/ppermute | solution.py:21
  14.4 2.6 %collective-permute-done.4 = bf16[24,1152]{1,0:T(8,128)(2,1)S(1)} collective-permute-done((bf16[24,1152]{1,0:T(8,128)(2,1)S(1)}, bf16[24,1152]{1,0:T(8,128)(2,1)S(1)}, u32[]{:S(2)}, u32[]{:S(2)}) %collective-permute-start.4) | collective-permute-done | bytes 55328 | tf_op jit(solution)/shard_map/ppermute | solution.py:21
  17.8 2.2 %collective-permute-start.6 = (bf16[96,768]{1,0:T(8,128)(2,1)S(1)}, bf16[96,768]{1,0:T(8,128)(2,1)S(1)}, u32[]{:S(2)}, u32[]{:S(2)}) collective-permute-start(bf16[96,768]{1,0:T(8,128)(2,1)S(1)} %slice.447), channel_id=1, source_target_pairs={{0,4},{4,0},{8,12},{12,8},{16,20},{20,16},{24,28},{28,24},{1,5},{5... | collective-permute-start | bytes 442376 | tf_op jit(solution)/shard_map/ppermute | solution.py:21
  20.9 4.1 %collective-permute-start.9 = (bf16[96,768]{1,0:T(8,128)(2,1)S(1)}, bf16[96,768]{1,0:T(8,128)(2,1)S(1)}, u32[]{:S(2)}, u32[]{:S(2)}) collective-permute-start(bf16[96,768]{1,0:T(8,128)(2,1)S(1)} %slice.447), channel_id=1, source_target_pairs={{0,16},{4,20},{8,24},{12,28},{16,0},{20,4},{24,8},{28,12},{1,17},{... | collective-permute-start | bytes 442376 | tf_op jit(solution)/shard_map/ppermute | solution.py:21
  25.7 3.4 %collective-permute-start.11 = (bf16[96,768]{1,0:T(8,128)(2,1)S(1)}, bf16[96,768]{1,0:T(8,128)(2,1)S(1)}, u32[]{:S(2)}, u32[]{:S(2)}) collective-permute-start(bf16[96,768]{1,0:T(8,128)(2,1)S(1)} %slice.447), channel_id=1, source_target_pairs={{0,24},{4,28},{8,16},{12,20},{16,8},{20,12},{24,0},{28,4},{1,25},{... | collective-permute-start | bytes 442376 | tf_op jit(solution)/shard_map/ppermute | solution.py:21
  29.3 6.2 %collective-permute-done.14 = bf16[96,768]{1,0:T(8,128)(2,1)S(1)} collective-permute-done((bf16[96,768]{1,0:T(8,128)(2,1)}, bf16[96,768]{1,0:T(8,128)(2,1)S(1)}, u32[]{:S(2)}, u32[]{:S(2)}) %collective-permute-start.14) | collective-permute-done | bytes 147488 | tf_op jit(solution)/shard_map/ppermute | solution.py:21
  35.4 5.3 %collective-permute-done.15 = bf16[96,768]{1,0:T(8,128)(2,1)S(1)} collective-permute-done((bf16[96,768]{1,0:T(8,128)(2,1)}, bf16[96,768]{1,0:T(8,128)(2,1)S(1)}, u32[]{:S(2)}, u32[]{:S(2)}) %collective-permute-start.15) | collective-permute-done | bytes 147488 | tf_op jit(solution)/shard_map/ppermute | solution.py:21
  42.1 4.2 %collective-permute-done.8 = bf16[96,768]{1,0:T(8,128)(2,1)S(1)} collective-permute-done((bf16[96,768]{1,0:T(8,128)(2,1)S(1)}, bf16[96,768]{1,0:T(8,128)(2,1)S(1)}, u32[]{:S(2)}, u32[]{:S(2)}) %collective-permute-start.8) | collective-permute-done | bytes 147488 | tf_op jit(solution)/shard_map/ppermute | solution.py:21
  48.5 4.1 %collective-permute-done.10 = bf16[96,768]{1,0:T(8,128)(2,1)S(1)} collective-permute-done((bf16[96,768]{1,0:T(8,128)(2,1)S(1)}, bf16[96,768]{1,0:T(8,128)(2,1)S(1)}, u32[]{:S(2)}, u32[]{:S(2)}) %collective-permute-start.10) | collective-permute-done | bytes 147488 | tf_op jit(solution)/shard_map/ppermute | solution.py:21
  52.6 6.3 %collective-permute-done.12 = bf16[96,768]{1,0:T(8,128)(2,1)S(1)} collective-permute-done((bf16[96,768]{1,0:T(8,128)(2,1)S(1)}, bf16[96,768]{1,0:T(8,128)(2,1)S(1)}, u32[]{:S(2)}, u32[]{:S(2)}) %collective-permute-start.12) | collective-permute-done | bytes 147488 | tf_op jit(solution)/shard_map/ppermute | solution.py:21
  68.2 2.3 %collective-permute-done.20 = bf16[96,768]{1,0:T(8,128)(2,1)S(1)} collective-permute-done((bf16[96,768]{1,0:T(8,128)(2,1)}, bf16[96,768]{1,0:T(8,128)(2,1)S(1)}, u32[]{:S(2)}, u32[]{:S(2)}) %collective-permute-start.20) | collective-permute-done | bytes 147488 | tf_op jit(solution)/shard_map/ppermute | solution.py:21
  74.3 8.2 %shard_map.203 = (bf16[512,768]{1,0:T(8,128)(2,1)S(1)}, f32[512,768]{1,0:T(8,128)}, f32[512,640]{1,0:T(8,128)}, f32[512,384]{1,0:T(8,128)S(1)}) custom-call(bf16[512,768]{1,0:T(8,128)(2,1)S(1)} %pad_maximum_fusion.2.x_ref, bf16[768,768]{1,0:T(8,128)(2,1)S(1)} %bitcast_dynamic-update-slice_fusion.8.w_ref, f32[8,640]{1,0:T(8,128)S(1)} %fusion.24.conv_ref, ...), custom_call_target="tpu_custom_call" | custom-call | tf_op jit(solution)/shard_map/pallas_call | solution.py:398
  83.4 2.8 %shard_map.204 = (f32[512,384]{1,0:T(8,128)S(1)}, f32[512,384]{1,0:T(8,128)S(1)}, f32[4,8,128]{2,1,0:T(8,128)S(1)}) custom-call(bf16[512,768]{1,0:T(8,128)(2,1)S(1)} %get-tuple-element.29.normed_ref, bf16[768,384]{1,0:T(8,128)(2,1)S(1)} %constant_dynamic-update-slice_fusion.2.wg_ref, bf16[512,768]{1,0:T(8,128)(2,1)} %pad_maximum_fusion.3.og_ref, ...), custom_call_target="tpu_custom_call" | custom-call | tf_op jit(solution)/shard_map/pallas_call | solution.py:398
  90.6 2.5 %collective-permute-done.22 = f32[4,8,128]{2,1,0:T(8,128)S(1)} collective-permute-done((f32[4,8,128]{2,1,0:T(8,128)S(1)}, f32[4,8,128]{2,1,0:T(8,128)S(1)}, u32[]{:S(2)}, u32[]{:S(2)}) %collective-permute-start.22) | collective-permute-done | bytes 16416 | tf_op jit(solution)/shard_map/ppermute | solution.py:21
  94.2 3.8 %shard_map.205 = (bf16[512,768]{1,0:T(8,128)(2,1)S(1)}, bf16[384,768]{1,0:T(8,128)(2,1)S(1)}, bf16[768,384]{1,0:T(8,128)(2,1)S(1)}, bf16[512,384]{1,0:T(8,128)(2...) custom-call(f32[4,8,128]{2,1,0:T(8,128)S(1)} %add.233.stats_ref, bf16[512,768]{1,0:T(8,128)(2,1)} %copy-done.1, ...), custom_call_target="tpu_custom_call" | custom-call | tf_op jit(solution)/shard_map/pallas_call | solution.py:398
  102.3 20.8 %shard_map.206 = (bf16[768,768]{1,0:T(8,128)(2,1)}, bf16[512,768]{1,0:T(8,128)(2,1)S(1)}, f32[8,640]{1,0:T(8,128)S(1)}, f32[8,128]{1,0:T(8,128)S(1)}, f32[8,768]{1,0:T(8,128)S(1)}) custom-call(bf16[512,768]{1,0:T(8,128)(2,1)S(1)} %pad_maximum_fusion.2.x_ref, bf16[512,768]{1,0:T(8,128)(2,1)S(1)} %copy-done.2, bf16[768,768]{1,0:T(8,128)(2,1)} %copy-done, ...), custom_call_target="tpu_custom_call" | custom-call | tf_op jit(solution)/shard_map/pallas_call | solution.py:398
  130.9 4.3 %collective-permute-done.27 = bf16[128,768]{1,0:T(8,128)(2,1)S(1)} collective-permute-done((bf16[128,768]{1,0:T(8,128)(2,1)S(1)}, bf16[128,768]{1,0:T(8,128)(2,1)S(1)}, u32[]{:S(2)}, u32[]{:S(2)}) %collective-permute-start.27) | collective-permute-done | bytes 196640 | tf_op jit(solution)/shard_map/ppermute | solution.py:21
  140.6 3.0 %collective-permute-done.24 = bf16[128,768]{1,0:T(8,128)(2,1)S(1)} collective-permute-done((bf16[128,768]{1,0:T(8,128)(2,1)S(1)}, bf16[128,768]{1,0:T(8,128)(2,1)S(1)}, u32[]{:S(2)}, u32[]{:S(2)}) %collective-permute-start.24) | collective-permute-done | bytes 196640 | tf_op jit(solution)/shard_map/ppermute | solution.py:21
  143.6 3.1 %collective-permute-done.25 = bf16[128,768]{1,0:T(8,128)(2,1)S(1)} collective-permute-done((bf16[128,768]{1,0:T(8,128)(2,1)S(1)}, bf16[128,768]{1,0:T(8,128)(2,1)S(1)}, u32[]{:S(2)}, u32[]{:S(2)}) %collective-permute-start.25) | collective-permute-done | bytes 196640 | tf_op jit(solution)/shard_map/ppermute | solution.py:21
  149.2 3.1 %collective-permute-start.35 = (bf16[96,768]{1,0:T(8,128)(2,1)S(1)}, bf16[96,768]{1,0:T(8,128)(2,1)S(1)}, u32[]{:S(2)}, u32[]{:S(2)}) collective-permute-start(bf16[96,768]{1,0:T(8,128)(2,1)S(1)} %get-tuple-element.78), channel_id=1, source_target_pairs={{0,16},{4,20},{8,24},{12,28},{16,0},{20,4},{24,8},{28,12},{1,17},{... | collective-permute-start | bytes 442376 | tf_op jit(solution)/shard_map/ppermute | solution.py:21
  153.9 3.1 %collective-permute-start.31 = (bf16[96,768]{1,0:T(8,128)(2,1)S(1)}, bf16[96,768]{1,0:T(8,128)(2,1)S(1)}, u32[]{:S(2)}, u32[]{:S(2)}) collective-permute-start(bf16[96,768]{1,0:T(8,128)(2,1)S(1)} %get-tuple-element.75), channel_id=1, source_target_pairs={{0,16},{4,20},{8,24},{12,28},{16,0},{20,4},{24,8},{28,12},{1,17},{... | collective-permute-start | bytes 442376 | tf_op jit(solution)/shard_map/ppermute | solution.py:21
  160.6 2.8 %collective-permute-done.35 = bf16[96,768]{1,0:T(8,128)(2,1)S(1)} collective-permute-done((bf16[96,768]{1,0:T(8,128)(2,1)S(1)}, bf16[96,768]{1,0:T(8,128)(2,1)S(1)}, u32[]{:S(2)}, u32[]{:S(2)}) %collective-permute-start.35) | collective-permute-done | bytes 147488 | tf_op jit(solution)/shard_map/ppermute | solution.py:21
  164.8 11.3 %collective-permute-done.31 = bf16[96,768]{1,0:T(8,128)(2,1)S(1)} collective-permute-done((bf16[96,768]{1,0:T(8,128)(2,1)S(1)}, bf16[96,768]{1,0:T(8,128)(2,1)S(1)}, u32[]{:S(2)}, u32[]{:S(2)}) %collective-permute-start.31) | collective-permute-done | bytes 147488 | tf_op jit(solution)/shard_map/ppermute | solution.py:21
  178.9 3.4 %collective-permute-done.38 = f32[24,1152]{1,0:T(8,128)S(1)} collective-permute-done((f32[24,1152]{1,0:T(8,128)S(1)}, f32[24,1152]{1,0:T(8,128)S(1)}, u32[]{:S(2)}, u32[]{:S(2)}) %collective-permute-start.38) | collective-permute-done | bytes 110624 | tf_op jit(solution)/shard_map/ppermute | solution.py:21
  (288 shorter events, 70.5 us)
Async XLA Ops:
  2.7 68.4 %collective-permute-start = (bf16[2,128,768]{2,1,0:T(8,128)(2,1)S(1)}, bf16[2,128,768]{2,1,0:T(8,128)(2,1)}, u32[]{:S(2)}, u32[]{:S(2)}) collective-permute-start(bf16[2,128,768]{2,1,0:T(8,128)(2,1)S(1)} %constant_dynamic-update-slice_fusion), channel_id=1, source_target_pairs={{0,1},{1,0},{2,3},{3,2},{4,5},{5,4},{6,7},{7,6},{8,9},{9,8},{10,11... | collective-permute-start | bytes 1179656 | tf_op jit(solution)/shard_map/ppermute | solution.py:21
  3.3 67.8 %collective-permute-start.1 = (bf16[2,128,768]{2,1,0:T(8,128)(2,1)S(1)}, bf16[2,128,768]{2,1,0:T(8,128)(2,1)}, u32[]{:S(2)}, u32[]{:S(2)}) collective-permute-start(bf16[2,128,768]{2,1,0:T(8,128)(2,1)S(1)} %constant_dynamic-update-slice_fusion), channel_id=1, source_target_pairs={{0,2},{1,3},{2,0},{3,1},{4,6},{5,7},{6,4},{7,5},{8,10},{9,11},{10,... | collective-permute-start | bytes 1179656 | tf_op jit(solution)/shard_map/ppermute | solution.py:21
  9.8 7.8 %collective-permute-start.5 = (bf16[24,1152]{1,0:T(8,128)(2,1)S(1)}, bf16[24,1152]{1,0:T(8,128)(2,1)S(1)}, u32[]{:S(2)}, u32[]{:S(2)}) collective-permute-start(bf16[24,1152]{1,0:T(8,128)(2,1)S(1)} %get-tuple-element.96), channel_id=1, source_target_pairs={{0,3},{1,2},{2,1},{3,0},{4,7},{5,6},{6,5},{7,4},{8,11},{9,10},{10,... | collective-permute-start | bytes 165896 | tf_op jit(solution)/shard_map/ppermute | solution.py:21
  17.8 7.9 %collective-permute-start.6 = (bf16[96,768]{1,0:T(8,128)(2,1)S(1)}, bf16[96,768]{1,0:T(8,128)(2,1)S(1)}, u32[]{:S(2)}, u32[]{:S(2)}) collective-permute-start(bf16[96,768]{1,0:T(8,128)(2,1)S(1)} %slice.447), channel_id=1, source_target_pairs={{0,4},{4,0},{8,12},{12,8},{16,20},{20,16},{24,28},{28,24},{1,5},{5... | collective-permute-start | bytes 442376 | tf_op jit(solution)/shard_map/ppermute | solution.py:21
  19.9 9.3 %collective-permute-start.7 = (bf16[96,768]{1,0:T(8,128)(2,1)S(1)}, bf16[96,768]{1,0:T(8,128)(2,1)S(1)}, u32[]{:S(2)}, u32[]{:S(2)}) collective-permute-start(bf16[96,768]{1,0:T(8,128)(2,1)S(1)} %slice.447), channel_id=1, source_target_pairs={{0,8},{4,12},{8,0},{12,4},{16,24},{20,28},{24,16},{28,20},{1,9},{5... | collective-permute-start | bytes 442376 | tf_op jit(solution)/shard_map/ppermute | solution.py:21
  20.9 20.4 %collective-permute-start.9 = (bf16[96,768]{1,0:T(8,128)(2,1)S(1)}, bf16[96,768]{1,0:T(8,128)(2,1)S(1)}, u32[]{:S(2)}, u32[]{:S(2)}) collective-permute-start(bf16[96,768]{1,0:T(8,128)(2,1)S(1)} %slice.447), channel_id=1, source_target_pairs={{0,16},{4,20},{8,24},{12,28},{16,0},{20,4},{24,8},{28,12},{1,17},{... | collective-permute-start | bytes 442376 | tf_op jit(solution)/shard_map/ppermute | solution.py:21
  25.7 20.8 %collective-permute-start.11 = (bf16[96,768]{1,0:T(8,128)(2,1)S(1)}, bf16[96,768]{1,0:T(8,128)(2,1)S(1)}, u32[]{:S(2)}, u32[]{:S(2)}) collective-permute-start(bf16[96,768]{1,0:T(8,128)(2,1)S(1)} %slice.447), channel_id=1, source_target_pairs={{0,24},{4,28},{8,16},{12,20},{16,8},{20,12},{24,0},{28,4},{1,25},{... | collective-permute-start | bytes 442376 | tf_op jit(solution)/shard_map/ppermute | solution.py:21
  41.3 19.2 %collective-permute-start.17 = (bf16[96,768]{1,0:T(8,128)(2,1)}, bf16[96,768]{1,0:T(8,128)(2,1)S(1)}, u32[]{:S(2)}, u32[]{:S(2)}) collective-permute-start(bf16[96,768]{1,0:T(8,128)(2,1)} %get-tuple-element.50), channel_id=1, source_target_pairs={{0,16},{4,20},{8,24},{12,28},{16,0},{20,4},{24,8},{28,12},{1,17},{... | collective-permute-start | bytes 442376 | tf_op jit(solution)/shard_map/ppermute | solution.py:21
  46.5 14.1 %collective-permute-start.19 = (bf16[96,768]{1,0:T(8,128)(2,1)}, bf16[96,768]{1,0:T(8,128)(2,1)}, u32[]{:S(2)}, u32[]{:S(2)}) collective-permute-start(bf16[96,768]{1,0:T(8,128)(2,1)} %get-tuple-element.50), channel_id=1, source_target_pairs={{0,24},{4,28},{8,16},{12,20},{16,8},{20,12},{24,0},{28,4},{1,25},{... | collective-permute-start | bytes 442376 | tf_op jit(solution)/shard_map/ppermute | solution.py:21
  60.5 11.1 %collective-permute-start.2 = (bf16[2,128,768]{2,1,0:T(8,128)(2,1)S(1)}, bf16[2,128,768]{2,1,0:T(8,128)(2,1)S(1)}, u32[]{:S(2)}, u32[]{:S(2)}) collective-permute-start(bf16[2,128,768]{2,1,0:T(8,128)(2,1)S(1)} %constant_dynamic-update-slice_fusion), channel_id=1, source_target_pairs={{0,3},{1,2},{2,1},{3,0},{4,7},{5,6},{6,5},{7,4},{8,11},{9,10},{10,... | collective-permute-start | bytes 1179656 | tf_op jit(solution)/shard_map/ppermute | solution.py:21
  100.7 47.1 %collective-permute-start.33 = (bf16[4,96,768]{2,1,0:T(8,128)(2,1)}, bf16[4,96,768]{2,1,0:T(8,128)(2,1)}, u32[]{:S(2)}, u32[]{:S(2)}) collective-permute-start(bf16[4,96,768]{2,1,0:T(8,128)(2,1)} %fusion.3), channel_id=1, source_target_pairs={{0,4},{4,0},{8,12},{12,8},{16,20},{20,16},{24,28},{28,24},{1,5},{5... | collective-permute-start | bytes 1769480 | tf_op jit(solution)/shard_map/ppermute | solution.py:21
  127.3 7.8 %collective-permute-start.27 = (bf16[128,768]{1,0:T(8,128)(2,1)S(1)}, bf16[128,768]{1,0:T(8,128)(2,1)S(1)}, u32[]{:S(2)}, u32[]{:S(2)}) collective-permute-start(bf16[128,768]{1,0:T(8,128)(2,1)S(1)} %get-tuple-element.69), channel_id=1, source_target_pairs={{0,2},{1,3},{2,0},{3,1},{4,6},{5,7},{6,4},{7,5},{8,10},{9,11},{10,... | collective-permute-start | bytes 589832 | tf_op jit(solution)/shard_map/ppermute | solution.py:21
  128.6 9.7 %collective-permute-start.28 = (bf16[128,768]{1,0:T(8,128)(2,1)S(1)}, bf16[128,768]{1,0:T(8,128)(2,1)S(1)}, u32[]{:S(2)}, u32[]{:S(2)}) collective-permute-start(bf16[128,768]{1,0:T(8,128)(2,1)S(1)} %get-tuple-element.68), channel_id=1, source_target_pairs={{0,3},{1,2},{2,1},{3,0},{4,7},{5,6},{6,5},{7,4},{8,11},{9,10},{10,... | collective-permute-start | bytes 589832 | tf_op jit(solution)/shard_map/ppermute | solution.py:21
  129.4 24.2 %collective-permute-start.29 = (bf16[4,96,768]{2,1,0:T(8,128)(2,1)S(1)}, bf16[4,96,768]{2,1,0:T(8,128)(2,1)S(1)}, u32[]{:S(2)}, u32[]{:S(2)}) collective-permute-start(bf16[4,96,768]{2,1,0:T(8,128)(2,1)S(1)} %dynamic-slice_bitcast_fusion), channel_id=1, source_target_pairs={{0,4},{4,0},{8,12},{12,8},{16,20},{20,16},{24,28},{28,24},{1,5},{5... | collective-permute-start | bytes 1769480 | tf_op jit(solution)/shard_map/ppermute | solution.py:21
  130.5 10.1 %collective-permute-start.23 = (bf16[128,768]{1,0:T(8,128)(2,1)S(1)}, bf16[128,768]{1,0:T(8,128)(2,1)S(1)}, u32[]{:S(2)}, u32[]{:S(2)}) collective-permute-start(bf16[128,768]{1,0:T(8,128)(2,1)S(1)} %get-tuple-element.70), channel_id=1, source_target_pairs={{0,1},{1,0},{2,3},{3,2},{4,5},{5,4},{6,7},{7,6},{8,9},{9,8},{10,11... | collective-permute-start | bytes 589832 | tf_op jit(solution)/shard_map/ppermute | solution.py:21
  135.2 8.4 %collective-permute-start.24 = (bf16[128,768]{1,0:T(8,128)(2,1)S(1)}, bf16[128,768]{1,0:T(8,128)(2,1)S(1)}, u32[]{:S(2)}, u32[]{:S(2)}) collective-permute-start(bf16[128,768]{1,0:T(8,128)(2,1)S(1)} %get-tuple-element.72), channel_id=1, source_target_pairs={{0,2},{1,3},{2,0},{3,1},{4,6},{5,7},{6,4},{7,5},{8,10},{9,11},{10,... | collective-permute-start | bytes 589832 | tf_op jit(solution)/shard_map/ppermute | solution.py:21
  138.3 8.4 %collective-permute-start.25 = (bf16[128,768]{1,0:T(8,128)(2,1)S(1)}, bf16[128,768]{1,0:T(8,128)(2,1)S(1)}, u32[]{:S(2)}, u32[]{:S(2)}) collective-permute-start(bf16[128,768]{1,0:T(8,128)(2,1)S(1)} %get-tuple-element.71), channel_id=1, source_target_pairs={{0,3},{1,2},{2,1},{3,0},{4,7},{5,6},{6,5},{7,4},{8,11},{9,10},{10,... | collective-permute-start | bytes 589832 | tf_op jit(solution)/shard_map/ppermute | solution.py:21
  149.1 9.4 %collective-permute-start.34 = (bf16[96,768]{1,0:T(8,128)(2,1)S(1)}, bf16[96,768]{1,0:T(8,128)(2,1)S(1)}, u32[]{:S(2)}, u32[]{:S(2)}) collective-permute-start(bf16[96,768]{1,0:T(8,128)(2,1)S(1)} %get-tuple-element.76), channel_id=1, source_target_pairs={{0,8},{4,12},{8,0},{12,4},{16,24},{20,28},{24,16},{28,20},{1,9},{5... | collective-permute-start | bytes 442376 | tf_op jit(solution)/shard_map/ppermute | solution.py:21
  149.2 14.3 %collective-permute-start.35 = (bf16[96,768]{1,0:T(8,128)(2,1)S(1)}, bf16[96,768]{1,0:T(8,128)(2,1)S(1)}, u32[]{:S(2)}, u32[]{:S(2)}) collective-permute-start(bf16[96,768]{1,0:T(8,128)(2,1)S(1)} %get-tuple-element.78), channel_id=1, source_target_pairs={{0,16},{4,20},{8,24},{12,28},{16,0},{20,4},{24,8},{28,12},{1,17},{... | collective-permute-start | bytes 442376 | tf_op jit(solution)/shard_map/ppermute | solution.py:21
  152.3 11.1 %collective-permute-start.36 = (bf16[96,768]{1,0:T(8,128)(2,1)S(1)}, bf16[96,768]{1,0:T(8,128)(2,1)S(1)}, u32[]{:S(2)}, u32[]{:S(2)}) collective-permute-start(bf16[96,768]{1,0:T(8,128)(2,1)S(1)} %get-tuple-element.77), channel_id=1, source_target_pairs={{0,24},{4,28},{8,16},{12,20},{16,8},{20,12},{24,0},{28,4},{1,25},{... | collective-permute-start | bytes 442376 | tf_op jit(solution)/shard_map/ppermute | solution.py:21
  153.8 11.0 %collective-permute-start.30 = (bf16[96,768]{1,0:T(8,128)(2,1)S(1)}, bf16[96,768]{1,0:T(8,128)(2,1)S(1)}, u32[]{:S(2)}, u32[]{:S(2)}) collective-permute-start(bf16[96,768]{1,0:T(8,128)(2,1)S(1)} %get-tuple-element.73), channel_id=1, source_target_pairs={{0,8},{4,12},{8,0},{12,4},{16,24},{20,28},{24,16},{28,20},{1,9},{5... | collective-permute-start | bytes 442376 | tf_op jit(solution)/shard_map/ppermute | solution.py:21
  153.9 22.2 %collective-permute-start.31 = (bf16[96,768]{1,0:T(8,128)(2,1)S(1)}, bf16[96,768]{1,0:T(8,128)(2,1)S(1)}, u32[]{:S(2)}, u32[]{:S(2)}) collective-permute-start(bf16[96,768]{1,0:T(8,128)(2,1)S(1)} %get-tuple-element.75), channel_id=1, source_target_pairs={{0,16},{4,20},{8,24},{12,28},{16,0},{20,4},{24,8},{28,12},{1,17},{... | collective-permute-start | bytes 442376 | tf_op jit(solution)/shard_map/ppermute | solution.py:21
  158.5 17.6 %collective-permute-start.32 = (bf16[96,768]{1,0:T(8,128)(2,1)S(1)}, bf16[96,768]{1,0:T(8,128)(2,1)S(1)}, u32[]{:S(2)}, u32[]{:S(2)}) collective-permute-start(bf16[96,768]{1,0:T(8,128)(2,1)S(1)} %get-tuple-element.74), channel_id=1, source_target_pairs={{0,24},{4,28},{8,16},{12,20},{16,8},{20,12},{24,0},{28,4},{1,25},{... | collective-permute-start | bytes 442376 | tf_op jit(solution)/shard_map/ppermute | solution.py:21
  178.2 9.1 %collective-permute-start.40 = (f32[48,768]{1,0:T(8,128)S(1)}, f32[48,768]{1,0:T(8,128)S(1)}, u32[]{:S(2)}, u32[]{:S(2)}) collective-permute-start(f32[48,768]{1,0:T(8,128)S(1)} %pad_maximum_fusion.13), channel_id=1, source_target_pairs={{0,0},{4,1},{8,2},{12,3},{16,4},{20,5},{24,6},{28,7},{1,8},{5,9},{... | collective-permute-start | bytes 442376 | tf_op jit(solution)/shard_map/ppermute | solution.py:561
  (47 other events, 297.1 us)

commit v2 on v1

--- a/solution.py
+++ b/solution.py
@@ -9,9 +9,11 @@
 STATE = 128
 CONV = 4
 CHUNK = 128
+VMEM_LIMIT = 56 * 2**20
 LANES = 128
 EPSILON = 1e-05
 FULL = lax.Precision.HIGHEST
+MOST = lax.Precision.HIGH
 F32 = jnp.float32
 BF16 = jnp.bfloat16
 
@@ -53,29 +55,40 @@
     return inner
 
 
-def gather_dp(x):
+def far_offsets():
     count = lax.axis_size("dp")
     inner = inner_of(count)
-    far = [x] + [swap(x, "dp", k * inner) for k in range(1, count // inner)]
+    return [k * inner for k in range(1, count // inner)]
+
+
+def gather_far(x):
+    return [x] + [swap(x, "dp", k) for k in far_offsets()]
+
+
+def gather_near(far):
+    inner = inner_of(lax.axis_size("dp"))
     near = [[piece] + [swap(piece, "dp", j) for j in range(1, inner)] for piece in far]
-    return [near[m // inner][m % inner] for m in range(count)]
-
-
-def reduce_dp(grads):
+    return [piece for group in near for piece in group]
+
+
+def reduce_near(grads):
     count = lax.axis_size("dp")
     inner = inner_of(count)
-    place = lax.axis_index("dp")
-    outer_place, inner_place = place // inner, place % inner
+    inner_place = lax.axis_index("dp") % inner
     shaped = grads.reshape(count // inner, inner, *grads.shape[1:])
     parts = []
     for j in range(inner):
         slab = lax.dynamic_index_in_dim(shaped, inner_place ^ j, 1, False)
         parts.append(swap(slab, "dp", j) if j else slab)
-    near = tree_sum([p.astype(F32) for p in parts]).astype(BF16)
-    parts = []
-    for k in range(count // inner):
-        slab = lax.dynamic_index_in_dim(near, outer_place ^ k, 0, False)
-        parts.append(swap(slab, "dp", k * inner) if k else slab)
+    return tree_sum([p.astype(F32) for p in parts]).astype(BF16)
+
+
+def reduce_far(near):
+    outer_place = lax.axis_index("dp") // inner_of(lax.axis_size("dp"))
+    parts = [lax.dynamic_index_in_dim(near, outer_place, 0, False)]
+    for k, offset in enumerate(far_offsets()):
+        slab = lax.dynamic_index_in_dim(near, outer_place ^ (k + 1), 0, False)
+        parts.append(swap(slab, "dp", offset))
     return tree_sum([p.astype(F32) for p in parts])
 
 
@@ -85,16 +98,20 @@
     )
 
 
+def exact(a, b):
+    return dot(a, b, 1, 0, FULL)
+
+
 def mm(a, b):
-    return dot(a, b, 1, 0, FULL)
+    return dot(a, b, 1, 0, MOST)
 
 
 def mm_nt(a, b):
-    return dot(a, b, 1, 1, FULL)
+    return dot(a, b, 1, 1, MOST)
 
 
 def mm_tn(a, b):
-    return dot(a, b, 0, 0, FULL)
+    return dot(a, b, 0, 0, MOST)
 
 
 def softplus(x):
@@ -117,10 +134,43 @@
     return row >= column if lower else row <= column
 
 
-def masks_of(segment_col, segment_rows, i):
-    far = (segment_col == segment_rows[i]).astype(F32)
-    near = (segment_col == segment_rows[i + 1]).astype(F32)
-    own = (segment_col == segment_rows[i + 2]) & triangle(True)
+def head_rows(bias_ref, decay_ref, skip_ref, heads_here):
+    rows = jnp.concatenate([bias_ref[...], decay_ref[...], skip_ref[...]], 0)
+    count = rows.shape[1]
+    rows = jnp.concatenate([rows, jnp.zeros((3, LANES - count), F32)], 1)
+    rows = jnp.concatenate([rows, jnp.zeros((5, LANES), F32)], 0)
+    place = lax.axis_index("seq")
+    mine = rows
+    for j in range(1, count // heads_here):
+        moved = jnp.concatenate([rows[:, j * heads_here :], rows[:, : j * heads_here]], 1)
+        mine = jnp.where(place == j, moved, mine)
+    return mine
+
+
+def spread_segments(seg_ref, seg_col, seg_row):
+    seg_row[:, : 2 * CHUNK] = jnp.full((8, 2 * CHUNK), -1.0, F32)
+    for i in range(seg_ref.shape[1] // CHUNK):
+        now = seg_ref[:, i * CHUNK : (i + 1) * CHUNK].astype(F32)
+        seg_row[:, (i + 2) * CHUNK : (i + 3) * CHUNK] = jnp.broadcast_to(now, (8, CHUNK))
+        seg_col[i * CHUNK : (i + 1) * CHUNK, :] = jnp.broadcast_to(now, (CHUNK, CHUNK)).T
+
+
+def same_segment(seg_col, back, width):
+    now = seg_col[...]
+    row = lax.broadcasted_iota(jnp.int32, now.shape, 0)
+    same = ((now == pltpu.roll(now, back, 0)) & (row >= back)).astype(F32)
+    return jnp.concatenate([same] * (width // LANES), 1)
+
+
+def masks_of(seg_col, seg_row, i):
+    column = seg_col[pl.ds(pl.multiple_of(i * CHUNK, CHUNK), CHUNK), :]
+
+    def row(j):
+        return seg_row[:, pl.ds(pl.multiple_of((i + j) * CHUNK, CHUNK), CHUNK)][:1]
+
+    far = (column == row(0)).astype(F32)
+    near = (column == row(1)).astype(F32)
+    own = (column == row(2)) & triangle(True)
     return far, near, own
 
 
@@ -146,9 +196,9 @@
 
 
 def fill_sources(i, v, step, decay, expand, vd, vt, ecx):
-    cumulative = mm(triangle(True).astype(F32), decay)
-    step_x = mm(step, expand)
-    cum_x = mm(cumulative, expand)
+    cumulative = exact(triangle(True).astype(F32), decay)
+    step_x = exact(step, expand)
+    cum_x = exact(cumulative, expand)
     last = cum_x[CHUNK - 1 :]
     vd_now = v * step_x
     vd[pl.ds(i * CHUNK, CHUNK), :] = vd_now
@@ -162,20 +212,96 @@
     return jnp.exp(jnp.where(own, gap, -1e30))
 
 
-def forward_kernel(width, lane_of_gain):
+def put_in_order(pieces, place, target, source=None, lanes=None):
+    for m, piece in enumerate(pieces):
+        source_rows = slice(0, piece.shape[0]) if source is None else source
+        rows = source_rows.stop - source_rows.start
+        start = pl.multiple_of((place ^ m) * rows, rows)
+        if lanes is None:
+            target[pl.ds(start, rows), :] = piece[...]
+        else:
+            target[pl.ds(start, rows), lanes[0]] = piece[source_rows, lanes[1]]
+
+
+def dp_index(pieces):
+    return lax.axis_index("dp") if len(pieces) > 1 else 0
+
+
+def put_second(pieces, place, wg_ref=None, wo_ref=None):
+    rows, both = pieces[0].shape
+    width = both // 2
+    if wg_ref is not None:
+        put_in_order(pieces, place, wg_ref, slice(0, rows), (slice(0, width), slice(0, width)))
+    if wo_ref is not None:
+        folds = wo_ref.shape[1] // width
+        part = rows // folds
+        for k in range(folds):
+            to = (slice(k * width, (k + 1) * width), slice(width, 2 * width))
+            put_in_order(pieces, place, wo_ref, slice(k * part, (k + 1) * part), to)
+
+
+def small_spots(rows, lengths):
+    group = min(rows, len(lengths))
+    return [(i % group, (i // group) * max(lengths)) for i in range(len(lengths))]
+
+
+def pack_kernel(width, inner, heads_here, count):
+    def body(w_ref, taps_ref, shift_ref, gate_ref, norm_ref, *refs):
+        outs, blocks = refs[:-1], refs[-1]
+        rows = w_ref.shape[0]
+        stride = blocks.shape[0] // count
+        states = 2 * inner + 2 * STATE
+        norm = jnp.concatenate([norm_ref[...].astype(F32), jnp.zeros((1, LANES - rows), F32)], 1)
+        column = jnp.broadcast_to(norm, (LANES, LANES)).T[:rows]
+        taps = taps_ref[...].astype(F32)
+        vectors = [taps[i : i + 1] for i in range(CONV)]
+        vectors += [shift_ref[...].astype(F32), gate_ref[...].astype(F32)]
+        spots = small_spots(rows, [v.shape[1] for v in vectors])
+        lane = lax.broadcasted_iota(jnp.int32, (rows, LANES), 1)
+        row = lax.broadcasted_iota(jnp.int32, (rows, LANES), 0)
+        shared = jnp.where(lane == heads_here, column, 0.0)
+        for vector, (at_row, at_lane) in zip(vectors, spots):
+            start = heads_here + 1 + at_lane
+            pieces = [jnp.zeros((1, start), F32), vector]
+            pieces.append(jnp.zeros((1, LANES - start - vector.shape[1]), F32))
+            shared = shared + jnp.where(row == at_row, jnp.concatenate(pieces, 1), 0.0)
+        for j in range(count):
+            at = slice(j * stride, j * stride + rows)
+            first = states + j * heads_here
+            blocks[at, :width] = w_ref[:, inner + j * width : inner + (j + 1) * width].astype(F32)
+            blocks[at, width : width + 2 * STATE] = w_ref[:, 2 * inner : states].astype(F32)
+            steps = w_ref[:, first : first + heads_here].astype(F32)
+            tail = jnp.concatenate([steps, shared[:, heads_here:]], 1)
+            blocks[at, width + 2 * STATE : width + 2 * STATE + LANES] = tail
+            gate = w_ref[:, j * width : (j + 1) * width].astype(F32)
+            blocks[at, width + 2 * STATE + LANES :] = gate
+        for k in range(count):
+            start = pl.multiple_of((lax.axis_index("seq") ^ k) * stride, stride)
+            outs[k][...] = blocks[pl.ds(start, rows), :].astype(BF16)
+
+    return body
+
+
+def forward_kernel(width, lane_of_gain, x_count, w_count):
     heads_here = width // HEAD_DIM
 
-    def body(x_ref, w_ref, conv_ref, same_ref, seg_ref, segr_ref, head_ref, normed_ref, proj_ref, pre_ref, y_ref, bpad, vd, vt, ecx):
+    def body(*refs):
+        x_pieces, refs = refs[:x_count], refs[x_count:]
+        w_pieces, refs = refs[:w_count], refs[w_count:]
+        conv_ref, seg_ref, bias_ref, decay_ref, skip_ref, normed_ref, proj_ref, pre_ref, y_ref, bpad, vd, vt, ecx, seg_col, seg_row, x_ref, w_ref = refs
+        put_in_order(x_pieces, lax.axis_index("seq"), x_ref)
+        put_in_order(w_pieces, dp_index(w_pieces), w_ref)
         x = x_ref[...].astype(F32)
         gain = gain_row(w_ref[...], lane_of_gain)
         normed_ref[...] = (x * rms_inverse(x) * gain).astype(BF16)
         proj_ref[...] = dot(normed_ref[...], w_ref[...], 1, 0)
+        spread_segments(seg_ref, seg_col, seg_row)
         channels = width + 2 * STATE
         u = proj_ref[:, :channels]
         running = conv_ref[CONV : CONV + 1, :] + conv_ref[CONV - 1 : CONV, :] * u
         for back in range(1, CONV):
             tap = conv_ref[CONV - 1 - back : CONV - back, :]
-            running = running + tap * pltpu.roll(u, back, 0) * same_ref[:, back : back + 1]
+            running = running + tap * pltpu.roll(u, back, 0) * same_segment(seg_col, back, channels)
         pre_ref[...] = running
         bpad[pl.ds(0, 2 * CHUNK), :] = jnp.zeros((2 * CHUNK, STATE), F32)
         vt[pl.ds(0, 2 * CHUNK), :] = jnp.zeros((2 * CHUNK, width), F32)
@@ -184,8 +310,8 @@
         bpad[pl.ds(2 * CHUNK, x.shape[0]), :] = b_pre * jax.nn.sigmoid(b_pre)
         expand = expand_matrix(width)
         low, high = lane_halves()
-        heads = head_ref[...]
-        skip_x = mm(jnp.broadcast_to(heads[2:3], (8, LANES)), expand)[:1]
+        heads = head_rows(bias_ref, decay_ref, skip_ref, heads_here)
+        skip_x = exact(jnp.broadcast_to(heads[2:3], (8, LANES)), expand)[:1]
 
         def chunk(i, carry):
             rows = pl.ds(pl.multiple_of(i * CHUNK, CHUNK), CHUNK)
@@ -196,7 +322,7 @@
             step, decay = decays(proj_ref[rows, channels:], heads)
             cumulative, _, _, _ = fill_sources(i, v, step, decay, expand, vd, vt, ecx)
             cumulative_t = cumulative.T
-            far, near, own = masks_of(seg_ref[rows, :], segr_ref, i)
+            far, near, own = masks_of(seg_col, seg_row, i)
             window = pl.ds(pl.multiple_of(i * CHUNK, CHUNK), 3 * CHUNK)
             scores = mm_nt(c, bpad[window, :])
             s_far = scores[:, :CHUNK] * far
@@ -222,8 +348,13 @@
     return body
 
 
-def gate_kernel(width):
-    def body(normed_ref, wg_ref, og_ref, wo_ref, y_ref, gain_ref, gate_ref, dg_ref, stats_ref):
+def gate_kernel(og_count, w_count):
+    def body(*refs):
+        og_pieces, refs = refs[:og_count], refs[og_count:]
+        w_pieces, refs = refs[:w_count], refs[w_count:]
+        normed_ref, y_ref, gain_ref, gate_ref, dg_ref, stats_ref, og_ref, wg_ref, wo_ref = refs
+        put_in_order(og_pieces, lax.axis_index("seq"), og_ref)
+        put_second(w_pieces, dp_index(w_pieces), wg_ref, wo_ref)
         gate = dot(normed_ref[...], wg_ref[...], 1, 0)
         gate_ref[...] = gate
         d_gated = dot(og_ref[...], wo_ref[...], 1, 1)
@@ -240,11 +371,18 @@
     return body
 
 
-def out_kernel(width, whole_width):
-    def body(stats_ref, normed_ref, gate_ref, dg_ref, y_ref, gain_ref, og_ref, wo_ref, out_ref, gout_ref, ggate_ref, dgate_ref, dy_ref, ggain_ref):
+def out_kernel(width, whole_width, og_count, w_count):
+    def body(*refs):
+        og_pieces, refs = refs[:og_count], refs[og_count:]
+        w_pieces, refs = refs[:w_count], refs[w_count:]
+        stats, refs = refs[:og_count], refs[og_count:]
+        normed_ref, gate_ref, dg_ref, y_ref, gain_ref, out_ref, gout_ref, ggate_ref, dgate_ref, dy_ref, ggain_ref, og_ref, wo_ref = refs
+        put_in_order(og_pieces, lax.axis_index("seq"), og_ref)
+        put_second(w_pieces, dp_index(w_pieces), None, wo_ref)
         columns = []
-        for i in range(stats_ref.shape[0]):
-            square = jnp.concatenate([stats_ref[i], jnp.zeros((CHUNK - 8, LANES), F32)], 0)
+        for i in range(stats[0].shape[0]):
+            total = tree_sum([part[i] for part in stats])
+            square = jnp.concatenate([total, jnp.zeros((CHUNK - 8, LANES), F32)], 0)
             columns.append(square.T)
         columns = jnp.concatenate(columns, 0)
         inverse = lax.rsqrt(columns[:, 0:1] / whole_width + EPSILON)
@@ -270,18 +408,19 @@
     return body
 
 
-def backward_kernel(width, lane_of_gain):
+def mixer_back_kernel(width):
     heads_here = width // HEAD_DIM
 
-    def body(x_ref, normed_ref, w_ref, wg_ref, conv_ref, same_ref, seg_ref, segr_ref, head_ref, proj_ref, pre_ref, y_ref, dy_ref, dgate_ref, gin_ref, dn_ref, conv_grad_ref, head_grad_ref, norm_grad_ref, bpad, vd, vt, ecx, tailx, stepx, cums, ua, db, dpre, draw):
-        length = x_ref.shape[0]
+    def body(conv_ref, seg_ref, bias_ref, decay_ref, skip_ref, proj_ref, pre_ref, y_ref, dy_ref, dconv_ref, draw, conv_grad_ref, head_grad_ref, bpad, vd, vt, ecx, seg_col, seg_row, tailx, stepx, cums, ua, db, dpre):
+        length = proj_ref.shape[0]
+        spread_segments(seg_ref, seg_col, seg_row)
         chunks = length // CHUNK
         channels = width + 2 * STATE
         expand = expand_matrix(width)
         low, high = lane_halves()
-        heads = head_ref[...]
+        heads = head_rows(bias_ref, decay_ref, skip_ref, heads_here)
         rate = jnp.exp(heads[1:2])
-        skip_x = mm(jnp.broadcast_to(heads[2:3], (8, LANES)), expand)[:1]
+        skip_x = exact(jnp.broadcast_to(heads[2:3], (8, LANES)), expand)[:1]
         bpad[pl.ds(0, 2 * CHUNK), :] = jnp.zeros((2 * CHUNK, STATE), F32)
         vt[pl.ds(0, 2 * CHUNK), :] = jnp.zeros((2 * CHUNK, width), F32)
         tailx[pl.ds(0, 2 * CHUNK), :] = jnp.zeros((2 * CHUNK, width), F32)
@@ -321,7 +460,7 @@
             step, decay = decays(raw, heads)
             cumulative = cums[rows, :]
             cumulative_t = cumulative.T
-            far, near, own = masks_of(seg_ref[rows, :], segr_ref, i)
+            far, near, own = masks_of(seg_col, seg_row, i)
             b_window = bpad[window, :]
             scores = mm_nt(c, b_window)
             s_far = scores[:, :CHUNK] * far
@@ -352,10 +491,10 @@
             received = dot(dy * (y_ref[rows, :] - skip_x * v), expand, 1, 1, FULL)
             d_step = dot(v * u_total, expand, 1, 1, FULL)
             gap = received - step * d_step
-            d_decay = mm(triangle(False).astype(F32), gap) + later
+            d_decay = exact(triangle(False).astype(F32), gap) + later
             d_step = d_step - d_decay * rate
             d_raw = d_step * jax.nn.sigmoid(raw + heads[0:1])
-            draw[rows, :] = d_raw
+            draw[rows, :] = d_raw.astype(BF16)
             dv = stepx[rows, :] * u_total + skip_x * dy
             dpre[rows, :width] = dv * (v_sig * (1.0 + v_pre * (1.0 - v_sig)))
             b_pre = pre_ref[rows, width : width + STATE]
@@ -375,20 +514,36 @@
         du = conv_ref[CONV - 1 : CONV, :] * d
         taps = [jnp.sum(d * u, axis=0, keepdims=True)]
         for back in range(1, CONV):
-            masked = d * same_ref[:, back : back + 1]
+            masked = d * same_segment(seg_col, back, channels)
             taps.insert(0, jnp.sum(masked * pltpu.roll(u, back, 0), axis=0, keepdims=True))
             du = du + conv_ref[CONV - 1 - back : CONV - back, :] * pltpu.roll(masked, length - back, 0)
         taps.append(jnp.sum(d, axis=0, keepdims=True))
         taps.append(jnp.zeros((8 - CONV - 1, channels), F32))
         conv_grad_ref[...] = jnp.concatenate(taps, 0)
-        d_proj = jnp.concatenate([du, draw[...]], 1).astype(BF16)
-        gin_ref[...] = dot(normed_ref[...], d_proj, 0, 0).astype(BF16)
-        dn = dot(d_proj, w_ref[...], 1, 1) + dot(dgate_ref[...], wg_ref[...], 1, 1)
+        dconv_ref[...] = du.astype(BF16)
+
+    return body
+
+
+def weight_back_kernel(x_count, w_count):
+    def body(*refs):
+        x_pieces, refs = refs[:x_count], refs[x_count:]
+        w_pieces, refs = refs[:w_count], refs[w_count:]
+        g_pieces, refs = refs[:w_count], refs[w_count:]
+        normed_ref, dconv_ref, draw_ref, dgate_ref, gin_ref, dn_ref, norm_grad_ref, x_ref, w_ref, wg_ref = refs
+        put_in_order(x_pieces, lax.axis_index("seq"), x_ref)
+        put_in_order(w_pieces, dp_index(w_pieces), w_ref)
+        put_second(g_pieces, dp_index(w_pieces), wg_ref)
+        channels = dconv_ref.shape[1]
+        dconv, draw = dconv_ref[...], draw_ref[...]
+        dn = dot(dconv, w_ref[:, :channels], 1, 1) + dot(draw, w_ref[:, channels:], 1, 1)
+        dn = dn + dot(dgate_ref[...], wg_ref[...], 1, 1)
         dn_ref[...] = dn.astype(BF16)
+        gin_ref[:, :channels] = dot(normed_ref[...], dconv, 0, 0).astype(BF16)
         x = x_ref[...].astype(F32)
-        norm_grad_ref[...] = jnp.broadcast_to(
-            jnp.sum(dn * (x * rms_inverse(x)), axis=0, keepdims=True), (8, x.shape[1])
-        )
+        along = jnp.sum(dn * (x * rms_inverse(x)), axis=0, keepdims=True)
+        norm_grad_ref[...] = along
+        gin_ref[:, channels:] = dot(normed_ref[...], draw, 0, 0).astype(BF16)
 
     return body
 
@@ -400,8 +555,11 @@
         out_shape=[jax.ShapeDtypeStruct(shape, kind) for shape, kind in outs],
         in_specs=[vmem] * len(operands),
         out_specs=[vmem] * len(outs),
-        scratch_shapes=[pltpu.VMEM(shape, F32) for shape in scratch],
-        compiler_params=pltpu.CompilerParams(vmem_limit_bytes=50 * 2**20),
+        scratch_shapes=[
+            pltpu.VMEM(*shape) if isinstance(shape[0], tuple) else pltpu.VMEM(shape, F32)
+            for shape in scratch
+        ],
+        compiler_params=pltpu.CompilerParams(vmem_limit_bytes=VMEM_LIMIT),
     )(*operands)
 
 
@@ -441,32 +599,19 @@
     conv_here = conv_bias.shape[0]
     gate_here = gate_gain.shape[0]
 
-    conv_flat = jnp.concatenate([conv_weight.reshape(1, -1), conv_bias.reshape(1, -1)], 1)
-    conv_slots = slots(conv_flat, rows)
-    gate_slots = slots(gate_gain.reshape(1, -1), rows)
-    conv_lanes, gate_lanes = conv_slots.shape[1], gate_slots.shape[1]
-    rest = LANES - heads_here - 1 - conv_lanes - gate_lanes
-    shared = [norm_gain[:, None], conv_slots, gate_slots, jnp.zeros((rows, rest), BF16)]
-    both_states = in_weight[:, 2 * inner : 2 * inner + 2 * STATE]
-    to_send = []
-    for j in range(seq_n):
-        first = 2 * inner + 2 * STATE + j * heads_here
-        to_send.append(
-            jnp.concatenate(
-                [in_weight[:, inner + j * width : inner + (j + 1) * width], both_states]
-                + [in_weight[:, first : first + heads_here]]
-                + shared
-                + [in_weight[:, j * width : (j + 1) * width]],
-                axis=1,
-            )
-        )
-    mine = jnp.concatenate(in_order(scatter_xor(jnp.stack(to_send), "seq"), place), 0)
+    stride = -(-rows // 16) * 16
+    blocks = call(
+        pack_kernel(width, inner, heads_here, seq_n),
+        [((rows, cols + width), BF16)] * seq_n,
+        [(seq_n * stride, cols + width)],
+        in_weight, conv_weight, conv_bias[None], gate_gain[None], norm_gain[None],
+    )
+    blocks = [b if k == 0 else swap(b, "seq", k) for k, b in enumerate(blocks)]
+    mine = jnp.concatenate(in_order(blocks, place), 0)
     first_part, gate_part = mine[:, :cols], mine[:, cols:]
-    w_first = jnp.concatenate(in_order(gather_dp(first_part), dp_place), 0)
-
-    acts = in_order(gather_xor(jnp.stack([hidden_in[0], out_grad[0]]), "seq"), place)
-    x_row = jnp.concatenate([a[0] for a in acts], 0)
-    og_row = jnp.concatenate([a[1] for a in acts], 0)
+    far_first = gather_far(first_part)
+    x_pieces = gather_xor(hidden_in[0], "seq")
+    og_pieces = gather_xor(out_grad[0], "seq")
 
     def linear(d, s):
         return d * seq_n + s
@@ -478,23 +623,34 @@
         [out_block[:, k * width : (k + 1) * width] for k in range(model // width)], 0
     )
     second = jnp.concatenate([gate_part, folded], 1)
-    w_second = in_order(gather_dp(second), dp_place)
-    w_gate = jnp.concatenate([p[:, :width] for p in w_second], 0)
-    w_out = jnp.concatenate(
-        [
-            jnp.concatenate(
-                [p[k * out_rows : (k + 1) * out_rows, width:] for k in range(model // width)], 1
-            )
-            for p in w_second
-        ],
-        0,
-    )
-
-    tail = w_first[:, channels:]
-    at = heads_here + 1
-    conv_all = tail[:, at : at + conv_lanes].reshape(owners, rows * conv_lanes)
-    conv_all = conv_all[:, : (CONV + 1) * conv_here].reshape(owners, CONV + 1, conv_here)
-    conv_all = conv_all.transpose(1, 0, 2).reshape(CONV + 1, owners * conv_here)
+    far_second = gather_far(second)
+    w_first = gather_near(far_first)
+    w_second = gather_near(far_second)
+    split_here = not out_rows % 16
+    if not split_here:
+        w_first = [jnp.concatenate(in_order(w_first, dp_place), 0)]
+        w_second = in_order(w_second, dp_place)
+        folds = [slice(k * out_rows, (k + 1) * out_rows) for k in range(model // width)]
+        w_out = jnp.concatenate([p[f, width:] for f in folds for p in w_second], 0)
+        w_second = [
+            jnp.concatenate([jnp.concatenate([p[:, :width] for p in w_second], 0), w_out], 1)
+        ]
+    if len(w_first) > 1:
+        tail = jnp.concatenate(in_order([p[:, channels:] for p in w_first], dp_place), 0)
+    else:
+        tail = w_first[0][:, channels:]
+    tail = tail.reshape(owners, rows, LANES)
+    lengths = [conv_here] * (CONV + 1) + [gate_here]
+    spots = small_spots(rows, lengths)
+    if rows >= len(lengths):
+        conv_all = tail[:, : CONV + 1, heads_here + 1 : heads_here + 1 + conv_here]
+        conv_all = conv_all.transpose(1, 0, 2).reshape(CONV + 1, owners * conv_here)
+    else:
+        conv_all = []
+        for r, lane in spots[: CONV + 1]:
+            first = heads_here + 1 + lane
+            conv_all.append(tail[:, r, first : first + conv_here].reshape(1, -1))
+        conv_all = jnp.concatenate(conv_all, 0)
     conv_mine = jnp.concatenate(
         [
             lax.dynamic_slice_in_dim(conv_all[:, :inner], place * width, width, 1),
@@ -503,78 +659,70 @@
         1,
     )
     conv_mine = jnp.pad(conv_mine.astype(F32), ((0, 8 - CONV - 1), (0, 0)))
-    at = at + conv_lanes
-    gain_all = tail[:, at : at + gate_lanes].reshape(owners, rows * gate_lanes)[:, :gate_here]
+    first = heads_here + 1 + spots[-1][1]
+    gain_all = tail[:, spots[-1][0], first : first + gate_here]
     gain_mine = lax.dynamic_slice_in_dim(gain_all.reshape(1, inner), place * width, width, 1)
     gain_mine = gain_mine.astype(F32)
 
-    head_params = jnp.stack([step_bias, decay_log, skip_weight])
-    head_params = lax.dynamic_slice_in_dim(head_params, place * heads_here, heads_here, 1)
-    head_params = jnp.pad(head_params, ((0, 5), (0, LANES - heads_here)))
-    row_segments = segments[0]
-    same = [jnp.ones((length,), F32)]
-    for back in range(1, CONV):
-        matches = (row_segments[back:] == row_segments[:-back]).astype(F32)
-        same.append(jnp.concatenate([jnp.zeros((back,), F32), matches]))
-    same = jnp.pad(jnp.stack(same, 1), ((0, 0), (0, 8 - CONV)))
-    segment_col = row_segments[:, None]
-    padded = jnp.concatenate([jnp.full((2 * CHUNK,), -1, jnp.int32), row_segments])
-    segment_rows = padded.reshape(-1, 1, CHUNK)
+    head_params = (step_bias[None], decay_log[None], skip_weight[None])
 
     chunks = length // CHUNK
     tall = length + 2 * CHUNK
     sources = [(tall, STATE), (length, width), (tall, width), (length + 8, width)]
+    sources += [(length, LANES), (8, tall)]
     normed, proj, pre, y = call(
-        forward_kernel(width, heads_here),
-        [((length, model), BF16), ((length, cols), F32), ((length, channels), F32), ((length, width), F32)],
-        sources,
-        x_row, w_first, conv_mine, same, segment_col, segment_rows, head_params,
-    )
+        forward_kernel(width, heads_here, len(x_pieces), len(w_first)),
+        [((length, model), BF16)]
+        + [((length, cols), F32), ((length, channels), F32), ((length, width), F32)],
+        sources + [((length, model), BF16), ((model, cols), BF16)],
+        *x_pieces, *w_first, conv_mine, segments, *head_params,
+    )
+    og_scratch, wg_scratch = ((length, model), BF16), ((model, width), BF16)
+    wo_scratch = ((width, model), BF16)
     gate, d_gated, stats = call(
-        gate_kernel(width),
+        gate_kernel(len(og_pieces), len(w_second)),
         [((length, width), F32), ((length, width), F32), ((chunks, 8, LANES), F32)],
-        [],
-        normed, w_gate, og_row, w_out, y, gain_mine,
-    )
-    step = 1
-    while step < seq_n:
-        stats = stats + swap(stats, "seq", step)
-        step *= 2
+        [og_scratch, wg_scratch, wo_scratch],
+        *og_pieces, *w_second, normed, y, gain_mine,
+    )
+    stats = gather_xor(stats, "seq")
     out_part, g_out, g_gate, d_gate, dy, g_gain = call(
-        out_kernel(width, inner),
+        out_kernel(width, inner, len(og_pieces), len(w_second)),
         [((length, model), BF16), ((width, model), BF16), ((model, width), BF16)]
         + [((length, width), BF16), ((length, width), F32), ((8, width), F32)],
-        [],
-        stats, normed, gate, d_gated, y, gain_mine, og_row, w_out,
+        [og_scratch, wo_scratch],
+        *og_pieces, *w_second, *stats, normed, gate, d_gated, y, gain_mine,
     )
 
     g_out = g_out.reshape(dp_n, out_rows, model)
     g_out = jnp.concatenate(
         [g_out[:, :, k * width : (k + 1) * width] for k in range(model // width)], 1
     )
-    early = reduce_dp(jnp.concatenate([g_gate.reshape(dp_n, -1, width), g_out], 2))
-    own_out = early[:, width:]
-    own_out = jnp.concatenate(
-        [own_out[k * out_rows : (k + 1) * out_rows] for k in range(model // width)], 1
-    )
-    back_pairs = [(target, source) for source, target in to_heads]
-    grad_out_w = lax.ppermute(own_out, ("dp", "seq"), back_pairs)
+    near_early = jnp.concatenate([g_gate.reshape(dp_n, -1, width), g_out], 2)
+    near_early = reduce_near(near_early)
     result = tree_sum(
         [p.astype(F32) for p in scatter_xor(out_part.reshape(seq_n, piece, model), "seq")]
     )
     result = hidden_in[0].astype(F32) + result
 
-    g_in, dn, conv_grad, head_grad, norm_grad = call(
-        backward_kernel(width, heads_here),
-        [((model, cols), BF16), ((length, model), BF16), ((8, channels), F32)]
-        + [((8, LANES), F32), ((8, model), F32)],
+    dconv, draw, conv_grad, head_grad = call(
+        mixer_back_kernel(width),
+        [((length, channels), BF16), ((length, LANES), BF16)]
+        + [((8, channels), F32), ((8, LANES), F32)],
         sources
         + [(tall, width), (length, width), (length, LANES), (tall, width), (tall, STATE)]
-        + [(length, channels), (length, LANES)],
-        x_row, normed, w_first, w_gate, conv_mine, same, segment_col, segment_rows, head_params,
-        proj, pre, y, dy, d_gate,
-    )
-
+        + [(length, channels)],
+        conv_mine, segments, *head_params, proj, pre, y, dy,
+    )
+
+    g_in, dn, norm_grad = call(
+        weight_back_kernel(len(x_pieces), len(w_first)),
+        [((model, cols), BF16), ((length, model), BF16), ((1, model), F32)],
+        [((length, model), BF16), ((model, cols), BF16), wg_scratch],
+        *x_pieces, *w_first, *w_second, normed, dconv, draw, d_gate,
+    )
+    near_late = reduce_near(g_in.reshape(dp_n, -1, cols))
+    early = reduce_far(near_early)
     conv_full = jnp.zeros((CONV + 1, inner), F32)
     conv_full = lax.dynamic_update_slice_in_dim(
         conv_full, conv_grad[: CONV + 1, :width], place * width, 1
@@ -589,7 +737,7 @@
     )
     small = jnp.concatenate(
         [
-            norm_grad[0].reshape(owners, rows),
+            norm_grad.reshape(owners, rows),
             conv_full.reshape(owners, -1),
             gain_full.reshape(owners, gate_here),
             jnp.broadcast_to(heads_full.reshape(1, -1), (owners, 3 * head_count)),
@@ -597,18 +745,23 @@
         1,
     )
     small_count = small.shape[1]
-    small = slots(small, rows).astype(BF16)
+    small = slots(small, rows)
     small_lanes = small.shape[1]
-    tail_block = g_in[:, channels:] + jnp.pad(
-        small, ((0, 0), (heads_here, LANES - heads_here - small_lanes))
-    )
-    late = jnp.concatenate([g_in[:, :channels], tail_block], 1).reshape(dp_n, -1, cols)
-    late = reduce_dp(late)
+    small = jnp.pad(small, ((0, 0), (heads_here, LANES - heads_here - small_lanes))).astype(BF16)
+    near_small = reduce_near(small.reshape(dp_n, -1, LANES))
+    near_late = near_late + jnp.pad(near_small, ((0, 0), (0, 0), (channels, 0)))
+    late = reduce_far(near_late)
+    own_out = early[:, width:]
+    own_out = jnp.concatenate(
+        [own_out[k * out_rows : (k + 1) * out_rows] for k in range(model // width)], 1
+    )
+    back_pairs = [(target, source) for source, target in to_heads]
+    grad_out_w = lax.ppermute(own_out, ("dp", "seq"), back_pairs)
     dn_parts = scatter_xor(dn.reshape(seq_n, piece, model), "seq")
     d_normed = tree_sum([p.astype(F32) for p in dn_parts])
 
     both = jnp.concatenate([late, early[:, :width]], 1).reshape(seq_n, rows, cols + width)
-    parts = scatter_xor(both, "seq")
+    parts = [p.astype(F32) for p in scatter_xor(both.astype(BF16), "seq")]
     ordered = in_order(parts, place)
     grad_in_w = jnp.concatenate(
         [b[:, cols:] for b in ordered]
@@ -620,8 +773,8 @@
     first = channels + heads_here
     small = tree_sum([p[:, first : first + small_lanes] for p in parts])
     small = small.reshape(-1)[:small_count]
+    grad_norm = small[:rows]
     at = rows
-    grad_norm = small[:at]
     conv_own = small[at : at + (CONV + 1) * conv_here].reshape(CONV + 1, conv_here)
     at += (CONV + 1) * conv_here
     grad_gain = small[at : at + gate_here]
@@ -630,7 +783,7 @@
 
     widened = hidden_in[0].astype(F32)
     inverse = lax.rsqrt(jnp.mean(widened * widened, axis=-1, keepdims=True) + EPSILON)
-    gain_full_row = tail[:, heads_here].astype(F32)[None, :]
+    gain_full_row = tail[:, :, heads_here].reshape(1, -1).astype(F32)
     scaled = d_normed * gain_full_row
     along = jnp.mean(scaled * widened, axis=-1, keepdims=True)
     grad_hidden = out_grad[0].astype(F32) + inverse * (scaled - widened * (inverse * inverse * along))
@@ -677,6 +830,7 @@
         P(("dp", "seq")),
         P(("dp", "seq"), None),
     )
+
     return jax.shard_map(
         on_device, mesh=mesh, in_specs=in_specs, out_specs=out_specs, check_vma=False
     )

time: 191 us -> 188 us (0.984)
  local copies, waits for them, and re-layouts: 24 us -> 14.2 us
  starting transfers between devices: 43.6 us -> 52.3 us
  Pallas kernels: 35.7 us -> 43.9 us
  waiting for transfers between devices: 73.6 us -> 67.7 us
  other arithmetic: 9.29 us -> 4.64 us
    pallas_call x4 -> x6, Pallas kernels: 35.7 us -> 43.9 us  [call(): pl.pallas_call(body, out_shape=[jax.ShapeDtypeStruct(shape, kind) for sha...]
    ppermute x39 -> x44, starting transfers between devices: 42.3 us -> 50.1 us  [swap(): return lax.ppermute(x, axis, [(i, i ^ offset) for i in range(count)])]
    unnamed x85 -> x92, local copies, waits for them, and re-layouts: 10 us -> 2.88 us
    ppermute x39 -> x44, waiting for transfers between devices: 73.6 us -> 67.7 us  [swap(): return lax.ppermute(x, axis, [(i, i ^ offset) for i in range(count)])]
    slice x15 -> x1, local copies, waits for them, and re-layouts: 4.06 us -> 0.13 us  [on_device(): gain_all = tail[:, spots[-1][0], first:first + gate_here]]
    squeeze x2, local copies, waits for them, and re-layouts: 0.09 us -> 2.89 us  [scatter_xor(): lax.dynamic_index_in_dim(blocks, place ^ k, 0, False)]
    another operation x6 -> x1, local copies, waits for them, and re-layouts: 2.14 us -> 0.08 us  [the longest x1 0.96 us: on_device(): jnp.stack([hidden_in[0], out_grad[0]])]
  transfers between devices with their start and end apart: 41 -> 46, of which waited for: 24 -> 17; matrix products, arithmetic and copies ran while one was open for 11% -> 8% of each run, Pallas kernels for 11% -> 5%
where the time goes in v2:
time: 188 us; the launch traced here: 184 us
  waiting for transfers between devices  67.7 us (36%)
  starting transfers between devices  52.3 us (28%)
  Pallas kernels  43.9 us (23%)
  local copies, waits for them, and re-layouts  14.2 us (8%)
  other arithmetic  4.64 us (2%)
    ppermute x44, waiting for transfers between devices, swap(): return lax.ppermute(x, axis, [(i, i ^ offset) for i in range(count)])  67.7 us
    ppermute x44, starting transfers between devices, swap(): return lax.ppermute(x, axis, [(i, i ^ offset) for i in range(count)])  50.1 us
    pallas_call x6, Pallas kernels, call(): pl.pallas_call(body, out_shape=[jax.ShapeDtypeStruct(shape, kind) for sha...  43.9 us
  transfers between devices with their start and end apart: 46, of which 17 were waited for; matrix products, arithmetic and copies ran while one was open for 8% of the time, Pallas kernels for 5%

profile of v2, /device:TPU:0, one launch (start us, length us, event | category | flops | bytes accessed | tf_op | source)
XLA Modules:
  0.0 184.3 jit_solution(13049413708425901794)
XLA Ops:
  2.4 2.4 %collective-permute-start.5 = (bf16[24,1152]{1,0:T(8,128)(2,1)}, bf16[24,1152]{1,0:T(8,128)(2,1)S(1)}, u32[]{:S(2)}, u32[]{:S(2)}) collective-permute-start(bf16[24,1152]{1,0:T(8,128)(2,1)} %get-tuple-element.38), channel_id=1, source_target_pairs={{0,3},{1,2},{2,1},{3,0},{4,7},{5,6},{6,5},{7,4},{8,11},{9,10},{10,... | collective-permute-start | bytes 165896 | tf_op jit(solution)/shard_map/ppermute | solution.py:23
  12.3 4.5 %collective-permute-start.17 = (bf16[96,768]{1,0:T(8,128)(2,1)S(1)}, bf16[96,768]{1,0:T(8,128)(2,1)S(1)}, u32[]{:S(2)}, u32[]{:S(2)}) collective-permute-start(bf16[96,768]{1,0:T(8,128)(2,1)S(1)} %slice.243.refs_4_), channel_id=1, source_target_pairs={{0,4},{4,0},{8,12},{12,8},{16,20},{20,16},{24,28},{28,24},{1,5},{5... | collective-permute-start | bytes 442376 | tf_op jit(solution)/shard_map/ppermute | solution.py:23
  16.8 2.4 %collective-permute-start.18 = (bf16[96,768]{1,0:T(8,128)(2,1)S(1)}, bf16[96,768]{1,0:T(8,128)(2,1)S(1)}, u32[]{:S(2)}, u32[]{:S(2)}) collective-permute-start(bf16[96,768]{1,0:T(8,128)(2,1)S(1)} %slice.243.refs_4_), channel_id=1, source_target_pairs={{0,8},{4,12},{8,0},{12,4},{16,24},{20,28},{24,16},{28,20},{1,9},{5... | collective-permute-start | bytes 442376 | tf_op jit(solution)/shard_map/ppermute | solution.py:23
  21.0 3.6 %collective-permute-start.20 = (bf16[96,768]{1,0:T(8,128)(2,1)S(1)}, bf16[96,768]{1,0:T(8,128)(2,1)S(1)}, u32[]{:S(2)}, u32[]{:S(2)}) collective-permute-start(bf16[96,768]{1,0:T(8,128)(2,1)S(1)} %slice.243.refs_4_), channel_id=1, source_target_pairs={{0,16},{4,20},{8,24},{12,28},{16,0},{20,4},{24,8},{28,12},{1,17},{... | collective-permute-start | bytes 442376 | tf_op jit(solution)/shard_map/ppermute | solution.py:23
  24.6 7.5 %collective-permute-done.20.refs_8_ = bf16[96,768]{1,0:T(8,128)(2,1)S(1)} collective-permute-done((bf16[96,768]{1,0:T(8,128)(2,1)S(1)}, bf16[96,768]{1,0:T(8,128)(2,1)S(1)}, u32[]{:S(2)}, u32[]{:S(2)}) %collective-permute-start.20) | collective-permute-done | bytes 147488 | tf_op jit(solution)/shard_map/ppermute | solution.py:23
  32.1 2.9 %collective-permute-start.22 = (bf16[96,768]{1,0:T(8,128)(2,1)S(1)}, bf16[96,768]{1,0:T(8,128)(2,1)S(1)}, u32[]{:S(2)}, u32[]{:S(2)}) collective-permute-start(bf16[96,768]{1,0:T(8,128)(2,1)S(1)} %slice.243.refs_4_), channel_id=1, source_target_pairs={{0,24},{4,28},{8,16},{12,20},{16,8},{20,12},{24,0},{28,4},{1,25},{... | collective-permute-start | bytes 442376 | tf_op jit(solution)/shard_map/ppermute | solution.py:23
  35.3 4.3 %collective-permute-done.22.refs_10_ = bf16[96,768]{1,0:T(8,128)(2,1)S(1)} collective-permute-done((bf16[96,768]{1,0:T(8,128)(2,1)S(1)}, bf16[96,768]{1,0:T(8,128)(2,1)S(1)}, u32[]{:S(2)}, u32[]{:S(2)}) %collective-permute-start.22) | collective-permute-done | bytes 147488 | tf_op jit(solution)/shard_map/ppermute | solution.py:23
  41.0 4.9 %collective-permute-done.23.refs_11_ = bf16[96,768]{1,0:T(8,128)(2,1)S(1)} collective-permute-done((bf16[96,768]{1,0:T(8,128)(2,1)S(1)}, bf16[96,768]{1,0:T(8,128)(2,1)S(1)}, u32[]{:S(2)}, u32[]{:S(2)}) %collective-permute-start.23) | collective-permute-done | bytes 147488 | tf_op jit(solution)/shard_map/ppermute | solution.py:23
  45.9 2.3 %collective-permute-start.1 = (bf16[128,768]{1,0:T(8,128)(2,1)S(1)}, bf16[128,768]{1,0:T(8,128)(2,1)S(1)}, u32[]{:S(2)}, u32[]{:S(2)}) collective-permute-start(bf16[128,768]{1,0:T(8,128)(2,1)S(1)} %bitcast.186), channel_id=1, source_target_pairs={{0,2},{1,3},{2,0},{3,1},{4,6},{5,7},{6,4},{7,5},{8,10},{9,11},{10,... | collective-permute-start | bytes 589832 | tf_op jit(solution)/shard_map/ppermute | solution.py:23
  48.7 3.5 %collective-permute-start.10 = (bf16[96,768]{1,0:T(8,128)(2,1)S(1)}, bf16[96,768]{1,0:T(8,128)(2,1)S(1)}, u32[]{:S(2)}, u32[]{:S(2)}) collective-permute-start(bf16[96,768]{1,0:T(8,128)(2,1)S(1)} %maximum_maximum_fusion.refs_4_.refs_12_), channel_id=1, source_target_pairs={{0,16},{4,20},{8,24},{12,28},{16,0},{20,4},{24,8},{28,12},{1,17},{... | collective-permute-start | bytes 442376 | tf_op jit(solution)/shard_map/ppermute | solution.py:23
  56.2 6.9 %collective-permute-done.10.refs_8_.refs_16_ = bf16[96,768]{1,0:T(8,128)(2,1)S(1)} collective-permute-done((bf16[96,768]{1,0:T(8,128)(2,1)S(1)}, bf16[96,768]{1,0:T(8,128)(2,1)S(1)}, u32[]{:S(2)}, u32[]{:S(2)}) %collective-permute-start.10) | collective-permute-done | bytes 147488 | tf_op jit(solution)/shard_map/ppermute | solution.py:23
  65.9 9.8 %shard_map.204 = (bf16[512,768]{1,0:T(8,128)(2,1)}, f32[512,768]{1,0:T(8,128)}, f32[512,640]{1,0:T(8,128)}, f32[512,384]{1,0:T(8,128)}) custom-call(bf16[128,768]{1,0:T(8,128)(2,1)} %bitcast.179, bf16[128,768]{1,0:T(8,128)(2,1)} %copy-done.15, bf16[128,768]{1,0:T(8,128)(2,1)} %copy-done.16, bf16[128,768]{1,0:T(8,128)(2,1)} %copy-done.17, ...), custom_call_target="tpu_custom_call" | custom-call | tf_op jit(solution)/shard_map/pallas_call | solution.py:553
  77.2 4.1 %shard_map.205 = (f32[512,384]{1,0:T(8,128)}, f32[512,384]{1,0:T(8,128)}, f32[4,8,128]{2,1,0:T(8,128)}) custom-call(bf16[128,768]{1,0:T(8,128)(2,1)} %bitcast.183, bf16[128,768]{1,0:T(8,128)(2,1)} %copy-done.18, bf16[128,768]{1,0:T(8,128)(2,1)} %copy-done.19, bf16[128,768]{1,0:T(8,128)(2,1)} %copy-done.20, bf16[96,768]{1,0:T(8,128)(2,1)} %copy-done.1, ...), custom_call_target="tpu_custom_call" | custom-call | tf_op jit(solution)/shard_map/pallas_call | solution.py:553
  85.9 5.5 %shard_map.206 = (bf16[512,768]{1,0:T(8,128)(2,1)}, bf16[384,768]{1,0:T(8,128)(2,1)}, bf16[768,384]{1,0:T(8,128)(2,1)}, bf16[512,384]{1,0:T(8,128)(2,1)}, f32[512,384]{1,0:T(8,128)}, /*index=5*/f32[8,384]{1,0:T(8,128)}) custom-call(bf16[128,768]{1,0:T(8,128)(2,1)} %bitcast.184, bf16[128,768]{1,0:T(8,128)(2,1)} %copy-done.18, bf16[128,768]{1,0:T(8,128)(2,1)} %copy-done.19, ...), custom_call_target="tpu_custom_call" | custom-call | tf_op jit(solution)/shard_map/pallas_call | solution.py:553
  91.4 16.9 %shard_map.207 = (bf16[512,640]{1,0:T(8,128)(2,1)}, bf16[512,128]{1,0:T(8,128)(2,1)}, f32[8,640]{1,0:T(8,128)}, f32[8,128]{1,0:T(8,128)}) custom-call(f32[8,640]{1,0:T(8,128)} %fusion.27.refs_12_.conv_ref, s32[1,512]{1,0:T(1,128)} %seg_ref.1, f32[1,24]{1,0:T(1,128)} %bitcast.208, f32[1,24]{1,0:T(1,128)} %bitcast.210, f32[1,24]{1,0:T(1,128)} %bitcast.212, ...), custom_call_target="tpu_custom_call" | custom-call | tf_op jit(solution)/shard_map/pallas_call | solution.py:553
  108.3 5.9 %shard_map.208 = (bf16[768,768]{1,0:T(8,128)(2,1)}, bf16[512,768]{1,0:T(8,128)(2,1)}, f32[1,768]{1,0:T(1,128)}) custom-call(bf16[128,768]{1,0:T(8,128)(2,1)} %bitcast.180, bf16[128,768]{1,0:T(8,128)(2,1)} %copy-done.15, bf16[128,768]{1,0:T(8,128)(2,1)} %copy-done.16, bf16[128,768]{1,0:T(8,128)(2,1)} %copy-done.17, bf16[96,768]{1,0:T(8,128)(2,1)} %copy-done.12, ...), custom_call_target="tpu_custom_call" | custom-call | tf_op jit(solution)/shard_map/pallas_call | solution.py:553
  126.0 3.9 %collective-permute-done.34 = bf16[4,96,128]{2,1,0:T(8,128)(2,1)S(1)} collective-permute-done((bf16[4,96,128]{2,1,0:T(8,128)(2,1)S(1)}, bf16[4,96,128]{2,1,0:T(8,128)(2,1)S(1)}, u32[]{:S(2)}, u32[]{:S(2)}) %collective-permute-start.34) | collective-permute-done | bytes 98336 | tf_op jit(solution)/shard_map/ppermute | solution.py:23
  133.0 3.3 %collective-permute-done.28 = bf16[128,768]{1,0:T(8,128)(2,1)S(1)} collective-permute-done((bf16[128,768]{1,0:T(8,128)(2,1)S(1)}, bf16[128,768]{1,0:T(8,128)(2,1)S(1)}, u32[]{:S(2)}, u32[]{:S(2)}) %collective-permute-start.28) | collective-permute-done | bytes 196640 | tf_op jit(solution)/shard_map/ppermute | solution.py:23
  137.4 9.5 %collective-permute-done.38 = bf16[4,96,768]{2,1,0:T(8,128)(2,1)S(1)} collective-permute-done((bf16[4,96,768]{2,1,0:T(8,128)(2,1)S(1)}, bf16[4,96,768]{2,1,0:T(8,128)(2,1)S(1)}, u32[]{:S(2)}, u32[]{:S(2)}) %collective-permute-start.38) | collective-permute-done | bytes 589856 | tf_op jit(solution)/shard_map/ppermute | solution.py:23
  147.1 2.2 %collective-permute-start.41 = (bf16[96,768]{1,0:T(8,128)(2,1)S(1)}, bf16[96,768]{1,0:T(8,128)(2,1)S(1)}, u32[]{:S(2)}, u32[]{:S(2)}) collective-permute-start(bf16[96,768]{1,0:T(8,128)(2,1)S(1)} %get-tuple-element.71), channel_id=1, source_target_pairs={{0,24},{4,28},{8,16},{12,20},{16,8},{20,12},{24,0},{28,4},{1,25},{... | collective-permute-start | bytes 442376 | tf_op jit(solution)/shard_map/ppermute | solution.py:23
  151.6 7.4 %collective-permute-done.33 = bf16[4,96,768]{2,1,0:T(8,128)(2,1)S(1)} collective-permute-done((bf16[4,96,768]{2,1,0:T(8,128)(2,1)S(1)}, bf16[4,96,768]{2,1,0:T(8,128)(2,1)S(1)}, u32[]{:S(2)}, u32[]{:S(2)}) %collective-permute-start.33) | collective-permute-done | bytes 589856 | tf_op jit(solution)/shard_map/ppermute | solution.py:23
  159.2 2.2 %collective-permute-start.37 = (bf16[96,768]{1,0:T(8,128)(2,1)S(1)}, bf16[96,768]{1,0:T(8,128)(2,1)S(1)}, u32[]{:S(2)}, u32[]{:S(2)}) collective-permute-start(bf16[96,768]{1,0:T(8,128)(2,1)S(1)} %get-tuple-element.68), channel_id=1, source_target_pairs={{0,24},{4,28},{8,16},{12,20},{16,8},{20,12},{24,0},{28,4},{1,25},{... | collective-permute-start | bytes 442376 | tf_op jit(solution)/shard_map/ppermute | solution.py:23
  163.8 4.1 %collective-permute-done.37 = bf16[96,768]{1,0:T(8,128)(2,1)S(1)} collective-permute-done((bf16[96,768]{1,0:T(8,128)(2,1)S(1)}, bf16[96,768]{1,0:T(8,128)(2,1)S(1)}, u32[]{:S(2)}, u32[]{:S(2)}) %collective-permute-start.37) | collective-permute-done | bytes 147488 | tf_op jit(solution)/shard_map/ppermute | solution.py:23
  167.9 6.4 %collective-permute-done.36 = bf16[96,768]{1,0:T(8,128)(2,1)S(1)} collective-permute-done((bf16[96,768]{1,0:T(8,128)(2,1)S(1)}, bf16[96,768]{1,0:T(8,128)(2,1)S(1)}, u32[]{:S(2)}, u32[]{:S(2)}) %collective-permute-start.36) | collective-permute-done | bytes 147488 | tf_op jit(solution)/shard_map/ppermute | solution.py:23
  (252 shorter events, 56.6 us)
Async XLA Ops:
  5.5 43.1 %collective-permute-start.14 = (bf16[128,768]{1,0:T(8,128)(2,1)}, bf16[128,768]{1,0:T(8,128)(2,1)S(1)}, u32[]{:S(2)}, u32[]{:S(2)}) collective-permute-start(bf16[128,768]{1,0:T(8,128)(2,1)} %bitcast.176), channel_id=1, source_target_pairs={{0,1},{1,0},{2,3},{3,2},{4,5},{5,4},{6,7},{7,6},{8,9},{9,8},{10,11... | collective-permute-start | bytes 589832 | tf_op jit(solution)/shard_map/ppermute | solution.py:23
  5.9 42.8 %collective-permute-start.15 = (bf16[128,768]{1,0:T(8,128)(2,1)}, bf16[128,768]{1,0:T(8,128)(2,1)S(1)}, u32[]{:S(2)}, u32[]{:S(2)}) collective-permute-start(bf16[128,768]{1,0:T(8,128)(2,1)} %bitcast.177), channel_id=1, source_target_pairs={{0,2},{1,3},{2,0},{3,1},{4,6},{5,7},{6,4},{7,5},{8,10},{9,11},{10,... | collective-permute-start | bytes 589832 | tf_op jit(solution)/shard_map/ppermute | solution.py:23
  7.4 44.8 %collective-permute-start.16 = (bf16[128,768]{1,0:T(8,128)(2,1)}, bf16[128,768]{1,0:T(8,128)(2,1)S(1)}, u32[]{:S(2)}, u32[]{:S(2)}) collective-permute-start(bf16[128,768]{1,0:T(8,128)(2,1)} %bitcast.178), channel_id=1, source_target_pairs={{0,3},{1,2},{2,1},{3,0},{4,7},{5,6},{6,5},{7,4},{8,11},{9,10},{10,... | collective-permute-start | bytes 589832 | tf_op jit(solution)/shard_map/ppermute | solution.py:23
  21.0 11.1 %collective-permute-start.20 = (bf16[96,768]{1,0:T(8,128)(2,1)S(1)}, bf16[96,768]{1,0:T(8,128)(2,1)S(1)}, u32[]{:S(2)}, u32[]{:S(2)}) collective-permute-start(bf16[96,768]{1,0:T(8,128)(2,1)S(1)} %slice.243.refs_4_), channel_id=1, source_target_pairs={{0,16},{4,20},{8,24},{12,28},{16,0},{20,4},{24,8},{28,12},{1,17},{... | collective-permute-start | bytes 442376 | tf_op jit(solution)/shard_map/ppermute | solution.py:23
  24.5 10.5 %collective-permute-start.19 = (bf16[96,768]{1,0:T(8,128)(2,1)S(1)}, bf16[96,768]{1,0:T(8,128)(2,1)S(1)}, u32[]{:S(2)}, u32[]{:S(2)}) collective-permute-start(bf16[96,768]{1,0:T(8,128)(2,1)S(1)} %collective-permute-done.18.refs_6_), channel_id=1, source_target_pairs={{0,4},{4,0},{8,12},{12,8},{16,20},{20,16},{24,28},{28,24},{1,5},{5... | collective-permute-start | bytes 442376 | tf_op jit(solution)/shard_map/ppermute | solution.py:23
  39.6 13.6 %collective-permute-start = (bf16[128,768]{1,0:T(8,128)(2,1)S(1)}, bf16[128,768]{1,0:T(8,128)(2,1)S(1)}, u32[]{:S(2)}, u32[]{:S(2)}) collective-permute-start(bf16[128,768]{1,0:T(8,128)(2,1)S(1)} %bitcast.185), channel_id=1, source_target_pairs={{0,1},{1,0},{2,3},{3,2},{4,5},{5,4},{6,7},{7,6},{8,9},{9,8},{10,11... | collective-permute-start | bytes 589832 | tf_op jit(solution)/shard_map/ppermute | solution.py:23
  48.7 14.4 %collective-permute-start.10 = (bf16[96,768]{1,0:T(8,128)(2,1)S(1)}, bf16[96,768]{1,0:T(8,128)(2,1)S(1)}, u32[]{:S(2)}, u32[]{:S(2)}) collective-permute-start(bf16[96,768]{1,0:T(8,128)(2,1)S(1)} %maximum_maximum_fusion.refs_4_.refs_12_), channel_id=1, source_target_pairs={{0,16},{4,20},{8,24},{12,28},{16,0},{20,4},{24,8},{28,12},{1,17},{... | collective-permute-start | bytes 442376 | tf_op jit(solution)/shard_map/ppermute | solution.py:23
  52.2 11.3 %collective-permute-start.12 = (bf16[96,768]{1,0:T(8,128)(2,1)S(1)}, bf16[96,768]{1,0:T(8,128)(2,1)S(1)}, u32[]{:S(2)}, u32[]{:S(2)}) collective-permute-start(bf16[96,768]{1,0:T(8,128)(2,1)S(1)} %maximum_maximum_fusion.refs_4_.refs_12_), channel_id=1, source_target_pairs={{0,24},{4,28},{8,16},{12,20},{16,8},{20,12},{24,0},{28,4},{1,25},{... | collective-permute-start | bytes 442376 | tf_op jit(solution)/shard_map/ppermute | solution.py:23
  53.2 23.0 %collective-permute-start.2 = (bf16[128,768]{1,0:T(8,128)(2,1)S(1)}, bf16[128,768]{1,0:T(8,128)(2,1)S(1)}, u32[]{:S(2)}, u32[]{:S(2)}) collective-permute-start(bf16[128,768]{1,0:T(8,128)(2,1)S(1)} %bitcast.187), channel_id=1, source_target_pairs={{0,3},{1,2},{2,1},{3,0},{4,7},{5,6},{6,5},{7,4},{8,11},{9,10},{10,... | collective-permute-start | bytes 589832 | tf_op jit(solution)/shard_map/ppermute | solution.py:23
  53.3 22.9 %collective-permute-start.7 = (bf16[96,768]{1,0:T(8,128)(2,1)S(1)}, bf16[96,768]{1,0:T(8,128)(2,1)S(1)}, u32[]{:S(2)}, u32[]{:S(2)}) collective-permute-start(bf16[96,768]{1,0:T(8,128)(2,1)S(1)} %maximum_maximum_fusion.refs_4_.refs_12_), channel_id=1, source_target_pairs={{0,4},{4,0},{8,12},{12,8},{16,20},{20,16},{24,28},{28,24},{1,5},{5... | collective-permute-start | bytes 442376 | tf_op jit(solution)/shard_map/ppermute | solution.py:23
  55.7 20.6 %collective-permute-start.9 = (bf16[96,768]{1,0:T(8,128)(2,1)S(1)}, bf16[96,768]{1,0:T(8,128)(2,1)S(1)}, u32[]{:S(2)}, u32[]{:S(2)}) collective-permute-start(bf16[96,768]{1,0:T(8,128)(2,1)S(1)} %collective-permute-done.8.refs_6_.refs_14_), channel_id=1, source_target_pairs={{0,4},{4,0},{8,12},{12,8},{16,20},{20,16},{24,28},{28,24},{1,5},{5... | collective-permute-start | bytes 442376 | tf_op jit(solution)/shard_map/ppermute | solution.py:23
  63.1 13.2 %collective-permute-start.11 = (bf16[96,768]{1,0:T(8,128)(2,1)S(1)}, bf16[96,768]{1,0:T(8,128)(2,1)S(1)}, u32[]{:S(2)}, u32[]{:S(2)}) collective-permute-start(bf16[96,768]{1,0:T(8,128)(2,1)S(1)} %collective-permute-done.10.refs_8_.refs_16_), channel_id=1, source_target_pairs={{0,4},{4,0},{8,12},{12,8},{16,20},{20,16},{24,28},{28,24},{1,5},{5... | collective-permute-start | bytes 442376 | tf_op jit(solution)/shard_map/ppermute | solution.py:23
  63.5 12.8 %collective-permute-start.13 = (bf16[96,768]{1,0:T(8,128)(2,1)S(1)}, bf16[96,768]{1,0:T(8,128)(2,1)S(1)}, u32[]{:S(2)}, u32[]{:S(2)}) collective-permute-start(bf16[96,768]{1,0:T(8,128)(2,1)S(1)} %collective-permute-done.12.refs_10_.refs_18_), channel_id=1, source_target_pairs={{0,4},{4,0},{8,12},{12,8},{16,20},{20,16},{24,28},{28,24},{1,5},{5... | collective-permute-start | bytes 442376 | tf_op jit(solution)/shard_map/ppermute | solution.py:23
  116.3 14.3 %collective-permute-start.32 = (bf16[128,768]{1,0:T(8,128)(2,1)}, bf16[128,768]{1,0:T(8,128)(2,1)S(1)}, u32[]{:S(2)}, u32[]{:S(2)}) collective-permute-start(bf16[128,768]{1,0:T(8,128)(2,1)} %get-tuple-element.62), channel_id=1, source_target_pairs={{0,3},{1,2},{2,1},{3,0},{4,7},{5,6},{6,5},{7,4},{8,11},{9,10},{10,... | collective-permute-start | bytes 589832 | tf_op jit(solution)/shard_map/ppermute | solution.py:23
  117.5 13.2 %collective-permute-start.31 = (bf16[128,768]{1,0:T(8,128)(2,1)}, bf16[128,768]{1,0:T(8,128)(2,1)S(1)}, u32[]{:S(2)}, u32[]{:S(2)}) collective-permute-start(bf16[128,768]{1,0:T(8,128)(2,1)} %get-tuple-element.63), channel_id=1, source_target_pairs={{0,2},{1,3},{2,0},{3,1},{4,6},{5,7},{6,4},{7,5},{8,10},{9,11},{10,... | collective-permute-start | bytes 589832 | tf_op jit(solution)/shard_map/ppermute | solution.py:23
  118.0 13.2 %collective-permute-start.30 = (bf16[128,768]{1,0:T(8,128)(2,1)}, bf16[128,768]{1,0:T(8,128)(2,1)S(1)}, u32[]{:S(2)}, u32[]{:S(2)}) collective-permute-start(bf16[128,768]{1,0:T(8,128)(2,1)} %get-tuple-element.61), channel_id=1, source_target_pairs={{0,1},{1,0},{2,3},{3,2},{4,5},{5,4},{6,7},{7,6},{8,9},{9,8},{10,11... | collective-permute-start | bytes 589832 | tf_op jit(solution)/shard_map/ppermute | solution.py:23
  119.0 14.0 %collective-permute-start.29 = (bf16[128,768]{1,0:T(8,128)(2,1)}, bf16[128,768]{1,0:T(8,128)(2,1)S(1)}, u32[]{:S(2)}, u32[]{:S(2)}) collective-permute-start(bf16[128,768]{1,0:T(8,128)(2,1)} %get-tuple-element.65), channel_id=1, source_target_pairs={{0,3},{1,2},{2,1},{3,0},{4,7},{5,6},{6,5},{7,4},{8,11},{9,10},{10,... | collective-permute-start | bytes 589832 | tf_op jit(solution)/shard_map/ppermute | solution.py:23
  130.6 16.3 %collective-permute-start.38 = (bf16[4,96,768]{2,1,0:T(8,128)(2,1)S(1)}, bf16[4,96,768]{2,1,0:T(8,128)(2,1)S(1)}, u32[]{:S(2)}, u32[]{:S(2)}) collective-permute-start(bf16[4,96,768]{2,1,0:T(8,128)(2,1)S(1)} %fusion.4), channel_id=1, source_target_pairs={{0,4},{4,0},{8,12},{12,8},{16,20},{20,16},{24,28},{28,24},{1,5},{5... | collective-permute-start | bytes 1769480 | tf_op jit(solution)/shard_map/ppermute | solution.py:23
  131.2 27.8 %collective-permute-start.33 = (bf16[4,96,768]{2,1,0:T(8,128)(2,1)S(1)}, bf16[4,96,768]{2,1,0:T(8,128)(2,1)S(1)}, u32[]{:S(2)}, u32[]{:S(2)}) collective-permute-start(bf16[4,96,768]{2,1,0:T(8,128)(2,1)S(1)} %dynamic-slice_bitcast_fusion), channel_id=1, source_target_pairs={{0,4},{4,0},{8,12},{12,8},{16,20},{20,16},{24,28},{28,24},{1,5},{5... | collective-permute-start | bytes 1769480 | tf_op jit(solution)/shard_map/ppermute | solution.py:23
  147.1 14.4 %collective-permute-start.41 = (bf16[96,768]{1,0:T(8,128)(2,1)S(1)}, bf16[96,768]{1,0:T(8,128)(2,1)S(1)}, u32[]{:S(2)}, u32[]{:S(2)}) collective-permute-start(bf16[96,768]{1,0:T(8,128)(2,1)S(1)} %get-tuple-element.71), channel_id=1, source_target_pairs={{0,24},{4,28},{8,16},{12,20},{16,8},{20,12},{24,0},{28,4},{1,25},{... | collective-permute-start | bytes 442376 | tf_op jit(solution)/shard_map/ppermute | solution.py:23
  149.3 14.4 %collective-permute-start.40 = (bf16[96,768]{1,0:T(8,128)(2,1)S(1)}, bf16[96,768]{1,0:T(8,128)(2,1)S(1)}, u32[]{:S(2)}, u32[]{:S(2)}) collective-permute-start(bf16[96,768]{1,0:T(8,128)(2,1)S(1)} %get-tuple-element.72), channel_id=1, source_target_pairs={{0,16},{4,20},{8,24},{12,28},{16,0},{20,4},{24,8},{28,12},{1,17},{... | collective-permute-start | bytes 442376 | tf_op jit(solution)/shard_map/ppermute | solution.py:23
  149.4 14.3 %collective-permute-start.39 = (bf16[96,768]{1,0:T(8,128)(2,1)S(1)}, bf16[96,768]{1,0:T(8,128)(2,1)S(1)}, u32[]{:S(2)}, u32[]{:S(2)}) collective-permute-start(bf16[96,768]{1,0:T(8,128)(2,1)S(1)} %get-tuple-element.70), channel_id=1, source_target_pairs={{0,8},{4,12},{8,0},{12,4},{16,24},{20,28},{24,16},{28,20},{1,9},{5... | collective-permute-start | bytes 442376 | tf_op jit(solution)/shard_map/ppermute | solution.py:23
  161.4 12.9 %collective-permute-start.36 = (bf16[96,768]{1,0:T(8,128)(2,1)S(1)}, bf16[96,768]{1,0:T(8,128)(2,1)S(1)}, u32[]{:S(2)}, u32[]{:S(2)}) collective-permute-start(bf16[96,768]{1,0:T(8,128)(2,1)S(1)} %get-tuple-element.69), channel_id=1, source_target_pairs={{0,16},{4,20},{8,24},{12,28},{16,0},{20,4},{24,8},{28,12},{1,17},{... | collective-permute-start | bytes 442376 | tf_op jit(solution)/shard_map/ppermute | solution.py:23
  161.5 12.8 %collective-permute-start.35 = (bf16[96,768]{1,0:T(8,128)(2,1)S(1)}, bf16[96,768]{1,0:T(8,128)(2,1)S(1)}, u32[]{:S(2)}, u32[]{:S(2)}) collective-permute-start(bf16[96,768]{1,0:T(8,128)(2,1)S(1)} %get-tuple-element.67), channel_id=1, source_target_pairs={{0,8},{4,12},{8,0},{12,4},{16,24},{20,28},{24,16},{28,20},{1,9},{5... | collective-permute-start | bytes 442376 | tf_op jit(solution)/shard_map/ppermute | solution.py:23
  (61 other events, 666.9 us)

commit v3 on v2

--- a/solution.py
+++ b/solution.py
@@ -71,6 +71,11 @@
     return [piece for group in near for piece in group]
 
 
+def reduce_slabs(slabs):
+    parts = [swap(p, "dp", j) if j else p for j, p in enumerate(slabs)]
+    return tree_sum([p.astype(F32) for p in parts]).astype(BF16)
+
+
 def reduce_near(grads):
     count = lax.axis_size("dp")
     inner = inner_of(count)
@@ -163,10 +168,10 @@
 
 
 def masks_of(seg_col, seg_row, i):
-    column = seg_col[pl.ds(pl.multiple_of(i * CHUNK, CHUNK), CHUNK), :]
+    column = seg_col[pl.ds(i * CHUNK, CHUNK), :]
 
     def row(j):
-        return seg_row[:, pl.ds(pl.multiple_of((i + j) * CHUNK, CHUNK), CHUNK)][:1]
+        return seg_row[:, pl.ds((i + j) * CHUNK, CHUNK)][:1]
 
     far = (column == row(0)).astype(F32)
     near = (column == row(1)).astype(F32)
@@ -195,10 +200,19 @@
     return step, step * (-jnp.exp(heads[1:2]))
 
 
-def fill_sources(i, v, step, decay, expand, vd, vt, ecx):
+def spread_heads(columns, low, width):
+    pairs = []
+    for pair in range(width // LANES):
+        first = columns[:, 2 * pair : 2 * pair + 1]
+        second = columns[:, 2 * pair + 1 : 2 * pair + 2]
+        pairs.append(jnp.where(low > 0.0, first, second))
+    return jnp.concatenate(pairs, 1)
+
+
+def fill_sources(i, v, step, decay, low, vd, vt, ecx):
     cumulative = exact(triangle(True).astype(F32), decay)
-    step_x = exact(step, expand)
-    cum_x = exact(cumulative, expand)
+    step_x = spread_heads(step, low, v.shape[1])
+    cum_x = spread_heads(cumulative, low, v.shape[1])
     last = cum_x[CHUNK - 1 :]
     vd_now = v * step_x
     vd[pl.ds(i * CHUNK, CHUNK), :] = vd_now
@@ -243,6 +257,59 @@
 def small_spots(rows, lengths):
     group = min(rows, len(lengths))
     return [(i % group, (i // group) * max(lengths)) for i in range(len(lengths))]
+
+
+def store_slabs(values, outs):
+    if len(outs[0].shape) == 2:
+        outs[0][...] = values[...].astype(BF16)
+        return
+    inner, (outer, rows, _) = len(outs), outs[0].shape
+    place = lax.axis_index("dp") % inner if inner > 1 else 0
+    for j, out in enumerate(outs):
+        for o in range(outer):
+            start = (o * inner + (place ^ j)) * rows
+            if inner > 1:
+                start = pl.multiple_of(start, rows)
+            out[o] = values[pl.ds(start, rows), :].astype(BF16)
+
+
+def store_pieces(values, outs):
+    rows = outs[0].shape[0]
+    for k, out in enumerate(outs):
+        start = pl.multiple_of((lax.axis_index("seq") ^ k) * rows, rows)
+        out[...] = values[pl.ds(start, rows), :].astype(BF16)
+
+
+def finish_kernel(width, inner, heads_here, lengths, spots):
+    def body(*refs):
+        count = inner // width
+        parts, refs = refs[:count], refs[count:]
+        grad_ref, outs, blocks = refs[0], refs[1:-1], refs[-1]
+        rows = grad_ref.shape[0]
+        stride = blocks.shape[0] // count
+        states, tail = width, width + 2 * STATE
+        for k, part in enumerate(parts):
+            start = pl.multiple_of((lax.axis_index("seq") ^ k) * stride, stride)
+            blocks[pl.ds(start, rows), :] = part[...].astype(F32)
+        steps = []
+        for j in range(count):
+            at = slice(j * stride, j * stride + rows)
+            grad_ref[:, j * width : (j + 1) * width] = blocks[at, tail + LANES :]
+            grad_ref[:, inner + j * width : inner + (j + 1) * width] = blocks[at, :width]
+            steps.append(blocks[at, tail : tail + heads_here])
+        both = tree_sum([part[:, states:tail].astype(F32) for part in parts])
+        grad_ref[:, 2 * inner : 2 * inner + 2 * STATE] = both
+        grad_ref[:, 2 * inner + 2 * STATE :] = jnp.concatenate(steps, 1)
+        total = tree_sum([part[:, tail : tail + LANES].astype(F32) for part in parts])
+        found = []
+        for length, (row, lane) in zip(lengths, spots):
+            first = heads_here + lane
+            found.append(total[row : row + 1, first : first + length])
+        outs[0][...] = jnp.concatenate(found[:CONV], 0)
+        for out, vector in zip(outs[1:], found[CONV:]):
+            out[...] = vector
+
+    return body
 
 
 def pack_kernel(width, inner, heads_here, count):
@@ -314,24 +381,24 @@
         skip_x = exact(jnp.broadcast_to(heads[2:3], (8, LANES)), expand)[:1]
 
         def chunk(i, carry):
-            rows = pl.ds(pl.multiple_of(i * CHUNK, CHUNK), CHUNK)
+            rows = pl.ds(i * CHUNK, CHUNK)
             v_pre = pre_ref[rows, :width]
             c_pre = pre_ref[rows, width + STATE :]
             v = v_pre * jax.nn.sigmoid(v_pre)
             c = c_pre * jax.nn.sigmoid(c_pre)
             step, decay = decays(proj_ref[rows, channels:], heads)
-            cumulative, _, _, _ = fill_sources(i, v, step, decay, expand, vd, vt, ecx)
+            cumulative, _, _, _ = fill_sources(i, v, step, decay, low, vd, vt, ecx)
             cumulative_t = cumulative.T
             far, near, own = masks_of(seg_col, seg_row, i)
-            window = pl.ds(pl.multiple_of(i * CHUNK, CHUNK), 3 * CHUNK)
+            window = pl.ds(i * CHUNK, 3 * CHUNK)
             scores = mm_nt(c, bpad[window, :])
             s_far = scores[:, :CHUNK] * far
             s_near = scores[:, CHUNK : 2 * CHUNK] * near
             s_own = scores[:, 2 * CHUNK :]
-            ecx_now = ecx[pl.ds(pl.multiple_of(i * CHUNK, 8) + 8, CHUNK), :]
-            last_before = ecx[pl.ds(pl.multiple_of(i * CHUNK, 8), 8), :][7:8]
+            ecx_now = ecx[pl.ds(i * CHUNK + 8, CHUNK), :]
+            last_before = ecx[pl.ds(i * CHUNK, 8), :][7:8]
             vt_far = vt[rows, :] * last_before
-            vt_near = vt[pl.ds(pl.multiple_of((i + 1) * CHUNK, CHUNK), CHUNK), :]
+            vt_near = vt[pl.ds((i + 1) * CHUNK, CHUNK), :]
             off = mm(s_far, vt_far) + mm(s_near, vt_near)
             y_ref[rows, :] = off * ecx_now + skip_x * v
             for pair in range(heads_here // 2):
@@ -343,7 +410,8 @@
                 y_ref[rows, lanes] = y_ref[rows, lanes] + both
             return carry
 
-        lax.fori_loop(0, x.shape[0] // CHUNK, chunk, 0)
+        for turn in range(x.shape[0] // CHUNK):
+            chunk(turn, 0)
 
     return body
 
@@ -371,12 +439,15 @@
     return body
 
 
-def out_kernel(width, whole_width, og_count, w_count):
+def out_kernel(width, whole_width, og_count, w_count, slab_count, block_rows):
     def body(*refs):
         og_pieces, refs = refs[:og_count], refs[og_count:]
         w_pieces, refs = refs[:w_count], refs[w_count:]
         stats, refs = refs[:og_count], refs[og_count:]
-        normed_ref, gate_ref, dg_ref, y_ref, gain_ref, out_ref, gout_ref, ggate_ref, dgate_ref, dy_ref, ggain_ref, og_ref, wo_ref = refs
+        normed_ref, gate_ref, dg_ref, y_ref, gain_ref = refs[:5]
+        out_refs, refs = refs[5 : 5 + og_count], refs[5 + og_count :]
+        slabs, refs = refs[:slab_count], refs[slab_count:]
+        dgate_ref, dy_ref, ggain_ref, og_ref, wo_ref, out_all, grad_all = refs
         put_in_order(og_pieces, lax.axis_index("seq"), og_ref)
         put_second(w_pieces, dp_index(w_pieces), None, wo_ref)
         columns = []
@@ -395,15 +466,24 @@
         gain = gain_ref[...]
         scaled = v * inverse
         gated = (scaled * gain).astype(BF16)
-        out_ref[...] = dot(gated, wo_ref[...], 1, 0).astype(BF16)
-        gout_ref[...] = dot(gated, og_ref[...], 0, 0).astype(BF16)
+        out_all[...] = dot(gated, wo_ref[...], 1, 0)
+        store_pieces(out_all, out_refs)
+        rows = block_rows
+        folds = og_ref.shape[1] // width
+        part = rows // folds
+        g_out = dot(gated, og_ref[...], 0, 0)
+        for d in range(grad_all.shape[0] // rows):
+            for k in range(folds):
+                to = slice(d * rows + k * part, d * rows + (k + 1) * part)
+                grad_all[to, width:] = g_out[d * part : (d + 1) * part, k * width : (k + 1) * width]
         d_gated = dg_ref[...]
         ggain_ref[...] = jnp.broadcast_to(jnp.sum(d_gated * scaled, axis=0, keepdims=True), (8, width))
         dv = inverse * (d_gated * gain - v * (inverse * inverse * cross))
         dy_ref[...] = dv * silu
         dgate = (dv * y * (sig * (1.0 + gate * (1.0 - sig)))).astype(BF16)
         dgate_ref[...] = dgate
-        ggate_ref[...] = dot(normed_ref[...], dgate, 0, 0).astype(BF16)
+        grad_all[:, :width] = dot(normed_ref[...], dgate, 0, 0)
+        store_slabs(grad_all, slabs)
 
     return body
 
@@ -431,25 +511,26 @@
         db[...] = jnp.zeros(db.shape, F32)
 
         def prepare(i, carry):
-            rows = pl.ds(pl.multiple_of(i * CHUNK, CHUNK), CHUNK)
+            rows = pl.ds(i * CHUNK, CHUNK)
             v_pre = pre_ref[rows, :width]
             v = v_pre * jax.nn.sigmoid(v_pre)
             step, decay = decays(proj_ref[rows, channels:], heads)
-            cumulative, step_x, cum_x, last = fill_sources(i, v, step, decay, expand, vd, vt, ecx)
+            cumulative, step_x, cum_x, last = fill_sources(i, v, step, decay, low, vd, vt, ecx)
             cums[rows, :] = cumulative
             stepx[rows, :] = step_x
-            tailx[pl.ds(pl.multiple_of((i + 2) * CHUNK, CHUNK), CHUNK), :] = jnp.exp(last - cum_x)
+            tailx[pl.ds((i + 2) * CHUNK, CHUNK), :] = jnp.exp(last - cum_x)
             return carry
 
-        lax.fori_loop(0, chunks, prepare, 0)
+        for turn in range(chunks):
+            prepare(turn, 0)
 
         def chunk(turn, carry):
             later, g_bias, g_rate, g_skip = carry
             i = chunks - 1 - turn
-            rows = pl.ds(pl.multiple_of(i * CHUNK, CHUNK), CHUNK)
-            rows_near = pl.ds(pl.multiple_of((i + 1) * CHUNK, CHUNK), CHUNK)
-            rows_own = pl.ds(pl.multiple_of((i + 2) * CHUNK, CHUNK), CHUNK)
-            window = pl.ds(pl.multiple_of(i * CHUNK, CHUNK), 3 * CHUNK)
+            rows = pl.ds(i * CHUNK, CHUNK)
+            rows_near = pl.ds((i + 1) * CHUNK, CHUNK)
+            rows_own = pl.ds((i + 2) * CHUNK, CHUNK)
+            window = pl.ds(i * CHUNK, 3 * CHUNK)
             v_pre = pre_ref[rows, :width]
             v_sig = jax.nn.sigmoid(v_pre)
             v = v_pre * v_sig
@@ -467,8 +548,8 @@
             s_near = scores[:, CHUNK : 2 * CHUNK] * near
             s_own = scores[:, 2 * CHUNK :]
             dy = dy_ref[rows, :]
-            dye = dy * ecx[pl.ds(pl.multiple_of(i * CHUNK, 8) + 8, CHUNK), :]
-            dye_far = dye * ecx[pl.ds(pl.multiple_of(i * CHUNK, 8), 8), :][7:8]
+            dye = dy * ecx[pl.ds(i * CHUNK + 8, CHUNK), :]
+            dye_far = dye * ecx[pl.ds(i * CHUNK, 8), :][7:8]
             ds_far = mm_nt(dye_far, vt[rows, :]) * far
             ds_near = mm_nt(dye, vt[rows_near, :]) * near
             ua[rows, :] = ua[rows, :] + tailx[rows, :] * mm_tn(s_far, dye_far)
@@ -488,8 +569,8 @@
             dc = mm(ds_all, b_window)
             db[window, :] = db[window, :] + mm_tn(ds_all, c)
             u_total = ua[rows_own, :]
-            received = dot(dy * (y_ref[rows, :] - skip_x * v), expand, 1, 1, FULL)
-            d_step = dot(v * u_total, expand, 1, 1, FULL)
+            received = mm_nt(dy * (y_ref[rows, :] - skip_x * v), expand)
+            d_step = mm_nt(v * u_total, expand)
             gap = received - step * d_step
             d_decay = exact(triangle(False).astype(F32), gap) + later
             d_step = d_step - d_decay * rate
@@ -501,13 +582,19 @@
             b_sig = jax.nn.sigmoid(b_pre)
             dpre[rows, width : width + STATE] = db[rows_own, :] * (b_sig * (1.0 + b_pre * (1.0 - b_sig)))
             dpre[rows, width + STATE :] = dc * (c_sig * (1.0 + c_pre * (1.0 - c_sig)))
-            g_skip = g_skip + jnp.sum(dot(dy * v, expand, 1, 1, FULL), axis=0, keepdims=True)
+            g_skip = g_skip + jnp.sum(dy * v, axis=0, keepdims=True)
             g_bias = g_bias + jnp.sum(d_raw, axis=0, keepdims=True)
             g_rate = g_rate + jnp.sum(d_decay * decay, axis=0, keepdims=True)
             return (later + jnp.sum(gap, axis=0, keepdims=True), g_bias, g_rate, g_skip)
 
         none = jnp.zeros((1, LANES), F32)
-        _, g_bias, g_rate, g_skip = lax.fori_loop(0, chunks, chunk, (none, none, none, none))
+        none_wide = jnp.zeros((1, heads_here * HEAD_DIM), F32)
+        start = (none, none, none, none_wide)
+        state = start
+        for turn in range(chunks):
+            state = chunk(turn, state)
+        _, g_bias, g_rate, g_skip = state
+        g_skip = dot(jnp.broadcast_to(g_skip, (8, g_skip.shape[1])), expand, 1, 1, FULL)[:1]
         head_grad_ref[...] = jnp.concatenate([g_bias, g_rate, g_skip, jnp.zeros((5, LANES), F32)], 0)
         u = proj_ref[:, :channels]
         d = dpre[...]
@@ -525,12 +612,15 @@
     return body
 
 
-def weight_back_kernel(x_count, w_count):
+def weight_back_kernel(x_count, w_count, slab_count):
     def body(*refs):
         x_pieces, refs = refs[:x_count], refs[x_count:]
         w_pieces, refs = refs[:w_count], refs[w_count:]
         g_pieces, refs = refs[:w_count], refs[w_count:]
-        normed_ref, dconv_ref, draw_ref, dgate_ref, gin_ref, dn_ref, norm_grad_ref, x_ref, w_ref, wg_ref = refs
+        normed_ref, dconv_ref, draw_ref, dgate_ref = refs[:4]
+        slabs, refs = refs[4 : 4 + slab_count], refs[4 + slab_count :]
+        dn_refs, refs = refs[:x_count], refs[x_count:]
+        norm_grad_ref, x_ref, w_ref, wg_ref, dn_all, gin_ref = refs
         put_in_order(x_pieces, lax.axis_index("seq"), x_ref)
         put_in_order(w_pieces, dp_index(w_pieces), w_ref)
         put_second(g_pieces, dp_index(w_pieces), wg_ref)
@@ -538,12 +628,14 @@
         dconv, draw = dconv_ref[...], draw_ref[...]
         dn = dot(dconv, w_ref[:, :channels], 1, 1) + dot(draw, w_ref[:, channels:], 1, 1)
         dn = dn + dot(dgate_ref[...], wg_ref[...], 1, 1)
-        dn_ref[...] = dn.astype(BF16)
-        gin_ref[:, :channels] = dot(normed_ref[...], dconv, 0, 0).astype(BF16)
+        dn_all[...] = dn
+        store_pieces(dn_all, dn_refs)
+        gin_ref[:, :channels] = dot(normed_ref[...], dconv, 0, 0)
         x = x_ref[...].astype(F32)
         along = jnp.sum(dn * (x * rms_inverse(x)), axis=0, keepdims=True)
         norm_grad_ref[...] = along
-        gin_ref[:, channels:] = dot(normed_ref[...], draw, 0, 0).astype(BF16)
+        gin_ref[:, channels:] = dot(normed_ref[...], draw, 0, 0)
+        store_slabs(gin_ref, slabs)
 
     return body
 
@@ -561,12 +653,6 @@
         ],
         compiler_params=pltpu.CompilerParams(vmem_limit_bytes=VMEM_LIMIT),
     )(*operands)
-
-
-def slots(flat, rows):
-    owners, count = flat.shape
-    lanes = -(-count // rows)
-    return jnp.pad(flat, ((0, 0), (0, lanes * rows - count))).reshape(owners * rows, lanes)
 
 
 def on_device(
@@ -686,22 +772,32 @@
         *og_pieces, *w_second, normed, y, gain_mine,
     )
     stats = gather_xor(stats, "seq")
-    out_part, g_out, g_gate, d_gate, dy, g_gain = call(
-        out_kernel(width, inner, len(og_pieces), len(w_second)),
-        [((length, model), BF16), ((width, model), BF16), ((model, width), BF16)]
+    block_rows = rows * seq_n
+    dp_inner = inner_of(dp_n)
+    if split_here:
+        slabs = [((dp_n // dp_inner, block_rows, cols), BF16)] * dp_inner
+    else:
+        slabs = [((model, cols), BF16)]
+    pieces = [((piece, model), BF16)] * seq_n
+
+    def near_sum(made):
+        if split_here:
+            return reduce_slabs(made)
+        return reduce_near(made[0].reshape(dp_n, -1, made[0].shape[-1]))
+
+    second_slabs = [((*shape[:-1], 2 * width), kind) for shape, kind in slabs]
+    made = call(
+        out_kernel(width, inner, len(og_pieces), len(w_second), len(slabs), block_rows),
+        pieces + second_slabs
         + [((length, width), BF16), ((length, width), F32), ((8, width), F32)],
-        [og_scratch, wo_scratch],
+        [og_scratch, wo_scratch, (length, model), (model, 2 * width)],
         *og_pieces, *w_second, *stats, normed, gate, d_gated, y, gain_mine,
     )
-
-    g_out = g_out.reshape(dp_n, out_rows, model)
-    g_out = jnp.concatenate(
-        [g_out[:, :, k * width : (k + 1) * width] for k in range(model // width)], 1
-    )
-    near_early = jnp.concatenate([g_gate.reshape(dp_n, -1, width), g_out], 2)
-    near_early = reduce_near(near_early)
+    out_parts, made = made[:seq_n], made[seq_n:]
+    near_early = near_sum(made[: len(slabs)])
+    d_gate, dy, g_gain = made[len(slabs) :]
     result = tree_sum(
-        [p.astype(F32) for p in scatter_xor(out_part.reshape(seq_n, piece, model), "seq")]
+        [(swap(p, "seq", k) if k else p).astype(F32) for k, p in enumerate(out_parts)]
     )
     result = hidden_in[0].astype(F32) + result
 
@@ -715,13 +811,14 @@
         conv_mine, segments, *head_params, proj, pre, y, dy,
     )
 
-    g_in, dn, norm_grad = call(
-        weight_back_kernel(len(x_pieces), len(w_first)),
-        [((model, cols), BF16), ((length, model), BF16), ((1, model), F32)],
-        [((length, model), BF16), ((model, cols), BF16), wg_scratch],
+    made = call(
+        weight_back_kernel(len(x_pieces), len(w_first), len(slabs)),
+        slabs + pieces + [((1, model), F32)],
+        [((length, model), BF16), ((model, cols), BF16), wg_scratch, (length, model), (model, cols)],
         *x_pieces, *w_first, *w_second, normed, dconv, draw, d_gate,
     )
-    near_late = reduce_near(g_in.reshape(dp_n, -1, cols))
+    dn_pieces, norm_grad = made[len(slabs) : -1], made[-1]
+    near_late = near_sum(made[: len(slabs)])
     early = reduce_far(near_early)
     conv_full = jnp.zeros((CONV + 1, inner), F32)
     conv_full = lax.dynamic_update_slice_in_dim(
@@ -735,19 +832,26 @@
     heads_full = lax.dynamic_update_slice_in_dim(
         jnp.zeros((3, head_count), F32), head_grad[:3, :heads_here], place * heads_here, 1
     )
+    heads_rows = jnp.broadcast_to(heads_full[None], (owners, 3, head_count))
+    lengths = [conv_here] * (CONV + 1) + [gate_here, rows] + [head_count] * 3
+    small_at = small_spots(rows, lengths)
+    group, longest = min(rows, len(lengths)), max(lengths)
+
+    def fit(vectors):
+        return jnp.pad(vectors, ((0, 0), (0, 0), (0, longest - vectors.shape[2])))
+
     small = jnp.concatenate(
-        [
-            norm_grad.reshape(owners, rows),
-            conv_full.reshape(owners, -1),
-            gain_full.reshape(owners, gate_here),
-            jnp.broadcast_to(heads_full.reshape(1, -1), (owners, 3 * head_count)),
-        ],
+        [fit(conv_full), fit(gain_full.reshape(owners, 1, gate_here))]
+        + [fit(norm_grad.reshape(owners, 1, rows)), fit(heads_rows)],
         1,
     )
-    small_count = small.shape[1]
-    small = slots(small, rows)
-    small_lanes = small.shape[1]
-    small = jnp.pad(small, ((0, 0), (heads_here, LANES - heads_here - small_lanes))).astype(BF16)
+    sets = -(-len(lengths) // group)
+    small = jnp.pad(small, ((0, 0), (0, sets * group - len(lengths)), (0, 0)))
+    small = jnp.concatenate([small[:, g * group : (g + 1) * group] for g in range(sets)], 2)
+    small = jnp.pad(
+        small,
+        ((0, 0), (0, rows - group), (heads_here, LANES - heads_here - small.shape[2])),
+    ).astype(BF16)
     near_small = reduce_near(small.reshape(dp_n, -1, LANES))
     near_late = near_late + jnp.pad(near_small, ((0, 0), (0, 0), (channels, 0)))
     late = reduce_far(near_late)
@@ -757,29 +861,18 @@
     )
     back_pairs = [(target, source) for source, target in to_heads]
     grad_out_w = lax.ppermute(own_out, ("dp", "seq"), back_pairs)
-    dn_parts = scatter_xor(dn.reshape(seq_n, piece, model), "seq")
+    dn_parts = [swap(p, "seq", k) if k else p for k, p in enumerate(dn_pieces)]
     d_normed = tree_sum([p.astype(F32) for p in dn_parts])
 
     both = jnp.concatenate([late, early[:, :width]], 1).reshape(seq_n, rows, cols + width)
-    parts = [p.astype(F32) for p in scatter_xor(both.astype(BF16), "seq")]
-    ordered = in_order(parts, place)
-    grad_in_w = jnp.concatenate(
-        [b[:, cols:] for b in ordered]
-        + [b[:, :width] for b in ordered]
-        + [tree_sum([p[:, width:channels] for p in parts])]
-        + [b[:, channels : channels + heads_here] for b in ordered],
-        1,
-    )
-    first = channels + heads_here
-    small = tree_sum([p[:, first : first + small_lanes] for p in parts])
-    small = small.reshape(-1)[:small_count]
-    grad_norm = small[:rows]
-    at = rows
-    conv_own = small[at : at + (CONV + 1) * conv_here].reshape(CONV + 1, conv_here)
-    at += (CONV + 1) * conv_here
-    grad_gain = small[at : at + gate_here]
-    at += gate_here
-    head_own = small[at:].reshape(3, head_count)
+    parts = scatter_xor(both.astype(BF16), "seq")
+    short = [((CONV, conv_here), F32)] + [((1, n), F32) for n in lengths[CONV:]]
+    grad_in_w, *short = call(
+        finish_kernel(width, inner, heads_here, lengths, small_at),
+        [((rows, in_weight.shape[1]), F32)] + short,
+        [(seq_n * stride, cols + width)],
+        *parts,
+    )
 
     widened = hidden_in[0].astype(F32)
     inverse = lax.rsqrt(jnp.mean(widened * widened, axis=-1, keepdims=True) + EPSILON)
@@ -790,14 +883,14 @@
     return (
         result[None],
         grad_hidden[None],
-        grad_norm,
+        short[3][0],
         grad_in_w,
-        conv_own[:CONV],
-        conv_own[CONV],
-        head_own[0],
-        head_own[1],
-        head_own[2],
-        grad_gain,
+        short[0],
+        short[1][0],
+        short[4][0],
+        short[5][0],
+        short[6][0],
+        short[2][0],
         grad_out_w,
     )
 

time: 188 us -> 172 us (0.915)
  the two profiles are of different devices: /device:TPU:0 before, /device:TPU:3 now
where the time goes in v3:
time: 172 us; the launch traced here: 171 us
  starting transfers between devices  65.8 us (38%)
  waiting for transfers between devices  54.3 us (32%)
  Pallas kernels  37.9 us (22%)
  local copies, waits for them, and re-layouts  6.78 us (4%)
  other arithmetic  5 us (3%)
    ppermute x44, starting transfers between devices, swap(): return lax.ppermute(x, axis, [(i, i ^ offset) for i in range(count)])  56 us
    ppermute x44, waiting for transfers between devices, swap(): return lax.ppermute(x, axis, [(i, i ^ offset) for i in range(count)])  50.4 us
    pallas_call x7, Pallas kernels, call(): pl.pallas_call(body, out_shape=[jax.ShapeDtypeStruct(shape, kind) for sha...  37.9 us
    ppermute x1, starting transfers between devices, on_device(): grad_out_w = lax.ppermute(own_out, ('dp', 'seq'), back_pairs)  5.04 us
    ppermute x1, starting transfers between devices, on_device(): out_block = lax.ppermute(out_weight, ('dp', 'seq'), to_heads)  4.74 us
  transfers between devices with their start and end apart: 46, of which 20 were waited for; matrix products, arithmetic and copies ran while one was open for 3% of the time, Pallas kernels for 5%

profile of v3, /device:TPU:3, one launch (start us, length us, event | category | flops | bytes accessed | tf_op | source)
XLA Modules:
  0.0 171.2 jit_solution(10152555533722238508)
XLA Ops:
  8.2 4.7 %collective-permute-start.6 = (bf16[48,768]{1,0:T(8,128)(2,1)}, bf16[48,768]{1,0:T(8,128)(2,1)S(1)}, u32[]{:S(2)}, u32[]{:S(2)}) collective-permute-start(bf16[48,768]{1,0:T(8,128)(2,1)} %param.22), channel_id=1, source_target_pairs={{0,0},{1,4},{2,8},{3,12},{4,16},{5,20},{6,24},{7,28},{8,1},{9,5},{... | collective-permute-start | bytes 221192 | tf_op jit(solution)/shard_map/ppermute | solution.py:706
  14.0 2.4 %collective-permute-start.17 = (bf16[96,768]{1,0:T(8,128)(2,1)S(1)}, bf16[96,768]{1,0:T(8,128)(2,1)S(1)}, u32[]{:S(2)}, u32[]{:S(2)}) collective-permute-start(bf16[96,768]{1,0:T(8,128)(2,1)S(1)} %slice.105.refs_4_), channel_id=1, source_target_pairs={{0,4},{4,0},{8,12},{12,8},{16,20},{20,16},{24,28},{28,24},{1,5},{5... | collective-permute-start | bytes 442376 | tf_op jit(solution)/shard_map/ppermute | solution.py:23
  23.1 4.9 %collective-permute-done.20.refs_8_ = bf16[96,768]{1,0:T(8,128)(2,1)S(1)} collective-permute-done((bf16[96,768]{1,0:T(8,128)(2,1)S(1)}, bf16[96,768]{1,0:T(8,128)(2,1)S(1)}, u32[]{:S(2)}, u32[]{:S(2)}) %collective-permute-start.20) | collective-permute-done | bytes 147488 | tf_op jit(solution)/shard_map/ppermute | solution.py:23
  28.0 3.5 %collective-permute-start.21 = (bf16[96,768]{1,0:T(8,128)(2,1)S(1)}, bf16[96,768]{1,0:T(8,128)(2,1)S(1)}, u32[]{:S(2)}, u32[]{:S(2)}) collective-permute-start(bf16[96,768]{1,0:T(8,128)(2,1)S(1)} %collective-permute-done.20.refs_8_), channel_id=1, source_target_pairs={{0,4},{4,0},{8,12},{12,8},{16,20},{20,16},{24,28},{28,24},{1,5},{5... | collective-permute-start | bytes 442376 | tf_op jit(solution)/shard_map/ppermute | solution.py:23
  33.8 4.9 %collective-permute-start = (bf16[128,768]{1,0:T(8,128)(2,1)S(1)}, bf16[128,768]{1,0:T(8,128)(2,1)S(1)}, u32[]{:S(2)}, u32[]{:S(2)}) collective-permute-start(bf16[128,768]{1,0:T(8,128)(2,1)S(1)} %bitcast.129), channel_id=1, source_target_pairs={{0,1},{1,0},{2,3},{3,2},{4,5},{5,4},{6,7},{7,6},{8,9},{9,8},{10,11... | collective-permute-start | bytes 589832 | tf_op jit(solution)/shard_map/ppermute | solution.py:23
  39.5 3.3 %collective-permute-done.23.refs_11_ = bf16[96,768]{1,0:T(8,128)(2,1)S(1)} collective-permute-done((bf16[96,768]{1,0:T(8,128)(2,1)S(1)}, bf16[96,768]{1,0:T(8,128)(2,1)S(1)}, u32[]{:S(2)}, u32[]{:S(2)}) %collective-permute-start.23) | collective-permute-done | bytes 147488 | tf_op jit(solution)/shard_map/ppermute | solution.py:23
  46.0 2.4 %collective-permute-start.10 = (bf16[96,768]{1,0:T(8,128)(2,1)S(1)}, bf16[96,768]{1,0:T(8,128)(2,1)S(1)}, u32[]{:S(2)}, u32[]{:S(2)}) collective-permute-start(bf16[96,768]{1,0:T(8,128)(2,1)S(1)} %maximum_maximum_fusion.refs_4_.refs_12_), channel_id=1, source_target_pairs={{0,16},{4,20},{8,24},{12,28},{16,0},{20,4},{24,8},{28,12},{1,17},{... | collective-permute-start | bytes 442376 | tf_op jit(solution)/shard_map/ppermute | solution.py:23
  48.6 4.1 %collective-permute-start.2 = (bf16[128,768]{1,0:T(8,128)(2,1)S(1)}, bf16[128,768]{1,0:T(8,128)(2,1)S(1)}, u32[]{:S(2)}, u32[]{:S(2)}) collective-permute-start(bf16[128,768]{1,0:T(8,128)(2,1)S(1)} %bitcast.131), channel_id=1, source_target_pairs={{0,3},{1,2},{2,1},{3,0},{4,7},{5,6},{6,5},{7,4},{8,11},{9,10},{10,... | collective-permute-start | bytes 589832 | tf_op jit(solution)/shard_map/ppermute | solution.py:23
  54.3 3.5 %collective-permute-done.12.refs_10_.refs_18_ = bf16[96,768]{1,0:T(8,128)(2,1)S(1)} collective-permute-done((bf16[96,768]{1,0:T(8,128)(2,1)S(1)}, bf16[96,768]{1,0:T(8,128)(2,1)S(1)}, u32[]{:S(2)}, u32[]{:S(2)}) %collective-permute-start.12) | collective-permute-done | bytes 147488 | tf_op jit(solution)/shard_map/ppermute | solution.py:23
  59.1 7.2 %shard_map.204 = (bf16[512,768]{1,0:T(8,128)(2,1)}, f32[512,768]{1,0:T(8,128)}, f32[512,640]{1,0:T(8,128)}, f32[512,384]{1,0:T(8,128)}) custom-call(bf16[128,768]{1,0:T(8,128)(2,1)} %bitcast.125, bf16[128,768]{1,0:T(8,128)(2,1)} %copy-done.12, bf16[128,768]{1,0:T(8,128)(2,1)} %copy-done.13, bf16[128,768]{1,0:T(8,128)(2,1)} %copy-done.14, ...), custom_call_target="tpu_custom_call" | custom-call | tf_op jit(solution)/shard_map/pallas_call | solution.py:645
  67.8 4.1 %shard_map.205 = (f32[512,384]{1,0:T(8,128)}, f32[512,384]{1,0:T(8,128)}, f32[4,8,128]{2,1,0:T(8,128)}) custom-call(bf16[128,768]{1,0:T(8,128)(2,1)} %bitcast.127, bf16[128,768]{1,0:T(8,128)(2,1)} %copy-done.15, bf16[128,768]{1,0:T(8,128)(2,1)} %copy-done.16, bf16[128,768]{1,0:T(8,128)(2,1)} %copy-done.17, bf16[96,768]{1,0:T(8,128)(2,1)} %copy-done.1, ...), custom_call_target="tpu_custom_call" | custom-call | tf_op jit(solution)/shard_map/pallas_call | solution.py:645
  71.8 4.9 %collective-permute-start.24 = (f32[4,8,128]{2,1,0:T(8,128)}, f32[4,8,128]{2,1,0:T(8,128)S(1)}, u32[]{:S(2)}, u32[]{:S(2)}) collective-permute-start(f32[4,8,128]{2,1,0:T(8,128)} %get-tuple-element.56.refs_12_), channel_id=1, source_target_pairs={{0,1},{1,0},{2,3},{3,2},{4,5},{5,4},{6,7},{7,6},{8,9},{9,8},{10,11... | collective-permute-start | bytes 49160 | tf_op jit(solution)/shard_map/ppermute | solution.py:23
  82.1 5.8 %shard_map.206 = (bf16[128,768]{1,0:T(8,128)(2,1)}, bf16[128,768]{1,0:T(8,128)(2,1)}, bf16[128,768]{1,0:T(8,128)(2,1)}, bf16[128,768]{1,0:T(8,128)(2,1)}, bf16[4...) custom-call(bf16[128,768]{1,0:T(8,128)(2,1)} %bitcast.128, ...), custom_call_target="tpu_custom_call" | custom-call | tf_op jit(solution)/shard_map/pallas_call | solution.py:645
  87.8 10.9 %shard_map.207 = (bf16[512,640]{1,0:T(8,128)(2,1)}, bf16[512,128]{1,0:T(8,128)(2,1)}, f32[8,640]{1,0:T(8,128)}, f32[8,128]{1,0:T(8,128)}) custom-call(f32[8,640]{1,0:T(8,128)} %fusion.23.refs_12_.conv_ref, s32[1,512]{1,0:T(1,128)} %seg_ref.1, f32[1,24]{1,0:T(1,128)} %bitcast.144, f32[1,24]{1,0:T(1,128)} %bitcast.146, f32[1,24]{1,0:T(1,128)} %bitcast.148, ...), custom_call_target="tpu_custom_call" | custom-call | tf_op jit(solution)/shard_map/pallas_call | solution.py:645
  99.4 6.5 %shard_map.208 = (bf16[4,96,768]{2,1,0:T(8,128)(2,1)}, bf16[4,96,768]{2,1,0:T(8,128)(2,1)}, bf16[128,768]{1,0:T(8,128)(2,1)}, bf16[128,768]{1,0:T(8,128)(2,1)}, ...) custom-call(bf16[128,768]{1,0:T(8,128)(2,1)} %bitcast.126, bf16[128,768]{1,0:T(8,128)(2,1)} %copy-done.12, ...), custom_call_target="tpu_custom_call" | custom-call | tf_op jit(solution)/shard_map/pallas_call | solution.py:645
  113.2 3.6 %collective-permute-done.32 = bf16[128,768]{1,0:T(8,128)(2,1)S(1)} collective-permute-done((bf16[128,768]{1,0:T(8,128)(2,1)}, bf16[128,768]{1,0:T(8,128)(2,1)S(1)}, u32[]{:S(2)}, u32[]{:S(2)}) %collective-permute-start.32) | collective-permute-done | bytes 196640 | tf_op jit(solution)/shard_map/ppermute | solution.py:23
  117.3 3.7 %collective-permute-done.31 = bf16[128,768]{1,0:T(8,128)(2,1)S(1)} collective-permute-done((bf16[128,768]{1,0:T(8,128)(2,1)}, bf16[128,768]{1,0:T(8,128)(2,1)S(1)}, u32[]{:S(2)}, u32[]{:S(2)}) %collective-permute-start.31) | collective-permute-done | bytes 196640 | tf_op jit(solution)/shard_map/ppermute | solution.py:23
  122.6 3.7 %collective-permute-done.38 = bf16[4,96,768]{2,1,0:T(8,128)(2,1)S(1)} collective-permute-done((bf16[4,96,768]{2,1,0:T(8,128)(2,1)S(1)}, bf16[4,96,768]{2,1,0:T(8,128)(2,1)S(1)}, u32[]{:S(2)}, u32[]{:S(2)}) %collective-permute-start.38) | collective-permute-done | bytes 589856 | tf_op jit(solution)/shard_map/ppermute | solution.py:23
  128.6 10.4 %collective-permute-done.33 = bf16[4,96,768]{2,1,0:T(8,128)(2,1)S(1)} collective-permute-done((bf16[4,96,768]{2,1,0:T(8,128)(2,1)}, bf16[4,96,768]{2,1,0:T(8,128)(2,1)S(1)}, u32[]{:S(2)}, u32[]{:S(2)}) %collective-permute-start.33) | collective-permute-done | bytes 589856 | tf_op jit(solution)/shard_map/ppermute | solution.py:23
  144.2 2.8 %collective-permute-done.37 = bf16[96,768]{1,0:T(8,128)(2,1)S(1)} collective-permute-done((bf16[96,768]{1,0:T(8,128)(2,1)S(1)}, bf16[96,768]{1,0:T(8,128)(2,1)S(1)}, u32[]{:S(2)}, u32[]{:S(2)}) %collective-permute-start.37) | collective-permute-done | bytes 147488 | tf_op jit(solution)/shard_map/ppermute | solution.py:23
  147.0 5.3 %collective-permute-start.27 = (bf16[128,768]{1,0:T(8,128)(2,1)S(1)}, bf16[128,768]{1,0:T(8,128)(2,1)S(1)}, u32[]{:S(2)}, u32[]{:S(2)}) collective-permute-start(bf16[128,768]{1,0:T(8,128)(2,1)S(1)} %copy-done.39), channel_id=1, source_target_pairs={{0,1},{1,0},{2,3},{3,2},{4,5},{5,4},{6,7},{7,6},{8,9},{9,8},{10,11... | collective-permute-start | bytes 589832 | tf_op jit(solution)/shard_map/ppermute | solution.py:23
  155.0 2.3 %collective-permute-start.42 = (bf16[24,1152]{1,0:T(8,128)(2,1)S(1)}, bf16[24,1152]{1,0:T(8,128)(2,1)S(1)}, u32[]{:S(2)}, u32[]{:S(2)}) collective-permute-start(bf16[24,1152]{1,0:T(8,128)(2,1)S(1)} %get-tuple-element.101), channel_id=1, source_target_pairs={{0,1},{1,0},{2,3},{3,2},{4,5},{5,4},{6,7},{7,6},{8,9},{9,8},{10,11... | collective-permute-start | bytes 165896 | tf_op jit(solution)/shard_map/ppermute | solution.py:23
  159.2 5.0 %collective-permute-start.45 = (f32[48,768]{1,0:T(8,128)S(1)}, f32[48,768]{1,0:T(8,128)S(1)}, u32[]{:S(2)}, u32[]{:S(2)}) collective-permute-start(f32[48,768]{1,0:T(8,128)S(1)} %pad_maximum_fusion.3), channel_id=1, source_target_pairs={{0,0},{4,1},{8,2},{12,3},{16,4},{20,5},{24,6},{28,7},{1,8},{5,9},{... | collective-permute-start | bytes 442376 | tf_op jit(solution)/shard_map/ppermute | solution.py:863
  167.7 2.8 %collective-permute-done.45 = f32[48,768]{1,0:T(8,128)S(1)} collective-permute-done((f32[48,768]{1,0:T(8,128)S(1)}, f32[48,768]{1,0:T(8,128)S(1)}, u32[]{:S(2)}, u32[]{:S(2)}) %collective-permute-start.45) | collective-permute-done | bytes 147488 | tf_op jit(solution)/shard_map/ppermute | solution.py:863
  (229 shorter events, 57.2 us)
Async XLA Ops:
  4.5 39.6 %collective-permute-start.14 = (bf16[128,768]{1,0:T(8,128)(2,1)}, bf16[128,768]{1,0:T(8,128)(2,1)S(1)}, u32[]{:S(2)}, u32[]{:S(2)}) collective-permute-start(bf16[128,768]{1,0:T(8,128)(2,1)} %bitcast.122), channel_id=1, source_target_pairs={{0,1},{1,0},{2,3},{3,2},{4,5},{5,4},{6,7},{7,6},{8,9},{9,8},{10,11... | collective-permute-start | bytes 589832 | tf_op jit(solution)/shard_map/ppermute | solution.py:23
  4.9 41.1 %collective-permute-start.15 = (bf16[128,768]{1,0:T(8,128)(2,1)}, bf16[128,768]{1,0:T(8,128)(2,1)S(1)}, u32[]{:S(2)}, u32[]{:S(2)}) collective-permute-start(bf16[128,768]{1,0:T(8,128)(2,1)} %bitcast.123), channel_id=1, source_target_pairs={{0,2},{1,3},{2,0},{3,1},{4,6},{5,7},{6,4},{7,5},{8,10},{9,11},{10,... | collective-permute-start | bytes 589832 | tf_op jit(solution)/shard_map/ppermute | solution.py:23
  7.0 41.3 %collective-permute-start.16 = (bf16[128,768]{1,0:T(8,128)(2,1)}, bf16[128,768]{1,0:T(8,128)(2,1)S(1)}, u32[]{:S(2)}, u32[]{:S(2)}) collective-permute-start(bf16[128,768]{1,0:T(8,128)(2,1)} %bitcast.124), channel_id=1, source_target_pairs={{0,3},{1,2},{2,1},{3,0},{4,7},{5,6},{6,5},{7,4},{8,11},{9,10},{10,... | collective-permute-start | bytes 589832 | tf_op jit(solution)/shard_map/ppermute | solution.py:23
  28.0 10.7 %collective-permute-start.21 = (bf16[96,768]{1,0:T(8,128)(2,1)S(1)}, bf16[96,768]{1,0:T(8,128)(2,1)S(1)}, u32[]{:S(2)}, u32[]{:S(2)}) collective-permute-start(bf16[96,768]{1,0:T(8,128)(2,1)S(1)} %collective-permute-done.20.refs_8_), channel_id=1, source_target_pairs={{0,4},{4,0},{8,12},{12,8},{16,20},{20,16},{24,28},{28,24},{1,5},{5... | collective-permute-start | bytes 442376 | tf_op jit(solution)/shard_map/ppermute | solution.py:23
  33.8 14.7 %collective-permute-start = (bf16[128,768]{1,0:T(8,128)(2,1)S(1)}, bf16[128,768]{1,0:T(8,128)(2,1)S(1)}, u32[]{:S(2)}, u32[]{:S(2)}) collective-permute-start(bf16[128,768]{1,0:T(8,128)(2,1)S(1)} %bitcast.129), channel_id=1, source_target_pairs={{0,1},{1,0},{2,3},{3,2},{4,5},{5,4},{6,7},{7,6},{8,9},{9,8},{10,11... | collective-permute-start | bytes 589832 | tf_op jit(solution)/shard_map/ppermute | solution.py:23
  42.8 9.9 %collective-permute-start.1 = (bf16[128,768]{1,0:T(8,128)(2,1)S(1)}, bf16[128,768]{1,0:T(8,128)(2,1)S(1)}, u32[]{:S(2)}, u32[]{:S(2)}) collective-permute-start(bf16[128,768]{1,0:T(8,128)(2,1)S(1)} %bitcast.130), channel_id=1, source_target_pairs={{0,2},{1,3},{2,0},{3,1},{4,6},{5,7},{6,4},{7,5},{8,10},{9,11},{10,... | collective-permute-start | bytes 589832 | tf_op jit(solution)/shard_map/ppermute | solution.py:23
  48.4 9.4 %collective-permute-start.12 = (bf16[96,768]{1,0:T(8,128)(2,1)S(1)}, bf16[96,768]{1,0:T(8,128)(2,1)S(1)}, u32[]{:S(2)}, u32[]{:S(2)}) collective-permute-start(bf16[96,768]{1,0:T(8,128)(2,1)S(1)} %maximum_maximum_fusion.refs_4_.refs_12_), channel_id=1, source_target_pairs={{0,24},{4,28},{8,16},{12,20},{16,8},{20,12},{24,0},{28,4},{1,25},{... | collective-permute-start | bytes 442376 | tf_op jit(solution)/shard_map/ppermute | solution.py:23
  48.6 18.3 %collective-permute-start.2 = (bf16[128,768]{1,0:T(8,128)(2,1)S(1)}, bf16[128,768]{1,0:T(8,128)(2,1)S(1)}, u32[]{:S(2)}, u32[]{:S(2)}) collective-permute-start(bf16[128,768]{1,0:T(8,128)(2,1)S(1)} %bitcast.131), channel_id=1, source_target_pairs={{0,3},{1,2},{2,1},{3,0},{4,7},{5,6},{6,5},{7,4},{8,11},{9,10},{10,... | collective-permute-start | bytes 589832 | tf_op jit(solution)/shard_map/ppermute | solution.py:23
  52.6 14.2 %collective-permute-start.7 = (bf16[96,768]{1,0:T(8,128)(2,1)S(1)}, bf16[96,768]{1,0:T(8,128)(2,1)S(1)}, u32[]{:S(2)}, u32[]{:S(2)}) collective-permute-start(bf16[96,768]{1,0:T(8,128)(2,1)S(1)} %maximum_maximum_fusion.refs_4_.refs_12_), channel_id=1, source_target_pairs={{0,4},{4,0},{8,12},{12,8},{16,20},{20,16},{24,28},{28,24},{1,5},{5... | collective-permute-start | bytes 442376 | tf_op jit(solution)/shard_map/ppermute | solution.py:23
  52.7 14.1 %collective-permute-start.9 = (bf16[96,768]{1,0:T(8,128)(2,1)S(1)}, bf16[96,768]{1,0:T(8,128)(2,1)S(1)}, u32[]{:S(2)}, u32[]{:S(2)}) collective-permute-start(bf16[96,768]{1,0:T(8,128)(2,1)S(1)} %collective-permute-done.8.refs_6_.refs_14_), channel_id=1, source_target_pairs={{0,4},{4,0},{8,12},{12,8},{16,20},{20,16},{24,28},{28,24},{1,5},{5... | collective-permute-start | bytes 442376 | tf_op jit(solution)/shard_map/ppermute | solution.py:23
  54.2 12.7 %collective-permute-start.11 = (bf16[96,768]{1,0:T(8,128)(2,1)S(1)}, bf16[96,768]{1,0:T(8,128)(2,1)S(1)}, u32[]{:S(2)}, u32[]{:S(2)}) collective-permute-start(bf16[96,768]{1,0:T(8,128)(2,1)S(1)} %collective-permute-done.10.refs_8_.refs_16_), channel_id=1, source_target_pairs={{0,4},{4,0},{8,12},{12,8},{16,20},{20,16},{24,28},{28,24},{1,5},{5... | collective-permute-start | bytes 442376 | tf_op jit(solution)/shard_map/ppermute | solution.py:23
  110.1 10.9 %collective-permute-start.31 = (bf16[128,768]{1,0:T(8,128)(2,1)}, bf16[128,768]{1,0:T(8,128)(2,1)S(1)}, u32[]{:S(2)}, u32[]{:S(2)}) collective-permute-start(bf16[128,768]{1,0:T(8,128)(2,1)} %get-tuple-element.71), channel_id=1, source_target_pairs={{0,2},{1,3},{2,0},{3,1},{4,6},{5,7},{6,4},{7,5},{8,10},{9,11},{10,... | collective-permute-start | bytes 589832 | tf_op jit(solution)/shard_map/ppermute | solution.py:23
  111.2 11.2 %collective-permute-start.30 = (bf16[128,768]{1,0:T(8,128)(2,1)}, bf16[128,768]{1,0:T(8,128)(2,1)S(1)}, u32[]{:S(2)}, u32[]{:S(2)}) collective-permute-start(bf16[128,768]{1,0:T(8,128)(2,1)} %get-tuple-element.70), channel_id=1, source_target_pairs={{0,1},{1,0},{2,3},{3,2},{4,5},{5,4},{6,7},{7,6},{8,9},{9,8},{10,11... | collective-permute-start | bytes 589832 | tf_op jit(solution)/shard_map/ppermute | solution.py:23
  111.4 47.3 %collective-permute-start.29 = (bf16[128,768]{1,0:T(8,128)(2,1)S(1)}, bf16[128,768]{1,0:T(8,128)(2,1)S(1)}, u32[]{:S(2)}, u32[]{:S(2)}) collective-permute-start(bf16[128,768]{1,0:T(8,128)(2,1)S(1)} %copy-done.41), channel_id=1, source_target_pairs={{0,3},{1,2},{2,1},{3,0},{4,7},{5,6},{6,5},{7,4},{8,11},{9,10},{10,... | collective-permute-start | bytes 589832 | tf_op jit(solution)/shard_map/ppermute | solution.py:23
  112.7 13.7 %collective-permute-start.38 = (bf16[4,96,768]{2,1,0:T(8,128)(2,1)S(1)}, bf16[4,96,768]{2,1,0:T(8,128)(2,1)S(1)}, u32[]{:S(2)}, u32[]{:S(2)}) collective-permute-start(bf16[4,96,768]{2,1,0:T(8,128)(2,1)S(1)} %copy-done.38), channel_id=1, source_target_pairs={{0,4},{4,0},{8,12},{12,8},{16,20},{20,16},{24,28},{28,24},{1,5},{5... | collective-permute-start | bytes 1769480 | tf_op jit(solution)/shard_map/ppermute | solution.py:23
  116.8 42.4 %collective-permute-start.28 = (bf16[128,768]{1,0:T(8,128)(2,1)S(1)}, bf16[128,768]{1,0:T(8,128)(2,1)S(1)}, u32[]{:S(2)}, u32[]{:S(2)}) collective-permute-start(bf16[128,768]{1,0:T(8,128)(2,1)S(1)} %copy-done.40), channel_id=1, source_target_pairs={{0,2},{1,3},{2,0},{3,1},{4,6},{5,7},{6,4},{7,5},{8,10},{9,11},{10,... | collective-permute-start | bytes 589832 | tf_op jit(solution)/shard_map/ppermute | solution.py:23
  121.0 18.0 %collective-permute-start.33 = (bf16[4,96,768]{2,1,0:T(8,128)(2,1)}, bf16[4,96,768]{2,1,0:T(8,128)(2,1)S(1)}, u32[]{:S(2)}, u32[]{:S(2)}) collective-permute-start(bf16[4,96,768]{2,1,0:T(8,128)(2,1)} %get-tuple-element.74), channel_id=1, source_target_pairs={{0,4},{4,0},{8,12},{12,8},{16,20},{20,16},{24,28},{28,24},{1,5},{5... | collective-permute-start | bytes 1769480 | tf_op jit(solution)/shard_map/ppermute | solution.py:23
  126.5 13.5 %collective-permute-start.41 = (bf16[96,768]{1,0:T(8,128)(2,1)S(1)}, bf16[96,768]{1,0:T(8,128)(2,1)S(1)}, u32[]{:S(2)}, u32[]{:S(2)}) collective-permute-start(bf16[96,768]{1,0:T(8,128)(2,1)S(1)} %get-tuple-element.95), channel_id=1, source_target_pairs={{0,24},{4,28},{8,16},{12,20},{16,8},{20,12},{24,0},{28,4},{1,25},{... | collective-permute-start | bytes 442376 | tf_op jit(solution)/shard_map/ppermute | solution.py:23
  128.4 13.9 %collective-permute-start.40 = (bf16[96,768]{1,0:T(8,128)(2,1)S(1)}, bf16[96,768]{1,0:T(8,128)(2,1)S(1)}, u32[]{:S(2)}, u32[]{:S(2)}) collective-permute-start(bf16[96,768]{1,0:T(8,128)(2,1)S(1)} %get-tuple-element.96), channel_id=1, source_target_pairs={{0,16},{4,20},{8,24},{12,28},{16,0},{20,4},{24,8},{28,12},{1,17},{... | collective-permute-start | bytes 442376 | tf_op jit(solution)/shard_map/ppermute | solution.py:23
  142.3 11.9 %collective-permute-start.36 = (bf16[96,768]{1,0:T(8,128)(2,1)S(1)}, bf16[96,768]{1,0:T(8,128)(2,1)S(1)}, u32[]{:S(2)}, u32[]{:S(2)}) collective-permute-start(bf16[96,768]{1,0:T(8,128)(2,1)S(1)} %get-tuple-element.93), channel_id=1, source_target_pairs={{0,16},{4,20},{8,24},{12,28},{16,0},{20,4},{24,8},{28,12},{1,17},{... | collective-permute-start | bytes 442376 | tf_op jit(solution)/shard_map/ppermute | solution.py:23
  143.7 10.5 %collective-permute-start.35 = (bf16[96,768]{1,0:T(8,128)(2,1)S(1)}, bf16[96,768]{1,0:T(8,128)(2,1)S(1)}, u32[]{:S(2)}, u32[]{:S(2)}) collective-permute-start(bf16[96,768]{1,0:T(8,128)(2,1)S(1)} %get-tuple-element.91), channel_id=1, source_target_pairs={{0,8},{4,12},{8,0},{12,4},{16,24},{20,28},{24,16},{28,20},{1,9},{5... | collective-permute-start | bytes 442376 | tf_op jit(solution)/shard_map/ppermute | solution.py:23
  147.0 17.2 %collective-permute-start.27 = (bf16[128,768]{1,0:T(8,128)(2,1)S(1)}, bf16[128,768]{1,0:T(8,128)(2,1)S(1)}, u32[]{:S(2)}, u32[]{:S(2)}) collective-permute-start(bf16[128,768]{1,0:T(8,128)(2,1)S(1)} %copy-done.39), channel_id=1, source_target_pairs={{0,1},{1,0},{2,3},{3,2},{4,5},{5,4},{6,7},{7,6},{8,9},{9,8},{10,11... | collective-permute-start | bytes 589832 | tf_op jit(solution)/shard_map/ppermute | solution.py:23
  155.0 10.3 %collective-permute-start.42 = (bf16[24,1152]{1,0:T(8,128)(2,1)S(1)}, bf16[24,1152]{1,0:T(8,128)(2,1)S(1)}, u32[]{:S(2)}, u32[]{:S(2)}) collective-permute-start(bf16[24,1152]{1,0:T(8,128)(2,1)S(1)} %get-tuple-element.101), channel_id=1, source_target_pairs={{0,1},{1,0},{2,3},{3,2},{4,5},{5,4},{6,7},{7,6},{8,9},{9,8},{10,11... | collective-permute-start | bytes 165896 | tf_op jit(solution)/shard_map/ppermute | solution.py:23
  159.2 11.4 %collective-permute-start.45 = (f32[48,768]{1,0:T(8,128)S(1)}, f32[48,768]{1,0:T(8,128)S(1)}, u32[]{:S(2)}, u32[]{:S(2)}) collective-permute-start(f32[48,768]{1,0:T(8,128)S(1)} %pad_maximum_fusion.3), channel_id=1, source_target_pairs={{0,0},{4,1},{8,2},{12,3},{16,4},{20,5},{24,6},{28,7},{1,8},{5,9},{... | collective-permute-start | bytes 442376 | tf_op jit(solution)/shard_map/ppermute | solution.py:863
  (64 other events, 701.1 us)

commit v4 on v3

--- a/solution.py
+++ b/solution.py
@@ -259,9 +259,9 @@
     return [(i % group, (i // group) * max(lengths)) for i in range(len(lengths))]
 
 
-def store_slabs(values, outs):
+def store_slabs(values, outs, lanes):
     if len(outs[0].shape) == 2:
-        outs[0][...] = values[...].astype(BF16)
+        outs[0][...] = values[:, lanes].astype(BF16)
         return
     inner, (outer, rows, _) = len(outs), outs[0].shape
     place = lax.axis_index("dp") % inner if inner > 1 else 0
@@ -270,14 +270,25 @@
             start = (o * inner + (place ^ j)) * rows
             if inner > 1:
                 start = pl.multiple_of(start, rows)
-            out[o] = values[pl.ds(start, rows), :].astype(BF16)
-
-
-def store_pieces(values, outs):
+            out[o] = values[pl.ds(start, rows), lanes].astype(BF16)
+
+
+def store_far(values, outs):
+    if len(outs) == 1:
+        outs[0][...] = values[...].astype(BF16)
+        return
     rows = outs[0].shape[0]
+    inner = inner_of(lax.axis_size("dp"))
+    for k, out in enumerate(outs):
+        start = pl.multiple_of(((lax.axis_index("dp") // inner) ^ k) * rows, rows)
+        out[...] = values[pl.ds(start, rows), :].astype(BF16)
+
+
+def store_pieces(values, outs, behind=0):
+    rows = outs[0].shape[0] - behind
     for k, out in enumerate(outs):
         start = pl.multiple_of((lax.axis_index("seq") ^ k) * rows, rows)
-        out[...] = values[pl.ds(start, rows), :].astype(BF16)
+        out[behind:, :] = values[pl.ds(start, rows), :].astype(BF16)
 
 
 def finish_kernel(width, inner, heads_here, lengths, spots):
@@ -483,7 +494,7 @@
         dgate = (dv * y * (sig * (1.0 + gate * (1.0 - sig)))).astype(BF16)
         dgate_ref[...] = dgate
         grad_all[:, :width] = dot(normed_ref[...], dgate, 0, 0)
-        store_slabs(grad_all, slabs)
+        store_far(grad_all, slabs)
 
     return body
 
@@ -617,6 +628,7 @@
         x_pieces, refs = refs[:x_count], refs[x_count:]
         w_pieces, refs = refs[:w_count], refs[w_count:]
         g_pieces, refs = refs[:w_count], refs[w_count:]
+        out_parts, refs = refs[:x_count], refs[x_count:]
         normed_ref, dconv_ref, draw_ref, dgate_ref = refs[:4]
         slabs, refs = refs[4 : 4 + slab_count], refs[4 + slab_count :]
         dn_refs, refs = refs[:x_count], refs[x_count:]
@@ -629,13 +641,17 @@
         dn = dot(dconv, w_ref[:, :channels], 1, 1) + dot(draw, w_ref[:, channels:], 1, 1)
         dn = dn + dot(dgate_ref[...], wg_ref[...], 1, 1)
         dn_all[...] = dn
-        store_pieces(dn_all, dn_refs)
+        store_pieces(dn_all, dn_refs, out_parts[0].shape[0])
+        for out_part, both_ref in zip(out_parts, dn_refs):
+            both_ref[: out_part.shape[0], :] = out_part[...]
         gin_ref[:, :channels] = dot(normed_ref[...], dconv, 0, 0)
         x = x_ref[...].astype(F32)
         along = jnp.sum(dn * (x * rms_inverse(x)), axis=0, keepdims=True)
         norm_grad_ref[...] = along
         gin_ref[:, channels:] = dot(normed_ref[...], draw, 0, 0)
-        store_slabs(gin_ref, slabs)
+        half = gin_ref.shape[1] // 2
+        store_slabs(gin_ref, slabs[: slab_count // 2], slice(0, half))
+        store_slabs(gin_ref, slabs[slab_count // 2 :], slice(half, 2 * half))
 
     return body
 
@@ -774,10 +790,14 @@
     stats = gather_xor(stats, "seq")
     block_rows = rows * seq_n
     dp_inner = inner_of(dp_n)
+    dp_outer = dp_n // dp_inner
+    half = cols // 2
     if split_here:
-        slabs = [((dp_n // dp_inner, block_rows, cols), BF16)] * dp_inner
+        halves = [((dp_outer, block_rows, half), BF16)] * dp_inner
+        far_blocks = [((dp_inner * block_rows, 2 * width), BF16)] * dp_outer
     else:
-        slabs = [((model, cols), BF16)]
+        halves = [((model, half), BF16)]
+        far_blocks = [((model, 2 * width), BF16)]
     pieces = [((piece, model), BF16)] * seq_n
 
     def near_sum(made):
@@ -785,22 +805,29 @@
             return reduce_slabs(made)
         return reduce_near(made[0].reshape(dp_n, -1, made[0].shape[-1]))
 
-    second_slabs = [((*shape[:-1], 2 * width), kind) for shape, kind in slabs]
+    def far_sum(made):
+        if not split_here:
+            outer_place = dp_place // dp_inner
+            blocks = made[0].reshape(dp_outer, dp_inner * block_rows, 2 * width)
+            made = [
+                lax.dynamic_index_in_dim(blocks, outer_place ^ k, 0, False)
+                for k in range(dp_outer)
+            ]
+        parts = [made[0]]
+        for k, offset in enumerate(far_offsets()):
+            parts.append(swap(made[k + 1], "dp", offset))
+        return tree_sum([p.astype(F32) for p in parts]).astype(BF16)
+
     made = call(
-        out_kernel(width, inner, len(og_pieces), len(w_second), len(slabs), block_rows),
-        pieces + second_slabs
+        out_kernel(width, inner, len(og_pieces), len(w_second), len(far_blocks), block_rows),
+        pieces + far_blocks
         + [((length, width), BF16), ((length, width), F32), ((8, width), F32)],
         [og_scratch, wo_scratch, (length, model), (model, 2 * width)],
         *og_pieces, *w_second, *stats, normed, gate, d_gated, y, gain_mine,
     )
     out_parts, made = made[:seq_n], made[seq_n:]
-    near_early = near_sum(made[: len(slabs)])
-    d_gate, dy, g_gain = made[len(slabs) :]
-    result = tree_sum(
-        [(swap(p, "seq", k) if k else p).astype(F32) for k, p in enumerate(out_parts)]
-    )
-    result = hidden_in[0].astype(F32) + result
-
+    far_early = far_sum(made[: len(far_blocks)])
+    d_gate, dy, g_gain = made[len(far_blocks) :]
     dconv, draw, conv_grad, head_grad = call(
         mixer_back_kernel(width),
         [((length, channels), BF16), ((length, LANES), BF16)]
@@ -812,14 +839,14 @@
     )
 
     made = call(
-        weight_back_kernel(len(x_pieces), len(w_first), len(slabs)),
-        slabs + pieces + [((1, model), F32)],
+        weight_back_kernel(len(x_pieces), len(w_first), 2 * len(halves)),
+        halves + halves + [((2 * piece, model), BF16)] * seq_n + [((1, model), F32)],
         [((length, model), BF16), ((model, cols), BF16), wg_scratch, (length, model), (model, cols)],
-        *x_pieces, *w_first, *w_second, normed, dconv, draw, d_gate,
-    )
-    dn_pieces, norm_grad = made[len(slabs) : -1], made[-1]
-    near_late = near_sum(made[: len(slabs)])
-    early = reduce_far(near_early)
+        *x_pieces, *w_first, *w_second, *out_parts, normed, dconv, draw, d_gate,
+    )
+    dn_pieces, norm_grad = made[2 * len(halves) : -1], made[-1]
+    near_values = near_sum(made[: len(halves)])
+    rest = made[len(halves) : 2 * len(halves)]
     conv_full = jnp.zeros((CONV + 1, inner), F32)
     conv_full = lax.dynamic_update_slice_in_dim(
         conv_full, conv_grad[: CONV + 1, :width], place * width, 1
@@ -852,19 +879,36 @@
         small,
         ((0, 0), (0, rows - group), (heads_here, LANES - heads_here - small.shape[2])),
     ).astype(BF16)
-    near_small = reduce_near(small.reshape(dp_n, -1, LANES))
-    near_late = near_late + jnp.pad(near_small, ((0, 0), (0, 0), (channels, 0)))
-    late = reduce_far(near_late)
+    inner_place = dp_place % dp_inner
+    small = small.reshape(dp_outer, dp_inner, block_rows, LANES)
+    far_early = far_early.reshape(dp_inner, block_rows, 2 * width)
+    if not split_here:
+        rest = rest[0].reshape(dp_outer, dp_inner, block_rows, half)
+        rest = [lax.dynamic_index_in_dim(rest, inner_place ^ j, 1, False) for j in range(dp_inner)]
+    together = []
+    for j, slab in enumerate(rest):
+        short = lax.dynamic_index_in_dim(small, inner_place ^ j, 1, False)
+        slab = slab + jnp.pad(short, ((0, 0), (0, 0), (half - LANES, 0)))
+        block = lax.dynamic_index_in_dim(far_early, inner_place ^ j, 0, False)
+        block = jnp.stack([block[:, :width], block[:, width:]])
+        together.append(jnp.concatenate([slab, block], 0))
+    together = [swap(t, "dp", j) if j else t for j, t in enumerate(together)]
+    together = tree_sum([t.astype(F32) for t in together])
+    near_rest = together[:dp_outer].astype(BF16)
+    early = jnp.concatenate([together[dp_outer], together[dp_outer + 1]], 1)
+    late = [reduce_far(near_values), reduce_far(near_rest)]
     own_out = early[:, width:]
     own_out = jnp.concatenate(
         [own_out[k * out_rows : (k + 1) * out_rows] for k in range(model // width)], 1
     )
     back_pairs = [(target, source) for source, target in to_heads]
-    grad_out_w = lax.ppermute(own_out, ("dp", "seq"), back_pairs)
+    grad_out_w = lax.ppermute(own_out.astype(BF16), ("dp", "seq"), back_pairs)
     dn_parts = [swap(p, "seq", k) if k else p for k, p in enumerate(dn_pieces)]
-    d_normed = tree_sum([p.astype(F32) for p in dn_parts])
-
-    both = jnp.concatenate([late, early[:, :width]], 1).reshape(seq_n, rows, cols + width)
+    rows_total = tree_sum([p.astype(F32) for p in dn_parts])
+    result = hidden_in[0].astype(F32) + rows_total[:piece]
+    d_normed = rows_total[piece:]
+
+    both = jnp.concatenate([*late, early[:, :width]], 1).reshape(seq_n, rows, cols + width)
     parts = scatter_xor(both.astype(BF16), "seq")
     short = [((CONV, conv_here), F32)] + [((1, n), F32) for n in lengths[CONV:]]
     grad_in_w, *short = call(
@@ -891,7 +935,7 @@
         short[5][0],
         short[6][0],
         short[2][0],
-        grad_out_w,
+        grad_out_w.astype(F32),
     )
 
 

time: 172 us -> 172 us (level)
  the two profiles are of different devices: /device:TPU:3 before, /device:TPU:0 now
where the time goes in v4:
time: 172 us
  waiting for transfers between devices  62.7 us (36%)
  starting transfers between devices  55.1 us (32%)
  Pallas kernels  38.3 us (22%)
  local copies, waits for them, and re-layouts  7.46 us (4%)
  other arithmetic  6.68 us (4%)
    ppermute x43, waiting for transfers between devices, swap(): return lax.ppermute(x, axis, [(i, i ^ offset) for i in range(count)])  62.7 us
    ppermute x43, starting transfers between devices, swap(): return lax.ppermute(x, axis, [(i, i ^ offset) for i in range(count)])  52.9 us
    pallas_call x7, Pallas kernels, call(): pl.pallas_call(body, out_shape=[jax.ShapeDtypeStruct(shape, kind) for sha...  38.3 us
  transfers between devices with their start and end apart: 45, of which 19 were waited for; matrix products, arithmetic and copies ran while one was open for 4% of the time, Pallas kernels for 4%

profile of v4, /device:TPU:0, one launch (start us, length us, event | category | flops | bytes accessed | tf_op | source)
XLA Modules:
  0.0 171.7 jit_solution(18223585810269842380)
XLA Ops:
  2.9 2.5 %collective-permute-start.4 = (bf16[24,1152]{1,0:T(8,128)(2,1)}, bf16[24,1152]{1,0:T(8,128)(2,1)S(1)}, u32[]{:S(2)}, u32[]{:S(2)}) collective-permute-start(bf16[24,1152]{1,0:T(8,128)(2,1)} %get-tuple-element.56), channel_id=1, source_target_pairs={{0,2},{1,3},{2,0},{3,1},{4,6},{5,7},{6,4},{7,5},{8,10},{9,11},{10,... | collective-permute-start | bytes 165896 | tf_op jit(solution)/shard_map/ppermute | solution.py:23
  8.9 4.6 %collective-permute-start.2 = (bf16[128,768]{1,0:T(8,128)(2,1)}, bf16[128,768]{1,0:T(8,128)(2,1)S(1)}, u32[]{:S(2)}, u32[]{:S(2)}) collective-permute-start(bf16[128,768]{1,0:T(8,128)(2,1)} %bitcast.138), channel_id=1, source_target_pairs={{0,3},{1,2},{2,1},{3,0},{4,7},{5,6},{6,5},{7,4},{8,11},{9,10},{10,... | collective-permute-start | bytes 589832 | tf_op jit(solution)/shard_map/ppermute | solution.py:23
  14.6 2.6 %collective-permute-start.6 = (bf16[96,768]{1,0:T(8,128)(2,1)S(1)}, bf16[96,768]{1,0:T(8,128)(2,1)S(1)}, u32[]{:S(2)}, u32[]{:S(2)}) collective-permute-start(bf16[96,768]{1,0:T(8,128)(2,1)S(1)} %slice.141.refs_4_), channel_id=1, source_target_pairs={{0,4},{4,0},{8,12},{12,8},{16,20},{20,16},{24,28},{28,24},{1,5},{5... | collective-permute-start | bytes 442376 | tf_op jit(solution)/shard_map/ppermute | solution.py:23
  17.3 4.3 %collective-permute-done.7.refs_6_ = bf16[96,768]{1,0:T(8,128)(2,1)S(1)} collective-permute-done((bf16[96,768]{1,0:T(8,128)(2,1)S(1)}, bf16[96,768]{1,0:T(8,128)(2,1)S(1)}, u32[]{:S(2)}, u32[]{:S(2)}) %collective-permute-start.7) | collective-permute-done | bytes 147488 | tf_op jit(solution)/shard_map/ppermute | solution.py:23
  21.6 3.5 %collective-permute-start.9 = (bf16[96,768]{1,0:T(8,128)(2,1)S(1)}, bf16[96,768]{1,0:T(8,128)(2,1)S(1)}, u32[]{:S(2)}, u32[]{:S(2)}) collective-permute-start(bf16[96,768]{1,0:T(8,128)(2,1)S(1)} %slice.141.refs_4_), channel_id=1, source_target_pairs={{0,16},{4,20},{8,24},{12,28},{16,0},{20,4},{24,8},{28,12},{1,17},{... | collective-permute-start | bytes 442376 | tf_op jit(solution)/shard_map/ppermute | solution.py:23
  25.1 6.3 %collective-permute-done.9.refs_8_ = bf16[96,768]{1,0:T(8,128)(2,1)S(1)} collective-permute-done((bf16[96,768]{1,0:T(8,128)(2,1)S(1)}, bf16[96,768]{1,0:T(8,128)(2,1)S(1)}, u32[]{:S(2)}, u32[]{:S(2)}) %collective-permute-start.9) | collective-permute-done | bytes 147488 | tf_op jit(solution)/shard_map/ppermute | solution.py:23
  34.9 4.0 %collective-permute-done.11.refs_10_ = bf16[96,768]{1,0:T(8,128)(2,1)S(1)} collective-permute-done((bf16[96,768]{1,0:T(8,128)(2,1)S(1)}, bf16[96,768]{1,0:T(8,128)(2,1)S(1)}, u32[]{:S(2)}, u32[]{:S(2)}) %collective-permute-start.11) | collective-permute-done | bytes 147488 | tf_op jit(solution)/shard_map/ppermute | solution.py:23
  40.5 3.7 %collective-permute-done.12.refs_11_ = bf16[96,768]{1,0:T(8,128)(2,1)S(1)} collective-permute-done((bf16[96,768]{1,0:T(8,128)(2,1)S(1)}, bf16[96,768]{1,0:T(8,128)(2,1)S(1)}, u32[]{:S(2)}, u32[]{:S(2)}) %collective-permute-start.12) | collective-permute-done | bytes 147488 | tf_op jit(solution)/shard_map/ppermute | solution.py:23
  46.7 2.4 %collective-permute-start.15 = (bf16[96,768]{1,0:T(8,128)(2,1)S(1)}, bf16[96,768]{1,0:T(8,128)(2,1)S(1)}, u32[]{:S(2)}, u32[]{:S(2)}) collective-permute-start(bf16[96,768]{1,0:T(8,128)(2,1)S(1)} %maximum_maximum_fusion.refs_4_.refs_12_), channel_id=1, source_target_pairs={{0,8},{4,12},{8,0},{12,4},{16,24},{20,28},{24,16},{28,20},{1,9},{5... | collective-permute-start | bytes 442376 | tf_op jit(solution)/shard_map/ppermute | solution.py:23
  50.9 2.5 %collective-permute-done.19.refs_10_.refs_18_ = bf16[96,768]{1,0:T(8,128)(2,1)S(1)} collective-permute-done((bf16[96,768]{1,0:T(8,128)(2,1)S(1)}, bf16[96,768]{1,0:T(8,128)(2,1)S(1)}, u32[]{:S(2)}, u32[]{:S(2)}) %collective-permute-start.19) | collective-permute-done | bytes 147488 | tf_op jit(solution)/shard_map/ppermute | solution.py:23
  54.8 5.3 %collective-permute-done.17.refs_8_.refs_16_ = bf16[96,768]{1,0:T(8,128)(2,1)S(1)} collective-permute-done((bf16[96,768]{1,0:T(8,128)(2,1)S(1)}, bf16[96,768]{1,0:T(8,128)(2,1)S(1)}, u32[]{:S(2)}, u32[]{:S(2)}) %collective-permute-start.17) | collective-permute-done | bytes 147488 | tf_op jit(solution)/shard_map/ppermute | solution.py:23
  62.9 7.2 %shard_map.204 = (bf16[512,768]{1,0:T(8,128)(2,1)}, f32[512,768]{1,0:T(8,128)}, f32[512,640]{1,0:T(8,128)}, f32[512,384]{1,0:T(8,128)}) custom-call(bf16[128,768]{1,0:T(8,128)(2,1)} %bitcast.139, bf16[128,768]{1,0:T(8,128)(2,1)} %copy-done.17, bf16[128,768]{1,0:T(8,128)(2,1)} %copy-done.16, bf16[128,768]{1,0:T(8,128)(2,1)} %copy-done.15, ...), custom_call_target="tpu_custom_call" | custom-call | tf_op jit(solution)/shard_map/pallas_call | solution.py:661
  71.5 4.1 %shard_map.205 = (f32[512,384]{1,0:T(8,128)}, f32[512,384]{1,0:T(8,128)}, f32[4,8,128]{2,1,0:T(8,128)}) custom-call(bf16[128,768]{1,0:T(8,128)(2,1)} %bitcast.145, bf16[128,768]{1,0:T(8,128)(2,1)} %copy-done.18, bf16[128,768]{1,0:T(8,128)(2,1)} %copy-done.14, bf16[128,768]{1,0:T(8,128)(2,1)} %copy-done.13, bf16[96,768]{1,0:T(8,128)(2,1)} %copy-done.2, ...), custom_call_target="tpu_custom_call" | custom-call | tf_op jit(solution)/shard_map/pallas_call | solution.py:661
  79.1 2.3 %collective-permute-done.25.refs_14_ = f32[4,8,128]{2,1,0:T(8,128)S(1)} collective-permute-done((f32[4,8,128]{2,1,0:T(8,128)}, f32[4,8,128]{2,1,0:T(8,128)S(1)}, u32[]{:S(2)}, u32[]{:S(2)}) %collective-permute-start.25) | collective-permute-done | bytes 16416 | tf_op jit(solution)/shard_map/ppermute | solution.py:23
  82.0 5.6 %shard_map.206 = (bf16[128,768]{1,0:T(8,128)(2,1)}, bf16[128,768]{1,0:T(8,128)(2,1)}, bf16[128,768]{1,0:T(8,128)(2,1)}, bf16[128,768]{1,0:T(8,128)(2,1)}, bf16[1...) custom-call(bf16[128,768]{1,0:T(8,128)(2,1)} %bitcast.146, ...), custom_call_target="tpu_custom_call" | custom-call | tf_op jit(solution)/shard_map/pallas_call | solution.py:661
  87.6 10.9 %shard_map.207 = (bf16[512,640]{1,0:T(8,128)(2,1)}, bf16[512,128]{1,0:T(8,128)(2,1)}, f32[8,640]{1,0:T(8,128)}, f32[8,128]{1,0:T(8,128)}) custom-call(f32[8,640]{1,0:T(8,128)} %fusion.22.refs_12_.conv_ref, s32[1,512]{1,0:T(1,128)} %seg_ref.1, f32[1,24]{1,0:T(1,128)} %bitcast.162, f32[1,24]{1,0:T(1,128)} %bitcast.164, f32[1,24]{1,0:T(1,128)} %bitcast.166, ...), custom_call_target="tpu_custom_call" | custom-call | tf_op jit(solution)/shard_map/pallas_call | solution.py:661
  101.4 6.9 %shard_map.208 = (bf16[4,96,384]{2,1,0:T(8,128)(2,1)}, bf16[4,96,384]{2,1,0:T(8,128)(2,1)}, bf16[4,96,384]{2,1,0:T(8,128)(2,1)}, bf16[4,96,384]{2,1,0:T(8,128)(2...) custom-call(bf16[128,768]{1,0:T(8,128)(2,1)} %bitcast.140, ...), custom_call_target="tpu_custom_call" | custom-call | tf_op jit(solution)/shard_map/pallas_call | solution.py:661
  110.9 2.6 %collective-permute-start.35 = (bf16[192,768]{1,0:T(8,128)(2,1)S(1)}, bf16[192,768]{1,0:T(8,128)(2,1)S(1)}, u32[]{:S(2)}, u32[]{:S(2)}) collective-permute-start(bf16[192,768]{1,0:T(8,128)(2,1)S(1)} %copy-done.41), channel_id=1, source_target_pairs={{0,16},{4,20},{8,24},{12,28},{16,0},{20,4},{24,8},{28,12},{1,17},{... | collective-permute-start | bytes 884744 | tf_op jit(solution)/shard_map/ppermute | solution.py:23
  116.4 3.2 %collective-permute-done.30 = bf16[4,96,384]{2,1,0:T(8,128)(2,1)S(1)} collective-permute-done((bf16[4,96,384]{2,1,0:T(8,128)(2,1)}, bf16[4,96,384]{2,1,0:T(8,128)(2,1)S(1)}, u32[]{:S(2)}, u32[]{:S(2)}) %collective-permute-start.30) | collective-permute-done | bytes 294944 | tf_op jit(solution)/shard_map/ppermute | solution.py:23
  120.1 5.4 %collective-permute-done.34 = bf16[192,768]{1,0:T(8,128)(2,1)S(1)} collective-permute-done((bf16[192,768]{1,0:T(8,128)(2,1)S(1)}, bf16[192,768]{1,0:T(8,128)(2,1)S(1)}, u32[]{:S(2)}, u32[]{:S(2)}) %collective-permute-start.34) | collective-permute-done | bytes 294944 | tf_op jit(solution)/shard_map/ppermute | solution.py:23
  125.5 9.0 %collective-permute-done.35 = bf16[192,768]{1,0:T(8,128)(2,1)S(1)} collective-permute-done((bf16[192,768]{1,0:T(8,128)(2,1)S(1)}, bf16[192,768]{1,0:T(8,128)(2,1)S(1)}, u32[]{:S(2)}, u32[]{:S(2)}) %collective-permute-start.35) | collective-permute-done | bytes 294944 | tf_op jit(solution)/shard_map/ppermute | solution.py:23
  138.8 5.0 %collective-permute-start.32 = (bf16[96,384]{1,0:T(8,128)(2,1)S(1)}, bf16[96,384]{1,0:T(8,128)(2,1)S(1)}, u32[]{:S(2)}, u32[]{:S(2)}) collective-permute-start(bf16[96,384]{1,0:T(8,128)(2,1)S(1)} %get-tuple-element.105), channel_id=1, source_target_pairs={{0,16},{4,20},{8,24},{12,28},{16,0},{20,4},{24,8},{28,12},{1,17},{... | collective-permute-start | bytes 221192 | tf_op jit(solution)/shard_map/ppermute | solution.py:23
  147.4 6.6 %collective-permute-done.37 = bf16[6,96,384]{2,1,0:T(8,128)(2,1)S(1)} collective-permute-done((bf16[6,96,384]{2,1,0:T(8,128)(2,1)S(1)}, bf16[6,96,384]{2,1,0:T(8,128)(2,1)S(1)}, u32[]{:S(2)}, u32[]{:S(2)}) %collective-permute-start.37) | collective-permute-done | bytes 442400 | tf_op jit(solution)/shard_map/ppermute | solution.py:23
  159.4 2.9 %collective-permute-done.40 = bf16[96,384]{1,0:T(8,128)(2,1)S(1)} collective-permute-done((bf16[96,384]{1,0:T(8,128)(2,1)S(1)}, bf16[96,384]{1,0:T(8,128)(2,1)S(1)}, u32[]{:S(2)}, u32[]{:S(2)}) %collective-permute-start.40) | collective-permute-done | bytes 73760 | tf_op jit(solution)/shard_map/ppermute | solution.py:23
  (237 shorter events, 56.9 us)
Async XLA Ops:
  5.5 39.1 %collective-permute-start.23 = (bf16[128,768]{1,0:T(8,128)(2,1)}, bf16[128,768]{1,0:T(8,128)(2,1)S(1)}, u32[]{:S(2)}, u32[]{:S(2)}) collective-permute-start(bf16[128,768]{1,0:T(8,128)(2,1)} %bitcast.143), channel_id=1, source_target_pairs={{0,3},{1,2},{2,1},{3,0},{4,7},{5,6},{6,5},{7,4},{8,11},{9,10},{10,... | collective-permute-start | bytes 589832 | tf_op jit(solution)/shard_map/ppermute | solution.py:23
  7.2 39.4 %collective-permute-start.22 = (bf16[128,768]{1,0:T(8,128)(2,1)}, bf16[128,768]{1,0:T(8,128)(2,1)S(1)}, u32[]{:S(2)}, u32[]{:S(2)}) collective-permute-start(bf16[128,768]{1,0:T(8,128)(2,1)} %bitcast.144), channel_id=1, source_target_pairs={{0,2},{1,3},{2,0},{3,1},{4,6},{5,7},{6,4},{7,5},{8,10},{9,11},{10,... | collective-permute-start | bytes 589832 | tf_op jit(solution)/shard_map/ppermute | solution.py:23
  8.9 37.8 %collective-permute-start.2 = (bf16[128,768]{1,0:T(8,128)(2,1)}, bf16[128,768]{1,0:T(8,128)(2,1)S(1)}, u32[]{:S(2)}, u32[]{:S(2)}) collective-permute-start(bf16[128,768]{1,0:T(8,128)(2,1)} %bitcast.138), channel_id=1, source_target_pairs={{0,3},{1,2},{2,1},{3,0},{4,7},{5,6},{6,5},{7,4},{8,11},{9,10},{10,... | collective-permute-start | bytes 589832 | tf_op jit(solution)/shard_map/ppermute | solution.py:23
  14.6 10.5 %collective-permute-start.6 = (bf16[96,768]{1,0:T(8,128)(2,1)S(1)}, bf16[96,768]{1,0:T(8,128)(2,1)S(1)}, u32[]{:S(2)}, u32[]{:S(2)}) collective-permute-start(bf16[96,768]{1,0:T(8,128)(2,1)S(1)} %slice.141.refs_4_), channel_id=1, source_target_pairs={{0,4},{4,0},{8,12},{12,8},{16,20},{20,16},{24,28},{28,24},{1,5},{5... | collective-permute-start | bytes 442376 | tf_op jit(solution)/shard_map/ppermute | solution.py:23
  21.6 9.8 %collective-permute-start.9 = (bf16[96,768]{1,0:T(8,128)(2,1)S(1)}, bf16[96,768]{1,0:T(8,128)(2,1)S(1)}, u32[]{:S(2)}, u32[]{:S(2)}) collective-permute-start(bf16[96,768]{1,0:T(8,128)(2,1)S(1)} %slice.141.refs_4_), channel_id=1, source_target_pairs={{0,16},{4,20},{8,24},{12,28},{16,0},{20,4},{24,8},{28,12},{1,17},{... | collective-permute-start | bytes 442376 | tf_op jit(solution)/shard_map/ppermute | solution.py:23
  38.9 10.3 %collective-permute-start.1 = (bf16[128,768]{1,0:T(8,128)(2,1)S(1)}, bf16[128,768]{1,0:T(8,128)(2,1)S(1)}, u32[]{:S(2)}, u32[]{:S(2)}) collective-permute-start(bf16[128,768]{1,0:T(8,128)(2,1)S(1)} %bitcast.141), channel_id=1, source_target_pairs={{0,2},{1,3},{2,0},{3,1},{4,6},{5,7},{6,4},{7,5},{8,10},{9,11},{10,... | collective-permute-start | bytes 589832 | tf_op jit(solution)/shard_map/ppermute | solution.py:23
  44.6 8.7 %collective-permute-start.19 = (bf16[96,768]{1,0:T(8,128)(2,1)S(1)}, bf16[96,768]{1,0:T(8,128)(2,1)S(1)}, u32[]{:S(2)}, u32[]{:S(2)}) collective-permute-start(bf16[96,768]{1,0:T(8,128)(2,1)S(1)} %maximum_maximum_fusion.refs_4_.refs_12_), channel_id=1, source_target_pairs={{0,24},{4,28},{8,16},{12,20},{16,8},{20,12},{24,0},{28,4},{1,25},{... | collective-permute-start | bytes 442376 | tf_op jit(solution)/shard_map/ppermute | solution.py:23
  46.6 13.5 %collective-permute-start.17 = (bf16[96,768]{1,0:T(8,128)(2,1)S(1)}, bf16[96,768]{1,0:T(8,128)(2,1)S(1)}, u32[]{:S(2)}, u32[]{:S(2)}) collective-permute-start(bf16[96,768]{1,0:T(8,128)(2,1)S(1)} %maximum_maximum_fusion.refs_4_.refs_12_), channel_id=1, source_target_pairs={{0,16},{4,20},{8,24},{12,28},{16,0},{20,4},{24,8},{28,12},{1,17},{... | collective-permute-start | bytes 442376 | tf_op jit(solution)/shard_map/ppermute | solution.py:23
  46.7 15.3 %collective-permute-start.15 = (bf16[96,768]{1,0:T(8,128)(2,1)S(1)}, bf16[96,768]{1,0:T(8,128)(2,1)S(1)}, u32[]{:S(2)}, u32[]{:S(2)}) collective-permute-start(bf16[96,768]{1,0:T(8,128)(2,1)S(1)} %maximum_maximum_fusion.refs_4_.refs_12_), channel_id=1, source_target_pairs={{0,8},{4,12},{8,0},{12,4},{16,24},{20,28},{24,16},{28,20},{1,9},{5... | collective-permute-start | bytes 442376 | tf_op jit(solution)/shard_map/ppermute | solution.py:23
  49.3 21.4 %collective-permute-start.21 = (bf16[128,768]{1,0:T(8,128)(2,1)S(1)}, bf16[128,768]{1,0:T(8,128)(2,1)S(1)}, u32[]{:S(2)}, u32[]{:S(2)}) collective-permute-start(bf16[128,768]{1,0:T(8,128)(2,1)S(1)} %bitcast.147), channel_id=1, source_target_pairs={{0,1},{1,0},{2,3},{3,2},{4,5},{5,4},{6,7},{7,6},{8,9},{9,8},{10,11... | collective-permute-start | bytes 589832 | tf_op jit(solution)/shard_map/ppermute | solution.py:23
  49.4 21.3 %collective-permute-start.14 = (bf16[96,768]{1,0:T(8,128)(2,1)S(1)}, bf16[96,768]{1,0:T(8,128)(2,1)S(1)}, u32[]{:S(2)}, u32[]{:S(2)}) collective-permute-start(bf16[96,768]{1,0:T(8,128)(2,1)S(1)} %maximum_maximum_fusion.refs_4_.refs_12_), channel_id=1, source_target_pairs={{0,4},{4,0},{8,12},{12,8},{16,20},{20,16},{24,28},{28,24},{1,5},{5... | collective-permute-start | bytes 442376 | tf_op jit(solution)/shard_map/ppermute | solution.py:23
  53.4 17.3 %collective-permute-start.20 = (bf16[96,768]{1,0:T(8,128)(2,1)S(1)}, bf16[96,768]{1,0:T(8,128)(2,1)S(1)}, u32[]{:S(2)}, u32[]{:S(2)}) collective-permute-start(bf16[96,768]{1,0:T(8,128)(2,1)S(1)} %collective-permute-done.19.refs_10_.refs_18_), channel_id=1, source_target_pairs={{0,4},{4,0},{8,12},{12,8},{16,20},{20,16},{24,28},{28,24},{1,5},{5... | collective-permute-start | bytes 442376 | tf_op jit(solution)/shard_map/ppermute | solution.py:23
  60.1 10.6 %collective-permute-start.18 = (bf16[96,768]{1,0:T(8,128)(2,1)S(1)}, bf16[96,768]{1,0:T(8,128)(2,1)S(1)}, u32[]{:S(2)}, u32[]{:S(2)}) collective-permute-start(bf16[96,768]{1,0:T(8,128)(2,1)S(1)} %collective-permute-done.17.refs_8_.refs_16_), channel_id=1, source_target_pairs={{0,4},{4,0},{8,12},{12,8},{16,20},{20,16},{24,28},{28,24},{1,5},{5... | collective-permute-start | bytes 442376 | tf_op jit(solution)/shard_map/ppermute | solution.py:23
  62.0 8.7 %collective-permute-start.16 = (bf16[96,768]{1,0:T(8,128)(2,1)S(1)}, bf16[96,768]{1,0:T(8,128)(2,1)S(1)}, u32[]{:S(2)}, u32[]{:S(2)}) collective-permute-start(bf16[96,768]{1,0:T(8,128)(2,1)S(1)} %collective-permute-done.15.refs_6_.refs_14_), channel_id=1, source_target_pairs={{0,4},{4,0},{8,12},{12,8},{16,20},{20,16},{24,28},{28,24},{1,5},{5... | collective-permute-start | bytes 442376 | tf_op jit(solution)/shard_map/ppermute | solution.py:23
  110.1 9.4 %collective-permute-start.30 = (bf16[4,96,384]{2,1,0:T(8,128)(2,1)}, bf16[4,96,384]{2,1,0:T(8,128)(2,1)S(1)}, u32[]{:S(2)}, u32[]{:S(2)}) collective-permute-start(bf16[4,96,384]{2,1,0:T(8,128)(2,1)} %get-tuple-element.78), channel_id=1, source_target_pairs={{0,4},{4,0},{8,12},{12,8},{16,20},{20,16},{24,28},{28,24},{1,5},{5... | collective-permute-start | bytes 884744 | tf_op jit(solution)/shard_map/ppermute | solution.py:23
  110.9 14.6 %collective-permute-start.34 = (bf16[192,768]{1,0:T(8,128)(2,1)S(1)}, bf16[192,768]{1,0:T(8,128)(2,1)S(1)}, u32[]{:S(2)}, u32[]{:S(2)}) collective-permute-start(bf16[192,768]{1,0:T(8,128)(2,1)S(1)} %copy-done.42), channel_id=1, source_target_pairs={{0,8},{4,12},{8,0},{12,4},{16,24},{20,28},{24,16},{28,20},{1,9},{5... | collective-permute-start | bytes 884744 | tf_op jit(solution)/shard_map/ppermute | solution.py:23
  110.9 23.6 %collective-permute-start.35 = (bf16[192,768]{1,0:T(8,128)(2,1)S(1)}, bf16[192,768]{1,0:T(8,128)(2,1)S(1)}, u32[]{:S(2)}, u32[]{:S(2)}) collective-permute-start(bf16[192,768]{1,0:T(8,128)(2,1)S(1)} %copy-done.41), channel_id=1, source_target_pairs={{0,16},{4,20},{8,24},{12,28},{16,0},{20,4},{24,8},{28,12},{1,17},{... | collective-permute-start | bytes 884744 | tf_op jit(solution)/shard_map/ppermute | solution.py:23
  113.5 20.9 %collective-permute-start.36 = (bf16[192,768]{1,0:T(8,128)(2,1)S(1)}, bf16[192,768]{1,0:T(8,128)(2,1)S(1)}, u32[]{:S(2)}, u32[]{:S(2)}) collective-permute-start(bf16[192,768]{1,0:T(8,128)(2,1)S(1)} %copy-done.40), channel_id=1, source_target_pairs={{0,24},{4,28},{8,16},{12,20},{16,8},{20,12},{24,0},{28,4},{1,25},{... | collective-permute-start | bytes 884744 | tf_op jit(solution)/shard_map/ppermute | solution.py:23
  115.3 31.8 %collective-permute-start.27 = (bf16[256,768]{1,0:T(8,128)(2,1)}, bf16[256,768]{1,0:T(8,128)(2,1)S(1)}, u32[]{:S(2)}, u32[]{:S(2)}) collective-permute-start(bf16[256,768]{1,0:T(8,128)(2,1)} %get-tuple-element.74), channel_id=1, source_target_pairs={{0,1},{1,0},{2,3},{3,2},{4,5},{5,4},{6,7},{7,6},{8,9},{9,8},{10,11... | collective-permute-start | bytes 1179656 | tf_op jit(solution)/shard_map/ppermute | solution.py:23
  119.5 27.5 %collective-permute-start.28 = (bf16[256,768]{1,0:T(8,128)(2,1)S(1)}, bf16[256,768]{1,0:T(8,128)(2,1)S(1)}, u32[]{:S(2)}, u32[]{:S(2)}) collective-permute-start(bf16[256,768]{1,0:T(8,128)(2,1)S(1)} %copy-done.39), channel_id=1, source_target_pairs={{0,2},{1,3},{2,0},{3,1},{4,6},{5,7},{6,4},{7,5},{8,10},{9,11},{10,... | collective-permute-start | bytes 1179656 | tf_op jit(solution)/shard_map/ppermute | solution.py:23
  125.5 21.6 %collective-permute-start.29 = (bf16[256,768]{1,0:T(8,128)(2,1)S(1)}, bf16[256,768]{1,0:T(8,128)(2,1)S(1)}, u32[]{:S(2)}, u32[]{:S(2)}) collective-permute-start(bf16[256,768]{1,0:T(8,128)(2,1)S(1)} %copy-done.38), channel_id=1, source_target_pairs={{0,3},{1,2},{2,1},{3,0},{4,7},{5,6},{6,5},{7,4},{8,11},{9,10},{10,... | collective-permute-start | bytes 1179656 | tf_op jit(solution)/shard_map/ppermute | solution.py:23
  134.5 9.5 %collective-permute-start.33 = (bf16[96,384]{1,0:T(8,128)(2,1)S(1)}, bf16[96,384]{1,0:T(8,128)(2,1)S(1)}, u32[]{:S(2)}, u32[]{:S(2)}) collective-permute-start(bf16[96,384]{1,0:T(8,128)(2,1)S(1)} %get-tuple-element.104), channel_id=1, source_target_pairs={{0,24},{4,28},{8,16},{12,20},{16,8},{20,12},{24,0},{28,4},{1,25},{... | collective-permute-start | bytes 221192 | tf_op jit(solution)/shard_map/ppermute | solution.py:23
  143.9 10.0 %collective-permute-start.37 = (bf16[6,96,384]{2,1,0:T(8,128)(2,1)S(1)}, bf16[6,96,384]{2,1,0:T(8,128)(2,1)S(1)}, u32[]{:S(2)}, u32[]{:S(2)}) collective-permute-start(bf16[6,96,384]{2,1,0:T(8,128)(2,1)S(1)} %pad_maximum_fusion), channel_id=1, source_target_pairs={{0,4},{4,0},{8,12},{12,8},{16,20},{20,16},{24,28},{28,24},{1,5},{5... | collective-permute-start | bytes 1327112 | tf_op jit(solution)/shard_map/ppermute | solution.py:23
  158.1 9.3 %collective-permute-start.44 = (bf16[48,768]{1,0:T(8,128)(2,1)S(1)}, bf16[48,768]{1,0:T(8,128)(2,1)S(1)}, u32[]{:S(2)}, u32[]{:S(2)}) collective-permute-start(bf16[48,768]{1,0:T(8,128)(2,1)S(1)} %pad_maximum_fusion.4), channel_id=1, source_target_pairs={{0,0},{4,1},{8,2},{12,3},{16,4},{20,5},{24,6},{28,7},{1,8},{5,9},{... | collective-permute-start | bytes 221192 | tf_op jit(solution)/shard_map/ppermute | solution.py:905
  (64 other events, 746.3 us)

commit v5 on v4

--- a/solution.py
+++ b/solution.py
@@ -9,7 +9,9 @@
 STATE = 128
 CONV = 4
 CHUNK = 128
-VMEM_LIMIT = 56 * 2**20
+VMEM_LIMIT = 60 * 2**20
+SMALL_LIMIT = 12 * 2**20
+SMALL = ("kernel_6",)
 LANES = 128
 EPSILON = 1e-05
 FULL = lax.Precision.HIGHEST
@@ -649,14 +651,14 @@
         along = jnp.sum(dn * (x * rms_inverse(x)), axis=0, keepdims=True)
         norm_grad_ref[...] = along
         gin_ref[:, channels:] = dot(normed_ref[...], draw, 0, 0)
-        half = gin_ref.shape[1] // 2
-        store_slabs(gin_ref, slabs[: slab_count // 2], slice(0, half))
-        store_slabs(gin_ref, slabs[slab_count // 2 :], slice(half, 2 * half))
+        early = slabs[0].shape[-1]
+        store_slabs(gin_ref, slabs[: slab_count // 2], slice(0, early))
+        store_slabs(gin_ref, slabs[slab_count // 2 :], slice(early, gin_ref.shape[1]))
 
     return body
 
 
-def call(body, outs, scratch, *operands):
+def call(name, body, outs, scratch, *operands):
     vmem = pl.BlockSpec(memory_space=pltpu.VMEM)
     return pl.pallas_call(
         body,
@@ -667,7 +669,7 @@
             pltpu.VMEM(*shape) if isinstance(shape[0], tuple) else pltpu.VMEM(shape, F32)
             for shape in scratch
         ],
-        compiler_params=pltpu.CompilerParams(vmem_limit_bytes=VMEM_LIMIT),
+        compiler_params=pltpu.CompilerParams(vmem_limit_bytes=SMALL_LIMIT if name in SMALL else VMEM_LIMIT),
     )(*operands)
 
 
@@ -703,6 +705,7 @@
 
     stride = -(-rows // 16) * 16
     blocks = call(
+        "pack",
         pack_kernel(width, inner, heads_here, seq_n),
         [((rows, cols + width), BF16)] * seq_n,
         [(seq_n * stride, cols + width)],
@@ -773,6 +776,7 @@
     sources = [(tall, STATE), (length, width), (tall, width), (length + 8, width)]
     sources += [(length, LANES), (8, tall)]
     normed, proj, pre, y = call(
+        "kernel_1",
         forward_kernel(width, heads_here, len(x_pieces), len(w_first)),
         [((length, model), BF16)]
         + [((length, cols), F32), ((length, channels), F32), ((length, width), F32)],
@@ -782,6 +786,7 @@
     og_scratch, wg_scratch = ((length, model), BF16), ((model, width), BF16)
     wo_scratch = ((width, model), BF16)
     gate, d_gated, stats = call(
+        "kernel_2",
         gate_kernel(len(og_pieces), len(w_second)),
         [((length, width), F32), ((length, width), F32), ((chunks, 8, LANES), F32)],
         [og_scratch, wg_scratch, wo_scratch],
@@ -791,12 +796,12 @@
     block_rows = rows * seq_n
     dp_inner = inner_of(dp_n)
     dp_outer = dp_n // dp_inner
-    half = cols // 2
+    part_lanes = (width + STATE, STATE + LANES)
     if split_here:
-        halves = [((dp_outer, block_rows, half), BF16)] * dp_inner
+        late_parts = [[((dp_outer, block_rows, n), BF16)] * dp_inner for n in part_lanes]
         far_blocks = [((dp_inner * block_rows, 2 * width), BF16)] * dp_outer
     else:
-        halves = [((model, half), BF16)]
+        late_parts = [[((model, n), BF16)] for n in part_lanes]
         far_blocks = [((model, 2 * width), BF16)]
     pieces = [((piece, model), BF16)] * seq_n
 
@@ -819,6 +824,7 @@
         return tree_sum([p.astype(F32) for p in parts]).astype(BF16)
 
     made = call(
+        "kernel_3",
         out_kernel(width, inner, len(og_pieces), len(w_second), len(far_blocks), block_rows),
         pieces + far_blocks
         + [((length, width), BF16), ((length, width), F32), ((8, width), F32)],
@@ -829,6 +835,7 @@
     far_early = far_sum(made[: len(far_blocks)])
     d_gate, dy, g_gain = made[len(far_blocks) :]
     dconv, draw, conv_grad, head_grad = call(
+        "kernel_4",
         mixer_back_kernel(width),
         [((length, channels), BF16), ((length, LANES), BF16)]
         + [((8, channels), F32), ((8, LANES), F32)],
@@ -839,14 +846,18 @@
     )
 
     made = call(
-        weight_back_kernel(len(x_pieces), len(w_first), 2 * len(halves)),
-        halves + halves + [((2 * piece, model), BF16)] * seq_n + [((1, model), F32)],
+        "kernel_5",
+        weight_back_kernel(len(x_pieces), len(w_first), 2 * len(late_parts[0])),
+        late_parts[0] + late_parts[1] + [((2 * piece, model), BF16)] * seq_n + [((1, model), F32)],
         [((length, model), BF16), ((model, cols), BF16), wg_scratch, (length, model), (model, cols)],
         *x_pieces, *w_first, *w_second, *out_parts, normed, dconv, draw, d_gate,
     )
-    dn_pieces, norm_grad = made[2 * len(halves) : -1], made[-1]
-    near_values = near_sum(made[: len(halves)])
-    rest = made[len(halves) : 2 * len(halves)]
+    slab_count = len(late_parts[0])
+    dn_pieces, norm_grad = made[2 * slab_count : -1], made[-1]
+    near_values = near_sum(made[:slab_count])
+    rest = made[slab_count : 2 * slab_count]
+    half = part_lanes[1]
+    folds = 2 * width // half
     conv_full = jnp.zeros((CONV + 1, inner), F32)
     conv_full = lax.dynamic_update_slice_in_dim(
         conv_full, conv_grad[: CONV + 1, :width], place * width, 1
@@ -890,12 +901,12 @@
         short = lax.dynamic_index_in_dim(small, inner_place ^ j, 1, False)
         slab = slab + jnp.pad(short, ((0, 0), (0, 0), (half - LANES, 0)))
         block = lax.dynamic_index_in_dim(far_early, inner_place ^ j, 0, False)
-        block = jnp.stack([block[:, :width], block[:, width:]])
+        block = jnp.stack([block[:, f * half : (f + 1) * half] for f in range(folds)])
         together.append(jnp.concatenate([slab, block], 0))
     together = [swap(t, "dp", j) if j else t for j, t in enumerate(together)]
     together = tree_sum([t.astype(F32) for t in together])
     near_rest = together[:dp_outer].astype(BF16)
-    early = jnp.concatenate([together[dp_outer], together[dp_outer + 1]], 1)
+    early = jnp.concatenate([together[dp_outer + f] for f in range(folds)], 1)
     late = [reduce_far(near_values), reduce_far(near_rest)]
     own_out = early[:, width:]
     own_out = jnp.concatenate(
@@ -912,6 +923,7 @@
     parts = scatter_xor(both.astype(BF16), "seq")
     short = [((CONV, conv_here), F32)] + [((1, n), F32) for n in lengths[CONV:]]
     grad_in_w, *short = call(
+        "kernel_6",
         finish_kernel(width, inner, heads_here, lengths, small_at),
         [((rows, in_weight.shape[1]), F32)] + short,
         [(seq_n * stride, cols + width)],

time: 172 us -> 173 us (level)
  waiting for transfers between devices: 62.7 us -> 68.1 us
  starting transfers between devices: 55.1 us -> 52.1 us
    ppermute x43, waiting for transfers between devices: 62.7 us -> 68 us  [swap(): return lax.ppermute(x, axis, [(i, i ^ offset) for i in range(count)])]
    ppermute x43, starting transfers between devices: 52.9 us -> 49.9 us  [swap(): return lax.ppermute(x, axis, [(i, i ^ offset) for i in range(count)])]
  transfers between devices with their start and end apart: 45 -> 45, of which waited for: 19 -> 18; matrix products, arithmetic and copies ran while one was open for 4% -> 4% of each run, Pallas kernels for 4% -> 4%
where the time goes in v5:
time: 173 us; the launch traced here: 172 us
  waiting for transfers between devices  68.1 us (39%)
  starting transfers between devices  52.1 us (30%)
  Pallas kernels  37.5 us (22%)
  other arithmetic  6.75 us (4%)
  local copies, waits for them, and re-layouts  6.36 us (4%)
    ppermute x43, waiting for transfers between devices, swap(): return lax.ppermute(x, axis, [(i, i ^ offset) for i in range(count)])  68 us
    ppermute x43, starting transfers between devices, swap(): return lax.ppermute(x, axis, [(i, i ^ offset) for i in range(count)])  49.9 us
    pallas_call x7, Pallas kernels, call(): pl.pallas_call(body, out_shape=[jax.ShapeDtypeStruct(shape, kind) for sha...  37.5 us
  transfers between devices with their start and end apart: 45, of which 18 were waited for; matrix products, arithmetic and copies ran while one was open for 4% of the time, Pallas kernels for 4%

profile of v5, /device:TPU:0, one launch (start us, length us, event | category | flops | bytes accessed | tf_op | source)
XLA Modules:
  0.0 172.3 jit_solution(12735245264927343776)
XLA Ops:
  2.9 2.5 %collective-permute-start.4 = (bf16[24,1152]{1,0:T(8,128)(2,1)}, bf16[24,1152]{1,0:T(8,128)(2,1)S(1)}, u32[]{:S(2)}, u32[]{:S(2)}) collective-permute-start(bf16[24,1152]{1,0:T(8,128)(2,1)} %get-tuple-element.56), channel_id=1, source_target_pairs={{0,2},{1,3},{2,0},{3,1},{4,6},{5,7},{6,4},{7,5},{8,10},{9,11},{10,... | collective-permute-start | bytes 165896 | tf_op jit(solution)/shard_map/ppermute | solution.py:25
  8.9 4.6 %collective-permute-start.2 = (bf16[128,768]{1,0:T(8,128)(2,1)}, bf16[128,768]{1,0:T(8,128)(2,1)S(1)}, u32[]{:S(2)}, u32[]{:S(2)}) collective-permute-start(bf16[128,768]{1,0:T(8,128)(2,1)} %bitcast.144), channel_id=1, source_target_pairs={{0,3},{1,2},{2,1},{3,0},{4,7},{5,6},{6,5},{7,4},{8,11},{9,10},{10,... | collective-permute-start | bytes 589832 | tf_op jit(solution)/shard_map/ppermute | solution.py:25
  14.6 2.6 %collective-permute-start.6 = (bf16[96,768]{1,0:T(8,128)(2,1)S(1)}, bf16[96,768]{1,0:T(8,128)(2,1)S(1)}, u32[]{:S(2)}, u32[]{:S(2)}) collective-permute-start(bf16[96,768]{1,0:T(8,128)(2,1)S(1)} %slice.156.refs_4_), channel_id=1, source_target_pairs={{0,4},{4,0},{8,12},{12,8},{16,20},{20,16},{24,28},{28,24},{1,5},{5... | collective-permute-start | bytes 442376 | tf_op jit(solution)/shard_map/ppermute | solution.py:25
  17.3 4.3 %collective-permute-done.7.refs_6_ = bf16[96,768]{1,0:T(8,128)(2,1)S(1)} collective-permute-done((bf16[96,768]{1,0:T(8,128)(2,1)S(1)}, bf16[96,768]{1,0:T(8,128)(2,1)S(1)}, u32[]{:S(2)}, u32[]{:S(2)}) %collective-permute-start.7) | collective-permute-done | bytes 147488 | tf_op jit(solution)/shard_map/ppermute | solution.py:25
  21.6 3.5 %collective-permute-start.9 = (bf16[96,768]{1,0:T(8,128)(2,1)S(1)}, bf16[96,768]{1,0:T(8,128)(2,1)S(1)}, u32[]{:S(2)}, u32[]{:S(2)}) collective-permute-start(bf16[96,768]{1,0:T(8,128)(2,1)S(1)} %slice.156.refs_4_), channel_id=1, source_target_pairs={{0,16},{4,20},{8,24},{12,28},{16,0},{20,4},{24,8},{28,12},{1,17},{... | collective-permute-start | bytes 442376 | tf_op jit(solution)/shard_map/ppermute | solution.py:25
  25.1 6.3 %collective-permute-done.9.refs_8_ = bf16[96,768]{1,0:T(8,128)(2,1)S(1)} collective-permute-done((bf16[96,768]{1,0:T(8,128)(2,1)S(1)}, bf16[96,768]{1,0:T(8,128)(2,1)S(1)}, u32[]{:S(2)}, u32[]{:S(2)}) %collective-permute-start.9) | collective-permute-done | bytes 147488 | tf_op jit(solution)/shard_map/ppermute | solution.py:25
  34.9 4.0 %collective-permute-done.11.refs_10_ = bf16[96,768]{1,0:T(8,128)(2,1)S(1)} collective-permute-done((bf16[96,768]{1,0:T(8,128)(2,1)S(1)}, bf16[96,768]{1,0:T(8,128)(2,1)S(1)}, u32[]{:S(2)}, u32[]{:S(2)}) %collective-permute-start.11) | collective-permute-done | bytes 147488 | tf_op jit(solution)/shard_map/ppermute | solution.py:25
  40.5 3.7 %collective-permute-done.12.refs_11_ = bf16[96,768]{1,0:T(8,128)(2,1)S(1)} collective-permute-done((bf16[96,768]{1,0:T(8,128)(2,1)S(1)}, bf16[96,768]{1,0:T(8,128)(2,1)S(1)}, u32[]{:S(2)}, u32[]{:S(2)}) %collective-permute-start.12) | collective-permute-done | bytes 147488 | tf_op jit(solution)/shard_map/ppermute | solution.py:25
  46.7 2.4 %collective-permute-start.15 = (bf16[96,768]{1,0:T(8,128)(2,1)S(1)}, bf16[96,768]{1,0:T(8,128)(2,1)S(1)}, u32[]{:S(2)}, u32[]{:S(2)}) collective-permute-start(bf16[96,768]{1,0:T(8,128)(2,1)S(1)} %maximum_maximum_fusion.refs_4_.refs_12_), channel_id=1, source_target_pairs={{0,8},{4,12},{8,0},{12,4},{16,24},{20,28},{24,16},{28,20},{1,9},{5... | collective-permute-start | bytes 442376 | tf_op jit(solution)/shard_map/ppermute | solution.py:25
  50.9 2.5 %collective-permute-done.19.refs_10_.refs_18_ = bf16[96,768]{1,0:T(8,128)(2,1)S(1)} collective-permute-done((bf16[96,768]{1,0:T(8,128)(2,1)S(1)}, bf16[96,768]{1,0:T(8,128)(2,1)S(1)}, u32[]{:S(2)}, u32[]{:S(2)}) %collective-permute-start.19) | collective-permute-done | bytes 147488 | tf_op jit(solution)/shard_map/ppermute | solution.py:25
  54.8 5.3 %collective-permute-done.17.refs_8_.refs_16_ = bf16[96,768]{1,0:T(8,128)(2,1)S(1)} collective-permute-done((bf16[96,768]{1,0:T(8,128)(2,1)S(1)}, bf16[96,768]{1,0:T(8,128)(2,1)S(1)}, u32[]{:S(2)}, u32[]{:S(2)}) %collective-permute-start.17) | collective-permute-done | bytes 147488 | tf_op jit(solution)/shard_map/ppermute | solution.py:25
  62.9 7.2 %shard_map.204 = (bf16[512,768]{1,0:T(8,128)(2,1)}, f32[512,768]{1,0:T(8,128)}, f32[512,640]{1,0:T(8,128)}, f32[512,384]{1,0:T(8,128)}) custom-call(bf16[128,768]{1,0:T(8,128)(2,1)} %bitcast.145, bf16[128,768]{1,0:T(8,128)(2,1)} %copy-done.17, bf16[128,768]{1,0:T(8,128)(2,1)} %copy-done.16, bf16[128,768]{1,0:T(8,128)(2,1)} %copy-done.15, ...), custom_call_target="tpu_custom_call" | custom-call | tf_op jit(solution)/shard_map/pallas_call | solution.py:663
  71.5 4.1 %shard_map.205 = (f32[512,384]{1,0:T(8,128)}, f32[512,384]{1,0:T(8,128)}, f32[4,8,128]{2,1,0:T(8,128)}) custom-call(bf16[128,768]{1,0:T(8,128)(2,1)} %bitcast.151, bf16[128,768]{1,0:T(8,128)(2,1)} %copy-done.18, bf16[128,768]{1,0:T(8,128)(2,1)} %copy-done.14, bf16[128,768]{1,0:T(8,128)(2,1)} %copy-done.13, bf16[96,768]{1,0:T(8,128)(2,1)} %copy-done.2, ...), custom_call_target="tpu_custom_call" | custom-call | tf_op jit(solution)/shard_map/pallas_call | solution.py:663
  79.1 2.3 %collective-permute-done.25.refs_14_ = f32[4,8,128]{2,1,0:T(8,128)S(1)} collective-permute-done((f32[4,8,128]{2,1,0:T(8,128)}, f32[4,8,128]{2,1,0:T(8,128)S(1)}, u32[]{:S(2)}, u32[]{:S(2)}) %collective-permute-start.25) | collective-permute-done | bytes 16416 | tf_op jit(solution)/shard_map/ppermute | solution.py:25
  82.0 5.7 %shard_map.206 = (bf16[128,768]{1,0:T(8,128)(2,1)}, bf16[128,768]{1,0:T(8,128)(2,1)}, bf16[128,768]{1,0:T(8,128)(2,1)}, bf16[128,768]{1,0:T(8,128)(2,1)}, bf16[1...) custom-call(bf16[128,768]{1,0:T(8,128)(2,1)} %bitcast.152, ...), custom_call_target="tpu_custom_call" | custom-call | tf_op jit(solution)/shard_map/pallas_call | solution.py:663
  87.7 10.9 %shard_map.207 = (bf16[512,640]{1,0:T(8,128)(2,1)}, bf16[512,128]{1,0:T(8,128)(2,1)}, f32[8,640]{1,0:T(8,128)}, f32[8,128]{1,0:T(8,128)}) custom-call(f32[8,640]{1,0:T(8,128)} %fusion.24.refs_12_.conv_ref, s32[1,512]{1,0:T(1,128)} %seg_ref.1, f32[1,24]{1,0:T(1,128)} %bitcast.166, f32[1,24]{1,0:T(1,128)} %bitcast.168, f32[1,24]{1,0:T(1,128)} %bitcast.170, ...), custom_call_target="tpu_custom_call" | custom-call | tf_op jit(solution)/shard_map/pallas_call | solution.py:663
  101.5 7.0 %shard_map.208 = (bf16[4,96,512]{2,1,0:T(8,128)(2,1)}, bf16[4,96,512]{2,1,0:T(8,128)(2,1)}, bf16[4,96,256]{2,1,0:T(8,128)(2,1)}, bf16[4,96,256]{2,1,0:T(8,128)(2...) custom-call(bf16[128,768]{1,0:T(8,128)(2,1)} %bitcast.146, ...), custom_call_target="tpu_custom_call" | custom-call | tf_op jit(solution)/shard_map/pallas_call | solution.py:663
  110.6 2.9 %collective-permute-start.35 = (bf16[192,768]{1,0:T(8,128)(2,1)S(1)}, bf16[192,768]{1,0:T(8,128)(2,1)S(1)}, u32[]{:S(2)}, u32[]{:S(2)}) collective-permute-start(bf16[192,768]{1,0:T(8,128)(2,1)S(1)} %copy-done.38), channel_id=1, source_target_pairs={{0,16},{4,20},{8,24},{12,28},{16,0},{20,4},{24,8},{28,12},{1,17},{... | collective-permute-start | bytes 884744 | tf_op jit(solution)/shard_map/ppermute | solution.py:25
  117.2 8.3 %collective-permute-done.34 = bf16[192,768]{1,0:T(8,128)(2,1)S(1)} collective-permute-done((bf16[192,768]{1,0:T(8,128)(2,1)S(1)}, bf16[192,768]{1,0:T(8,128)(2,1)S(1)}, u32[]{:S(2)}, u32[]{:S(2)}) %collective-permute-start.34) | collective-permute-done | bytes 294944 | tf_op jit(solution)/shard_map/ppermute | solution.py:25
  125.6 8.6 %collective-permute-done.35 = bf16[192,768]{1,0:T(8,128)(2,1)S(1)} collective-permute-done((bf16[192,768]{1,0:T(8,128)(2,1)S(1)}, bf16[192,768]{1,0:T(8,128)(2,1)S(1)}, u32[]{:S(2)}, u32[]{:S(2)}) %collective-permute-start.35) | collective-permute-done | bytes 294944 | tf_op jit(solution)/shard_map/ppermute | solution.py:25
  136.5 9.6 %collective-permute-done.30 = bf16[4,96,512]{2,1,0:T(8,128)(2,1)S(1)} collective-permute-done((bf16[4,96,512]{2,1,0:T(8,128)(2,1)S(1)}, bf16[4,96,512]{2,1,0:T(8,128)(2,1)S(1)}, u32[]{:S(2)}, u32[]{:S(2)}) %collective-permute-start.30) | collective-permute-done | bytes 393248 | tf_op jit(solution)/shard_map/ppermute | solution.py:25
  146.3 2.5 %collective-permute-start.33 = (bf16[96,512]{1,0:T(8,128)(2,1)S(1)}, bf16[96,512]{1,0:T(8,128)(2,1)S(1)}, u32[]{:S(2)}, u32[]{:S(2)}) collective-permute-start(bf16[96,512]{1,0:T(8,128)(2,1)S(1)} %get-tuple-element.102), channel_id=1, source_target_pairs={{0,24},{4,28},{8,16},{12,20},{16,8},{20,12},{24,0},{28,4},{1,25},{... | collective-permute-start | bytes 294920 | tf_op jit(solution)/shard_map/ppermute | solution.py:25
  152.9 4.3 %collective-permute-done.32 = bf16[96,512]{1,0:T(8,128)(2,1)S(1)} collective-permute-done((bf16[96,512]{1,0:T(8,128)(2,1)S(1)}, bf16[96,512]{1,0:T(8,128)(2,1)S(1)}, u32[]{:S(2)}, u32[]{:S(2)}) %collective-permute-start.32) | collective-permute-done | bytes 98336 | tf_op jit(solution)/shard_map/ppermute | solution.py:25
  157.7 2.9 %collective-permute-start.40 = (bf16[96,256]{1,0:T(8,128)(2,1)S(1)}, bf16[96,256]{1,0:T(8,128)(2,1)S(1)}, u32[]{:S(2)}, u32[]{:S(2)}) collective-permute-start(bf16[96,256]{1,0:T(8,128)(2,1)S(1)} %get-tuple-element.118), channel_id=1, source_target_pairs={{0,24},{4,28},{8,16},{12,20},{16,8},{20,12},{24,0},{28,4},{1,25},{... | collective-permute-start | bytes 147464 | tf_op jit(solution)/shard_map/ppermute | solution.py:25
  (232 shorter events, 52.9 us)
Async XLA Ops:
  5.5 8.0 %collective-permute-start.5 = (bf16[24,1152]{1,0:T(8,128)(2,1)}, bf16[24,1152]{1,0:T(8,128)(2,1)S(1)}, u32[]{:S(2)}, u32[]{:S(2)}) collective-permute-start(bf16[24,1152]{1,0:T(8,128)(2,1)} %get-tuple-element.57), channel_id=1, source_target_pairs={{0,3},{1,2},{2,1},{3,0},{4,7},{5,6},{6,5},{7,4},{8,11},{9,10},{10,... | collective-permute-start | bytes 165896 | tf_op jit(solution)/shard_map/ppermute | solution.py:25
  5.5 39.1 %collective-permute-start.23 = (bf16[128,768]{1,0:T(8,128)(2,1)}, bf16[128,768]{1,0:T(8,128)(2,1)S(1)}, u32[]{:S(2)}, u32[]{:S(2)}) collective-permute-start(bf16[128,768]{1,0:T(8,128)(2,1)} %bitcast.149), channel_id=1, source_target_pairs={{0,3},{1,2},{2,1},{3,0},{4,7},{5,6},{6,5},{7,4},{8,11},{9,10},{10,... | collective-permute-start | bytes 589832 | tf_op jit(solution)/shard_map/ppermute | solution.py:25
  7.2 39.4 %collective-permute-start.22 = (bf16[128,768]{1,0:T(8,128)(2,1)}, bf16[128,768]{1,0:T(8,128)(2,1)S(1)}, u32[]{:S(2)}, u32[]{:S(2)}) collective-permute-start(bf16[128,768]{1,0:T(8,128)(2,1)} %bitcast.150), channel_id=1, source_target_pairs={{0,2},{1,3},{2,0},{3,1},{4,6},{5,7},{6,4},{7,5},{8,10},{9,11},{10,... | collective-permute-start | bytes 589832 | tf_op jit(solution)/shard_map/ppermute | solution.py:25
  8.9 37.8 %collective-permute-start.2 = (bf16[128,768]{1,0:T(8,128)(2,1)}, bf16[128,768]{1,0:T(8,128)(2,1)S(1)}, u32[]{:S(2)}, u32[]{:S(2)}) collective-permute-start(bf16[128,768]{1,0:T(8,128)(2,1)} %bitcast.144), channel_id=1, source_target_pairs={{0,3},{1,2},{2,1},{3,0},{4,7},{5,6},{6,5},{7,4},{8,11},{9,10},{10,... | collective-permute-start | bytes 589832 | tf_op jit(solution)/shard_map/ppermute | solution.py:25
  14.6 10.5 %collective-permute-start.6 = (bf16[96,768]{1,0:T(8,128)(2,1)S(1)}, bf16[96,768]{1,0:T(8,128)(2,1)S(1)}, u32[]{:S(2)}, u32[]{:S(2)}) collective-permute-start(bf16[96,768]{1,0:T(8,128)(2,1)S(1)} %slice.156.refs_4_), channel_id=1, source_target_pairs={{0,4},{4,0},{8,12},{12,8},{16,20},{20,16},{24,28},{28,24},{1,5},{5... | collective-permute-start | bytes 442376 | tf_op jit(solution)/shard_map/ppermute | solution.py:25
  21.6 9.8 %collective-permute-start.9 = (bf16[96,768]{1,0:T(8,128)(2,1)S(1)}, bf16[96,768]{1,0:T(8,128)(2,1)S(1)}, u32[]{:S(2)}, u32[]{:S(2)}) collective-permute-start(bf16[96,768]{1,0:T(8,128)(2,1)S(1)} %slice.156.refs_4_), channel_id=1, source_target_pairs={{0,16},{4,20},{8,24},{12,28},{16,0},{20,4},{24,8},{28,12},{1,17},{... | collective-permute-start | bytes 442376 | tf_op jit(solution)/shard_map/ppermute | solution.py:25
  38.9 10.3 %collective-permute-start.1 = (bf16[128,768]{1,0:T(8,128)(2,1)S(1)}, bf16[128,768]{1,0:T(8,128)(2,1)S(1)}, u32[]{:S(2)}, u32[]{:S(2)}) collective-permute-start(bf16[128,768]{1,0:T(8,128)(2,1)S(1)} %bitcast.147), channel_id=1, source_target_pairs={{0,2},{1,3},{2,0},{3,1},{4,6},{5,7},{6,4},{7,5},{8,10},{9,11},{10,... | collective-permute-start | bytes 589832 | tf_op jit(solution)/shard_map/ppermute | solution.py:25
  44.6 8.7 %collective-permute-start.19 = (bf16[96,768]{1,0:T(8,128)(2,1)S(1)}, bf16[96,768]{1,0:T(8,128)(2,1)S(1)}, u32[]{:S(2)}, u32[]{:S(2)}) collective-permute-start(bf16[96,768]{1,0:T(8,128)(2,1)S(1)} %maximum_maximum_fusion.refs_4_.refs_12_), channel_id=1, source_target_pairs={{0,24},{4,28},{8,16},{12,20},{16,8},{20,12},{24,0},{28,4},{1,25},{... | collective-permute-start | bytes 442376 | tf_op jit(solution)/shard_map/ppermute | solution.py:25
  46.6 13.5 %collective-permute-start.17 = (bf16[96,768]{1,0:T(8,128)(2,1)S(1)}, bf16[96,768]{1,0:T(8,128)(2,1)S(1)}, u32[]{:S(2)}, u32[]{:S(2)}) collective-permute-start(bf16[96,768]{1,0:T(8,128)(2,1)S(1)} %maximum_maximum_fusion.refs_4_.refs_12_), channel_id=1, source_target_pairs={{0,16},{4,20},{8,24},{12,28},{16,0},{20,4},{24,8},{28,12},{1,17},{... | collective-permute-start | bytes 442376 | tf_op jit(solution)/shard_map/ppermute | solution.py:25
  46.7 15.3 %collective-permute-start.15 = (bf16[96,768]{1,0:T(8,128)(2,1)S(1)}, bf16[96,768]{1,0:T(8,128)(2,1)S(1)}, u32[]{:S(2)}, u32[]{:S(2)}) collective-permute-start(bf16[96,768]{1,0:T(8,128)(2,1)S(1)} %maximum_maximum_fusion.refs_4_.refs_12_), channel_id=1, source_target_pairs={{0,8},{4,12},{8,0},{12,4},{16,24},{20,28},{24,16},{28,20},{1,9},{5... | collective-permute-start | bytes 442376 | tf_op jit(solution)/shard_map/ppermute | solution.py:25
  49.3 21.4 %collective-permute-start.21 = (bf16[128,768]{1,0:T(8,128)(2,1)S(1)}, bf16[128,768]{1,0:T(8,128)(2,1)S(1)}, u32[]{:S(2)}, u32[]{:S(2)}) collective-permute-start(bf16[128,768]{1,0:T(8,128)(2,1)S(1)} %bitcast.153), channel_id=1, source_target_pairs={{0,1},{1,0},{2,3},{3,2},{4,5},{5,4},{6,7},{7,6},{8,9},{9,8},{10,11... | collective-permute-start | bytes 589832 | tf_op jit(solution)/shard_map/ppermute | solution.py:25
  49.4 21.3 %collective-permute-start.14 = (bf16[96,768]{1,0:T(8,128)(2,1)S(1)}, bf16[96,768]{1,0:T(8,128)(2,1)S(1)}, u32[]{:S(2)}, u32[]{:S(2)}) collective-permute-start(bf16[96,768]{1,0:T(8,128)(2,1)S(1)} %maximum_maximum_fusion.refs_4_.refs_12_), channel_id=1, source_target_pairs={{0,4},{4,0},{8,12},{12,8},{16,20},{20,16},{24,28},{28,24},{1,5},{5... | collective-permute-start | bytes 442376 | tf_op jit(solution)/shard_map/ppermute | solution.py:25
  53.4 17.3 %collective-permute-start.20 = (bf16[96,768]{1,0:T(8,128)(2,1)S(1)}, bf16[96,768]{1,0:T(8,128)(2,1)S(1)}, u32[]{:S(2)}, u32[]{:S(2)}) collective-permute-start(bf16[96,768]{1,0:T(8,128)(2,1)S(1)} %collective-permute-done.19.refs_10_.refs_18_), channel_id=1, source_target_pairs={{0,4},{4,0},{8,12},{12,8},{16,20},{20,16},{24,28},{28,24},{1,5},{5... | collective-permute-start | bytes 442376 | tf_op jit(solution)/shard_map/ppermute | solution.py:25
  60.1 10.6 %collective-permute-start.18 = (bf16[96,768]{1,0:T(8,128)(2,1)S(1)}, bf16[96,768]{1,0:T(8,128)(2,1)S(1)}, u32[]{:S(2)}, u32[]{:S(2)}) collective-permute-start(bf16[96,768]{1,0:T(8,128)(2,1)S(1)} %collective-permute-done.17.refs_8_.refs_16_), channel_id=1, source_target_pairs={{0,4},{4,0},{8,12},{12,8},{16,20},{20,16},{24,28},{28,24},{1,5},{5... | collective-permute-start | bytes 442376 | tf_op jit(solution)/shard_map/ppermute | solution.py:25
  62.0 8.7 %collective-permute-start.16 = (bf16[96,768]{1,0:T(8,128)(2,1)S(1)}, bf16[96,768]{1,0:T(8,128)(2,1)S(1)}, u32[]{:S(2)}, u32[]{:S(2)}) collective-permute-start(bf16[96,768]{1,0:T(8,128)(2,1)S(1)} %collective-permute-done.15.refs_6_.refs_14_), channel_id=1, source_target_pairs={{0,4},{4,0},{8,12},{12,8},{16,20},{20,16},{24,28},{28,24},{1,5},{5... | collective-permute-start | bytes 442376 | tf_op jit(solution)/shard_map/ppermute | solution.py:25
  110.5 15.1 %collective-permute-start.34 = (bf16[192,768]{1,0:T(8,128)(2,1)S(1)}, bf16[192,768]{1,0:T(8,128)(2,1)S(1)}, u32[]{:S(2)}, u32[]{:S(2)}) collective-permute-start(bf16[192,768]{1,0:T(8,128)(2,1)S(1)} %copy-done.39), channel_id=1, source_target_pairs={{0,8},{4,12},{8,0},{12,4},{16,24},{20,28},{24,16},{28,20},{1,9},{5... | collective-permute-start | bytes 884744 | tf_op jit(solution)/shard_map/ppermute | solution.py:25
  110.6 23.5 %collective-permute-start.35 = (bf16[192,768]{1,0:T(8,128)(2,1)S(1)}, bf16[192,768]{1,0:T(8,128)(2,1)S(1)}, u32[]{:S(2)}, u32[]{:S(2)}) collective-permute-start(bf16[192,768]{1,0:T(8,128)(2,1)S(1)} %copy-done.38), channel_id=1, source_target_pairs={{0,16},{4,20},{8,24},{12,28},{16,0},{20,4},{24,8},{28,12},{1,17},{... | collective-permute-start | bytes 884744 | tf_op jit(solution)/shard_map/ppermute | solution.py:25
  113.5 21.3 %collective-permute-start.36 = (bf16[192,768]{1,0:T(8,128)(2,1)S(1)}, bf16[192,768]{1,0:T(8,128)(2,1)S(1)}, u32[]{:S(2)}, u32[]{:S(2)}) collective-permute-start(bf16[192,768]{1,0:T(8,128)(2,1)S(1)} %copy-done.37), channel_id=1, source_target_pairs={{0,24},{4,28},{8,16},{12,20},{16,8},{20,12},{24,0},{28,4},{1,25},{... | collective-permute-start | bytes 884744 | tf_op jit(solution)/shard_map/ppermute | solution.py:25
  115.0 31.4 %collective-permute-start.27 = (bf16[256,768]{1,0:T(8,128)(2,1)}, bf16[256,768]{1,0:T(8,128)(2,1)S(1)}, u32[]{:S(2)}, u32[]{:S(2)}) collective-permute-start(bf16[256,768]{1,0:T(8,128)(2,1)} %get-tuple-element.74), channel_id=1, source_target_pairs={{0,1},{1,0},{2,3},{3,2},{4,5},{5,4},{6,7},{7,6},{8,9},{9,8},{10,11... | collective-permute-start | bytes 1179656 | tf_op jit(solution)/shard_map/ppermute | solution.py:25
  115.0 33.9 %collective-permute-start.28 = (bf16[256,768]{1,0:T(8,128)(2,1)}, bf16[256,768]{1,0:T(8,128)(2,1)S(1)}, u32[]{:S(2)}, u32[]{:S(2)}) collective-permute-start(bf16[256,768]{1,0:T(8,128)(2,1)} %get-tuple-element.75), channel_id=1, source_target_pairs={{0,2},{1,3},{2,0},{3,1},{4,6},{5,7},{6,4},{7,5},{8,10},{9,11},{10,... | collective-permute-start | bytes 1179656 | tf_op jit(solution)/shard_map/ppermute | solution.py:25
  125.6 24.3 %collective-permute-start.29 = (bf16[256,768]{1,0:T(8,128)(2,1)S(1)}, bf16[256,768]{1,0:T(8,128)(2,1)S(1)}, u32[]{:S(2)}, u32[]{:S(2)}) collective-permute-start(bf16[256,768]{1,0:T(8,128)(2,1)S(1)} %copy-done.35), channel_id=1, source_target_pairs={{0,3},{1,2},{2,1},{3,0},{4,7},{5,6},{6,5},{7,4},{8,11},{9,10},{10,... | collective-permute-start | bytes 1179656 | tf_op jit(solution)/shard_map/ppermute | solution.py:25
  134.1 12.0 %collective-permute-start.30 = (bf16[4,96,512]{2,1,0:T(8,128)(2,1)S(1)}, bf16[4,96,512]{2,1,0:T(8,128)(2,1)S(1)}, u32[]{:S(2)}, u32[]{:S(2)}) collective-permute-start(bf16[4,96,512]{2,1,0:T(8,128)(2,1)S(1)} %copy-done.36), channel_id=1, source_target_pairs={{0,4},{4,0},{8,12},{12,8},{16,20},{20,16},{24,28},{28,24},{1,5},{5... | collective-permute-start | bytes 1179656 | tf_op jit(solution)/shard_map/ppermute | solution.py:25
  135.1 22.2 %collective-permute-start.37 = (bf16[7,96,256]{2,1,0:T(8,128)(2,1)S(1)}, bf16[7,96,256]{2,1,0:T(8,128)(2,1)S(1)}, u32[]{:S(2)}, u32[]{:S(2)}) collective-permute-start(bf16[7,96,256]{2,1,0:T(8,128)(2,1)S(1)} %pad_maximum_fusion), channel_id=1, source_target_pairs={{0,4},{4,0},{8,12},{12,8},{16,20},{20,16},{24,28},{28,24},{1,5},{5... | collective-permute-start | bytes 1032200 | tf_op jit(solution)/shard_map/ppermute | solution.py:25
  148.8 8.4 %collective-permute-start.32 = (bf16[96,512]{1,0:T(8,128)(2,1)S(1)}, bf16[96,512]{1,0:T(8,128)(2,1)S(1)}, u32[]{:S(2)}, u32[]{:S(2)}) collective-permute-start(bf16[96,512]{1,0:T(8,128)(2,1)S(1)} %get-tuple-element.103), channel_id=1, source_target_pairs={{0,16},{4,20},{8,24},{12,28},{16,0},{20,4},{24,8},{28,12},{1,17},{... | collective-permute-start | bytes 294920 | tf_op jit(solution)/shard_map/ppermute | solution.py:25
  (61 other events, 759.2 us)
